TPU v7x, 32 devices: a whole 2x2x4 slice. The times are simulated.
32 devices in a mesh: dp: 4 (over z), seq: 8 (over y, x, core).
Axes of the slice: x: 2, y: 2, z: 4, core: 2. Of those that a mesh axis runs over, the one named last changes fastest.
Arguments:
- signal: bfloat16 [8, 1024, 1536], P('dp', 'seq'), may hold values from -6 to 6
- dilated_tap_weight: bfloat16 [3, 1536, 768], P(None, 'dp'), may hold values from -0.09375 to 0.09375
- out_weight: bfloat16 [768, 1536], P(None, 'dp'), may hold values from -0.21875 to 0.21875
- cotangent: bfloat16 [8, 1024, 1536], P('dp', 'seq'), may hold values from -6 to 6
Outputs:
- result: bfloat16 [8, 1024, 1536], P('dp', 'seq')
- grad_signal: bfloat16 [8, 1024, 1536], P('dp', 'seq')
All inputs are finite; a program needn't handle non-finite values.
Results may differ from a plain program's by a relative error of at most 0.0034.
Values may be sent and summed in bfloat16 or wider, within the bound.
No kernel may reach another device: no remote copies, remote signals or barrier semaphores. Data moves between devices by JAX's collectives and lax.ppermute only.
A program may use at most 64 MiB of HBM per device.

v0:
```python
import jax
import jax.numpy as jnp
from jax import lax
from jax.sharding import PartitionSpec as P

DILATION_STEP = 32


def extended(block, sides, width):
    for axis, dim in sides:
        count = lax.axis_size(axis)
        forward = [(i, i + 1) for i in range(count - 1)]
        backward = [(target, source) for source, target in forward]
        low = lax.ppermute(
            lax.slice_in_dim(block, block.shape[dim] - width, None, axis=dim), axis, forward
        )
        high = lax.ppermute(lax.slice_in_dim(block, 0, width, axis=dim), axis, backward)
        block = jnp.concatenate([low, block, high], axis=dim)
    return block


def gelu_pull(point, grad):
    _, pull = jax.vjp(jax.nn.gelu, point)
    return pull(grad)[0]


def forward_taps(gelu_output, padded_signal, convolution_filter):
    sequence_length = gelu_output.shape[1]
    preactivation = jnp.einsum(
        "xzi,iv->xzv",
        padded_signal[:, 0:sequence_length],
        convolution_filter[0],
        preferred_element_type=jnp.float32,
    )
    preactivation = preactivation + jnp.einsum(
        "xzi,iv->xzv",
        padded_signal[:, DILATION_STEP : DILATION_STEP + sequence_length],
        convolution_filter[1],
        preferred_element_type=jnp.float32,
    )
    preactivation = preactivation + jnp.einsum(
        "xzi,iv->xzv",
        padded_signal[:, 2 * DILATION_STEP : 2 * DILATION_STEP + sequence_length],
        convolution_filter[2],
        preferred_element_type=jnp.float32,
    )
    return preactivation


def backward_taps(gradient_preactivation, gradient_padded_input, convolution_filter):
    sequence_length = gradient_preactivation.shape[1]
    gradient_activation = jnp.einsum(
        "wth,ch->wtc",
        gradient_padded_input[:, 2 * DILATION_STEP : 2 * DILATION_STEP + sequence_length],
        convolution_filter[0],
        preferred_element_type=jnp.float32,
    )
    gradient_activation = gradient_activation + jnp.einsum(
        "wth,ch->wtc",
        gradient_padded_input[:, DILATION_STEP : DILATION_STEP + sequence_length],
        convolution_filter[1],
        preferred_element_type=jnp.float32,
    )
    gradient_activation = gradient_activation + jnp.einsum(
        "wth,ch->wtc",
        gradient_padded_input[:, 0:sequence_length],
        convolution_filter[2],
        preferred_element_type=jnp.float32,
    )
    return gradient_activation


def per_device(signal, dilated_tap_weight, out_weight, cotangent):
    convolution_filter, output_map = (
        lax.all_gather(dilated_tap_weight, "dp", axis=1, tiled=True),
        lax.all_gather(out_weight, "dp", axis=1, tiled=True),
    )
    signal_wide = signal.astype(jnp.float32)
    gelu_output = jax.nn.gelu(signal_wide).astype(jnp.bfloat16)
    padded_signal = extended(gelu_output, (("seq", 1),), DILATION_STEP)
    preactivation = forward_taps(gelu_output, padded_signal, convolution_filter)
    active = jax.nn.gelu(preactivation).astype(jnp.bfloat16)
    output = signal_wide + jnp.einsum(
        "wth,hc->wtc", active, output_map, preferred_element_type=jnp.float32
    )
    grad_active = jnp.einsum(
        "wtc,hc->wth", cotangent, output_map, preferred_element_type=jnp.float32
    )
    gradient_preactivation = gelu_pull(preactivation, grad_active).astype(jnp.bfloat16)
    gradient_padded_input = extended(gradient_preactivation, (("seq", 1),), DILATION_STEP)
    gradient_activation = backward_taps(
        gradient_preactivation, gradient_padded_input, convolution_filter
    )
    grad_in = cotangent.astype(jnp.float32) + gelu_pull(signal_wide, gradient_activation)
    return (output.astype(jnp.bfloat16), grad_in.astype(jnp.bfloat16))


def solution(mesh):
    return jax.shard_map(
        per_device,
        mesh=mesh,
        in_specs=(P("dp", "seq", None), P(None, "dp", None), P(None, "dp"), P("dp", "seq", None)),
        out_specs=(P("dp", "seq", None), P("dp", "seq", None)),
        check_vma=False,
    )
```

profile of v0, /device:TPU:0, one launch (start us, length us, event | category | flops | bytes accessed | tf_op | source)
XLA Modules:
  0.0 212.7 jit_solution(15958082162178033405)
XLA Ops:
  7.2 0.0 all-gather.3.cloned.1.call-start
  7.2 0.7 all-gather.3.cloned.1.call-update
  7.9 0.0 all-gather.5.cloned.1.call-start
  8.0 0.7 all-gather.5.cloned.1.call-update
  8.7 0.5 fusion.18
  9.2 2.4 %collective-permute-start = (bf16[2,32,1536]{2,1,0:T(8,128)(2,1)S(1)}, bf16[2,32,1536]{2,1,0:T(8,128)(2,1)S(1)}, u32[]{:S(2)}, u32[]{:S(2)}) collective-permute-start(bf16[2,32,1536]{2,1,0:T(8,128)(2,1)S(1)} %get-tuple-element.2), channel_id=1, source_target_pairs={{0,1},{1,2},{2,3},{3,4},{4,5},{5,6},{6,7},{8,9},{9,10},{10,11},{11... | collective-permute-start | bytes 589832 | tf_op jit(solution)/shard_map/ppermute | solution.py:14
  11.6 1.3 collective-permute-start.1
  12.9 127.6 %all-gather.3.cloned.1.call-done = bf16[3,1536,768]{2,1,0:T(8,128)(2,1)} async-done(((bf16[3,384,768]{2,1,0:T(8,128)(2,1)}), bf16[3,1536,768]{2,1,0:T(8,128)(2,1)}) %all-gather.3.cloned.1.call-update) | async-done | bytes 7077904 | tf_op jit(solution)/shard_map/all_gather | solution.py:75
  140.5 2.9 %fusion.8 = f32[2,128,768]{2,1,0:T(8,128)S(1)} fusion(bf16[3,1536,768]{2,1,0:T(8,128)(2,1)} %all-gather.3.cloned.1.call-done, bf16[2,128,1536]{2,1,0:T(8,128)(2,1)S(1)} %copy-done), kind=kOutput, calls=%fused_computation.18 | convolution fusion | flops 607911936 | bytes 3932160 | tf_op jit(solution)/shard_map/xzi,iv->xzv/dot_general | solution.py:35
  143.4 0.8 copy-done.1
  144.2 0.8 fusion.10
  145.0 0.0 copy-start.3
  145.0 0.0 collective-permute-done
  145.0 0.8 fusion.22
  145.8 44.8 %all-gather.5.cloned.1.call-done = bf16[768,1536]{1,0:T(8,128)(2,1)} async-done(((bf16[768,384]{1,0:T(8,128)(2,1)}), bf16[768,1536]{1,0:T(8,128)(2,1)}) %all-gather.5.cloned.1.call-update) | async-done | bytes 2359312 | tf_op jit(solution)/shard_map/all_gather | solution.py:76
  190.7 2.9 %fusion.29 = bf16[2,128,768]{2,1,0:T(8,128)(2,1)S(1)} fusion(f32[2,128,768]{2,1,0:T(8,128)S(1)} %fusion.22, bf16[2,128,1536]{2,1,0:T(8,128)(2,1)S(1)} %copy-done.3, bf16[768,1536]{1,0:T(8,128)(2,1)} %all-gather.5.cloned.1.call-done), kind=kOutput, calls=%fused_computation.41 | convolution fusion | flops 607911936 | bytes 4325376 | tf_op jit(solution)/shard_map/wtc,hc->wth/dot_general | solution.py:86
  193.5 1.3 collective-permute-start.2
  194.9 3.3 %collective-permute-start.3 = (bf16[2,32,768]{2,1,0:T(8,128)(2,1)S(1)}, bf16[2,32,768]{2,1,0:T(8,128)(2,1)S(1)}, u32[]{:S(2)}, u32[]{:S(2)}) collective-permute-start(bf16[2,32,768]{2,1,0:T(8,128)(2,1)S(1)} %get-tuple-element.5), channel_id=1, source_target_pairs={{0,1},{1,2},{2,3},{3,4},{4,5},{5,6},{6,7},{8,9},{9,10},{10,11},{11... | collective-permute-start | bytes 294920 | tf_op jit(solution)/shard_map/ppermute | solution.py:14
  198.2 1.7 fusion.1
  199.9 2.5 %fusion.7 = f32[2,128,1536]{2,1,0:T(8,128)S(1)} fusion(bf16[2,128,768]{2,1,0:T(8,128)(2,1)S(1)} %fusion.29, bf16[3,1536,768]{2,1,0:T(8,128)(2,1)} %all-gather.3.cloned.1.call-done), kind=kOutput, calls=%fused_computation.17 | convolution fusion | flops 603979776 | bytes 4325376 | tf_op jit(solution)/shard_map/wth,ch->wtc/dot_general | solution.py:58
  202.4 0.0 collective-permute-done.3
  202.4 0.8 fusion.9
  203.2 0.0 collective-permute-done.2
  203.2 2.6 %fusion.14 = bf16[2,128,1536]{2,1,0:T(8,128)(2,1)} fusion(bf16[2,128,1536]{2,1,0:T(8,128)(2,1)S(1)} %copy-done, f32[2,128,1536]{2,1,0:T(8,128)S(1)} %fusion.9, f32[2,128,1536]{2,1,0:T(8,128)S(1)} %fusion.7, bf16[3,1536,768]{2,1,0:T(8,128)(2,1)S(1)} %bitcast.31, bf16[2,128,1536]{2,1,0:T(8,128)(2,1)S(1)} %copy-done.3, ...), kind=kOutput, calls=%fused_computation.24 | convolution fusion | flops 614596608 | bytes 8355840 | tf_op jit(solution)/shard_map/wth,ch->wtc/dot_general | solution.py:52
  (14 shorter events, 0.1 us)
Async XLA Ops:
  7.2 1.5 copy-start
  7.2 133.3 %all-gather.3.cloned.1.call-start = ((), (), s32[]{:S(2)}) async-start(), calls=%async_computation | async-start | bytes 8847360 | tf_op jit(solution)/shard_map/all_gather | solution.py:75
  7.9 182.7 %all-gather.5.cloned.1.call-start = ((), (), s32[]{:S(2)}) async-start(), calls=%async_computation.1 | async-start | bytes 2949120 | tf_op jit(solution)/shard_map/all_gather | solution.py:76
  9.2 135.8 %collective-permute-start = (bf16[2,32,1536]{2,1,0:T(8,128)(2,1)S(1)}, bf16[2,32,1536]{2,1,0:T(8,128)(2,1)S(1)}, u32[]{:S(2)}, u32[]{:S(2)}) collective-permute-start(bf16[2,32,1536]{2,1,0:T(8,128)(2,1)S(1)} %get-tuple-element.2), channel_id=1, source_target_pairs={{0,1},{1,2},{2,3},{3,4},{4,5},{5,6},{6,7},{8,9},{9,10},{10,11},{11... | collective-permute-start | bytes 589832 | tf_op jit(solution)/shard_map/ppermute | solution.py:14
  11.6 131.8 %collective-permute-start.1 = (bf16[2,32,1536]{2,1,0:T(8,128)(2,1)S(1)}, bf16[2,32,1536]{2,1,0:T(8,128)(2,1)S(1)}, u32[]{:S(2)}, u32[]{:S(2)}) collective-permute-start(bf16[2,32,1536]{2,1,0:T(8,128)(2,1)S(1)} %get-tuple-element.3), channel_id=1, source_target_pairs={{1,0},{2,1},{3,2},{4,3},{5,4},{6,5},{7,6},{9,8},{10,9},{11,10},{12... | collective-permute-start | bytes 589832 | tf_op jit(solution)/shard_map/ppermute | solution.py:17
  140.5 3.7 %copy-start.1 = (bf16[3,1536,768]{2,1,0:T(8,128)(2,1)S(1)}, bf16[3,1536,768]{2,1,0:T(8,128)(2,1)}, u32[]{:S(2)}) copy-start(bf16[3,1536,768]{2,1,0:T(8,128)(2,1)} %all-gather.3.cloned.1.call-done) | copy-start | bytes 21233668
  145.0 45.6 %copy-start.3 = (bf16[2,128,1536]{2,1,0:T(8,128)(2,1)S(1)}, bf16[2,128,1536]{2,1,0:T(8,128)(2,1)}, u32[]{:S(2)}) copy-start(bf16[2,128,1536]{2,1,0:T(8,128)(2,1)} %param.7) | copy-start | bytes 2359300
  190.6 7.5 %copy-start.2 = (bf16[768,1536]{1,0:T(8,128)(2,1)S(1)}, bf16[768,1536]{1,0:T(8,128)(2,1)}, u32[]{:S(2)}) copy-start(bf16[768,1536]{1,0:T(8,128)(2,1)} %all-gather.5.cloned.1.call-done) | copy-start | bytes 7077892
  190.7 11.7 %slice-start = ((s8[7077888]{0:T(1024)(128)(4,1)}), s8[4194304]{0:T(1024)(128)(4,1)S(1)}, s32[]{:S(2)}) async-start(s8[7077888]{0:T(1024)(128)(4,1)} %bitcast.30), calls=%async_computation.2 | async-start | bytes 8388608
  193.5 9.7 %collective-permute-start.2 = (bf16[2,32,768]{2,1,0:T(8,128)(2,1)S(1)}, bf16[2,32,768]{2,1,0:T(8,128)(2,1)S(1)}, u32[]{:S(2)}, u32[]{:S(2)}) collective-permute-start(bf16[2,32,768]{2,1,0:T(8,128)(2,1)S(1)} %get-tuple-element.4), channel_id=1, source_target_pairs={{1,0},{2,1},{3,2},{4,3},{5,4},{6,5},{7,6},{9,8},{10,9},{11,10},{12... | collective-permute-start | bytes 294920 | tf_op jit(solution)/shard_map/ppermute | solution.py:17
  194.8 7.5 %slice-start.1 = ((s8[7077888]{0:T(1024)(128)(4,1)}), s8[2883584]{0:T(1024)(128)(4,1)S(1)}, s32[]{:S(2)}) async-start(s8[7077888]{0:T(1024)(128)(4,1)} %bitcast.30), calls=%async_computation.3 | async-start | bytes 5767168
  194.9 7.5 %collective-permute-start.3 = (bf16[2,32,768]{2,1,0:T(8,128)(2,1)S(1)}, bf16[2,32,768]{2,1,0:T(8,128)(2,1)S(1)}, u32[]{:S(2)}, u32[]{:S(2)}) collective-permute-start(bf16[2,32,768]{2,1,0:T(8,128)(2,1)S(1)} %get-tuple-element.5), channel_id=1, source_target_pairs={{0,1},{1,2},{2,3},{3,4},{4,5},{5,6},{6,7},{8,9},{9,10},{10,11},{11... | collective-permute-start | bytes 294920 | tf_op jit(solution)/shard_map/ppermute | solution.py:14
Sparse Core Ops, SparseCore 0:
  9.6 130.8 all-gather.2
  142.1 48.4 all-gather.4
where the time goes:
time: 214 us; the launch traced here: 213 us
  waiting for transfers between devices  174 us (81%)
  matrix products  14.9 us (7%)
  between operations  14.2 us (7%)
  starting transfers between devices  8.33 us (4%)
    all_gather x1, waiting for transfers between devices, per_device(): lax.all_gather(dilated_tap_weight, 'dp', axis=1, tiled=True)  128 us
    all_gather x1, waiting for transfers between devices, per_device(): lax.all_gather(out_weight, 'dp', axis=1, tiled=True)  44.8 us
    ppermute x2, starting transfers between devices, extended(): lax.ppermute(lax.slice_in_dim(block, block.shape[dim] - width, None, axis...  5.67 us
  transfers between devices with their start and end apart: 6, of which 2 were waited for; matrix products, arithmetic and copies ran while one was open for 5% of the time, Pallas kernels for 0%

commit v1 on v0

v1 whole, which is shorter than its diff:
```python
import functools
import jax
import jax.numpy as jnp
from jax import lax
from jax.experimental import pallas as pl
from jax.experimental.pallas import tpu as pltpu
from jax.sharding import PartitionSpec as P

DILATION_STEP = 32
PLANE = 8
F32 = jnp.float32
BF16 = jnp.bfloat16
ROOT = 0.7978845608028654
CUBIC = 0.044715


def gelu(v):
    return 0.5 * v * (1.0 + jnp.tanh(ROOT * (v + CUBIC * (v * v * v))))


def gelu_slope(v):
    square = v * v
    t = jnp.tanh(ROOT * v * (1.0 + CUBIC * square))
    return 0.5 * (1.0 + t) + (0.5 * ROOT) * v * (1.0 - t * t) * (1.0 + 3.0 * CUBIC * square)


def flip(index, bit):
    return index + bit - 2 * bit * ((index // bit) % 2)


def plane_pairs(count, bit_even, bit_odd):
    return [(i, i ^ (bit_odd if i % 2 else bit_even)) for i in range(count)]


def halo(block, width):
    count = lax.axis_size("seq")
    forward = [(i, i + 1) for i in range(count - 1)]
    backward = [(target, source) for source, target in forward]
    low = lax.ppermute(block[:, -width:], "seq", forward)
    high = lax.ppermute(block[:, :width], "seq", backward)
    return low, high


def stack_rows(ref, low, high, shift, columns):
    rows = ref.shape[1]
    parts = []
    for w in range(ref.shape[0]):
        if shift < 0:
            parts += [low[w, :, columns], ref[w, : rows + shift, columns]]
        elif shift > 0:
            parts += [ref[w, shift:, columns], high[w, :, columns]]
        else:
            parts += [ref[w, :, columns]]
    return jnp.concatenate(parts, axis=0)


def slot_dots(slot, taps, outs, act, low, high, cot):
    width = outs.shape[1]
    z = lax.axis_index("dp")
    for bit in (1, 2):
        if slot & bit:
            z = flip(z, bit)
    columns = pl.ds(pl.multiple_of(z * width, 128), width)
    inner = None
    for k in range(3):
        lhs = stack_rows(act, low, high, (k - 1) * DILATION_STEP, columns)
        term = jnp.dot(lhs, taps[k], preferred_element_type=F32)
        inner = term if inner is None else inner + term
    lhs = stack_rows(cot, None, None, 0, columns)
    grad = lax.dot_general(lhs, outs[...], (((1,), (1,)), ((), ())), preferred_element_type=F32)
    return inner, grad


def own_kernel(act, low, high, cot, taps, outs, inner, grad):
    inner[...], grad[...] = slot_dots(0, taps, outs, act, low, high, cot)


def slot_kernel(slot, act, low, high, cot, own, own_far, other, other_far, inner_in, grad_in, inner, grad, taps, outs, sems):
    s = lax.axis_index("seq") % PLANE
    rows = own.shape[2]
    width = outs.shape[1]
    first = 2 + 2 * (s % 2)
    second = 6 - first

    def moved(index, step):
        return index + step - 2 * step * ((index // step) % 2)

    mate = flip(s, 1)
    order = (
        (own, s, moved(s, first)),
        (own_far, moved(s, second), flip(flip(s, 2), 4)),
        (other, mate, moved(mate, second)),
        (other_far, moved(mate, first), flip(flip(mate, 2), 4)),
    )
    copies = []
    for buffer, *places in order:
        for i, q in enumerate(places):
            copies.append((buffer.at[i, 0:3], taps.at[:, pl.ds(pl.multiple_of(q * rows, 16), rows), :]))
            at = pl.multiple_of(q * 2 * rows, 16)
            copies.append((buffer.at[i, 3, :, 0:width], outs.at[pl.ds(at, rows), :]))
            copies.append((buffer.at[i, 3, :, width : 2 * width], outs.at[pl.ds(at + rows, rows), :]))
    copies = [pltpu.make_async_copy(a, b, sems.at[n]) for n, (a, b) in enumerate(copies)]
    for copy in copies:
        copy.start()
    for copy in copies:
        copy.wait()
    more_inner, more_grad = slot_dots(slot, taps, outs, act, low, high, cot)
    inner[...] = inner_in[...] + more_inner
    grad[...] = grad_in[...] + more_grad


def middle_kernel(inner, grad, active, grad_inner):
    v = inner[...]
    square = v * v
    t = jnp.tanh(ROOT * v * (1.0 + CUBIC * square))
    active[...] = (0.5 * v * (1.0 + t)).astype(BF16)
    slope = 0.5 * (1.0 + t) + (0.5 * ROOT) * v * (1.0 - t * t) * (1.0 + 3.0 * CUBIC * square)
    grad_inner[...] = (grad[...] * slope).astype(BF16).reshape(grad_inner.shape)


def slot_columns(slot, width):
    z = lax.axis_index("dp")
    for bit in (1, 2):
        if slot & bit:
            z = flip(z, bit)
    return pl.ds(pl.multiple_of(z * width, 128), width)


def result_kernel(slots, *refs):
    signal, active, grad_inner = refs[:3]
    taps = refs[3 : 3 + slots]
    outs = refs[3 + slots : 3 + 2 * slots]
    result, partial = refs[3 + 2 * slots :]
    width = outs[0].shape[1]
    windows, rows = signal.shape[:2]
    lhs = active[...]
    gi = grad_inner[...].reshape(windows * rows, -1)
    for slot in range(slots):
        columns = slot_columns(slot, width)
        more = jnp.dot(lhs, outs[slot][...], preferred_element_type=F32).reshape(windows, rows, width)
        result[:, :, columns] = (signal[:, :, columns].astype(F32) + more).astype(BF16)
        partial[:, :, columns] = lax.dot_general(
            gi, taps[slot][1], (((1,), (1,)), ((), ())), preferred_element_type=F32
        ).reshape(windows, rows, width)


def final_kernel(slots, *refs):
    cot, slope, partial, grad_inner, low, high = refs[:6]
    taps = refs[6 : 6 + slots]
    out = refs[6 + slots]
    windows, rows = cot.shape[:2]
    everything = slice(None)
    later = stack_rows(grad_inner, low, high, DILATION_STEP, everything)
    earlier = stack_rows(grad_inner, low, high, -DILATION_STEP, everything)
    width = taps[0].shape[1]
    dims = (((1,), (1,)), ((), ()))
    for slot in range(slots):
        columns = slot_columns(slot, width)
        more = lax.dot_general(later, taps[slot][0], dims, preferred_element_type=F32)
        more = more + lax.dot_general(earlier, taps[slot][2], dims, preferred_element_type=F32)
        total = partial[:, :, columns] + more.reshape(windows, rows, width)
        out[:, :, columns] = (cot[:, :, columns].astype(F32) + total * slope[:, :, columns]).astype(BF16)


def params(mib):
    return pltpu.CompilerParams(vmem_limit_bytes=mib << 20)


def per_device(slots, signal, tap, out, cot):
    windows, rows, channels = signal.shape
    hidden = tap.shape[2]
    width = tap.shape[1]
    total = windows * rows
    plane = lax.axis_index("seq") % PLANE
    piece = width // PLANE
    mine = lax.dynamic_slice_in_dim(tap, plane * piece, piece, axis=1)
    mine_out = lax.dynamic_slice_in_dim(out, plane * 2 * piece, 2 * piece, axis=0)
    mine = jnp.concatenate([mine, jnp.concatenate([mine_out[:piece], mine_out[piece:]], axis=1)[None]], axis=0)
    count = lax.axis_size("seq")
    gathered = []
    for slot in range(1, slots):
        got = lax.ppermute(mine, "dp", [(i, i ^ slot) for i in range(slots)])
        near = lax.ppermute(got, "seq", plane_pairs(count, 2, 4))
        own = jnp.stack([got, near])
        own_far = lax.ppermute(own, "seq", plane_pairs(count, 4, 2))
        other = lax.ppermute(own, "seq", plane_pairs(count, 1, 1))
        other_far = lax.ppermute(own_far, "seq", plane_pairs(count, 1, 1))
        gathered.append((own, own_far, other, other_far))

    wide = signal.astype(F32)
    act = gelu(wide).astype(BF16)
    slope = gelu_slope(wide)
    low, high = halo(act, DILATION_STEP)

    sums = [jax.ShapeDtypeStruct((total, hidden), F32)] * 2
    vmem = pl.BlockSpec(memory_space=pltpu.VMEM)
    hbm = pl.BlockSpec(memory_space=pl.ANY)
    inner, grad = pl.pallas_call(
        own_kernel, out_shape=sums, in_specs=[vmem] * 6, out_specs=[vmem] * 2, compiler_params=params(24)
    )(act, low, high, cot, tap, out)
    taps, outs = [tap], [out]
    for slot in range(1, slots):
        inner, grad, more_tap, more_out = pl.pallas_call(
            functools.partial(slot_kernel, slot),
            out_shape=sums + [jax.ShapeDtypeStruct(tap.shape, BF16), jax.ShapeDtypeStruct(out.shape, BF16)],
            in_specs=[vmem] * 4 + [hbm] * 4 + [vmem] * 2,
            out_specs=[vmem] * 4,
            scratch_shapes=[pltpu.SemaphoreType.DMA((24,))],
            input_output_aliases={8: 0, 9: 1},
            compiler_params=params(24),
        )(act, low, high, cot, *gathered[slot - 1], inner, grad)
        taps.append(more_tap)
        outs.append(more_out)
    active, grad_inner = pl.pallas_call(
        middle_kernel,
        out_shape=[jax.ShapeDtypeStruct((total, hidden), BF16), jax.ShapeDtypeStruct((windows, rows, hidden), BF16)],
        in_specs=[vmem] * 2,
        out_specs=[vmem] * 2,
        compiler_params=params(16),
    )(inner, grad)
    low, high = halo(grad_inner, DILATION_STEP)
    result, partial = pl.pallas_call(
        functools.partial(result_kernel, slots),
        out_shape=[jax.ShapeDtypeStruct(signal.shape, BF16), jax.ShapeDtypeStruct(signal.shape, F32)],
        in_specs=[vmem] * (3 + 2 * slots),
        out_specs=[vmem] * 2,
        compiler_params=params(32),
    )(signal, active, grad_inner, *taps, *outs)
    grad_signal = pl.pallas_call(
        functools.partial(final_kernel, slots),
        out_shape=jax.ShapeDtypeStruct(signal.shape, BF16),
        in_specs=[vmem] * (6 + slots),
        out_specs=vmem,
        compiler_params=params(32),
    )(cot, slope, partial, grad_inner, low, high, *taps)
    return result, grad_signal


def extended(block, width):
    low, high = halo(block, width)
    return jnp.concatenate([low, block, high], axis=1)


def per_device_general(signal, tap, out, cot):
    tap = lax.all_gather(tap, "dp", axis=1, tiled=True)
    out = lax.all_gather(out, "dp", axis=1, tiled=True)
    rows = signal.shape[1]
    wide = signal.astype(F32)
    act = extended(gelu(wide).astype(BF16), DILATION_STEP)

    def contract(rule, a, b):
        return jnp.einsum(rule, a, b, preferred_element_type=F32)

    def window(block, k):
        return block[:, k * DILATION_STEP : k * DILATION_STEP + rows]

    inner = sum(contract("wtc,ch->wth", window(act, k), tap[k]) for k in range(3))
    active = gelu(inner).astype(BF16)
    result = wide + contract("wth,hc->wtc", active, out)
    grad_inner = (contract("wtc,hc->wth", cot, out) * gelu_slope(inner)).astype(BF16)
    grad_inner = extended(grad_inner, DILATION_STEP)
    grad_act = sum(contract("wth,ch->wtc", window(grad_inner, 2 - k), tap[k]) for k in range(3))
    grad_signal = cot.astype(F32) + grad_act * gelu_slope(wide)
    return result.astype(BF16), grad_signal.astype(BF16)


def solution(mesh):
    dp, seq = mesh.shape["dp"], mesh.shape["seq"]

    def run(signal, tap, out, cot):
        width = tap.shape[1] // dp
        hidden = tap.shape[2]
        sliced = dp in (2, 4) and seq % PLANE == 0 and width % 128 == 0 and 2 * width == hidden
        body = functools.partial(per_device, dp) if sliced else per_device_general
        return jax.shard_map(
            body,
            mesh=mesh,
            in_specs=(P("dp", "seq", None), P(None, "dp", None), P(None, "dp"), P("dp", "seq", None)),
            out_specs=(P("dp", "seq", None), P("dp", "seq", None)),
            check_vma=False,
        )(signal, tap, out, cot)

    return run
```

time: 214 us -> 83 us (0.39)
  the two profiles are of different devices: /device:TPU:0 before, /device:TPU:20 now
where the time goes in v1:
time: 83 us; the launch traced here: 82.7 us
  waiting for transfers between devices  41.5 us (50%)
  starting transfers between devices  23.1 us (28%)
  Pallas kernels  13.9 us (17%)
  local copies, waits for them, and re-layouts  1.89 us (2%)
  other arithmetic  1.5 us (2%)
  between operations  0.86 us (1%)
    ppermute x3, waiting for transfers between devices, per_device(): got = lax.ppermute(mine, 'dp', [(i, i ^ slot) for i in range(slots)])  22.5 us
    ppermute x2, waiting for transfers between devices, halo(): low = lax.ppermute(block[:, -width:], 'seq', forward)  9.83 us
    ppermute x2, starting transfers between devices, halo(): low = lax.ppermute(block[:, -width:], 'seq', forward)  7.32 us
    pallas_call x3, Pallas kernels, per_device(): pl.pallas_call(functools.partial(slot_kernel, slot), out_shape=sums + [ja...  7.13 us
    ppermute x2, waiting for transfers between devices, halo(): high = lax.ppermute(block[:, :width], 'seq', backward)  5.34 us
    ppermute x3, starting transfers between devices, per_device(): near = lax.ppermute(got, 'seq', plane_pairs(count, 2, 4))  4.47 us
    ppermute x2, starting transfers between devices, halo(): high = lax.ppermute(block[:, :width], 'seq', backward)  3.84 us
    ppermute x3, waiting for transfers between devices, per_device(): near = lax.ppermute(got, 'seq', plane_pairs(count, 2, 4))  3.82 us
  transfers between devices with their start and end apart: 19, of which 7 were waited for; matrix products, arithmetic and copies ran while one was open for 2% of the time, Pallas kernels for 10%

profile of v1, /device:TPU:20, one launch (start us, length us, event | category | flops | bytes accessed | tf_op | source)
XLA Modules:
  0.0 82.7 jit_solution(985475854178821294)
XLA Ops:
  2.5 1.6 %collective-permute-start.12 = (bf16[4,48,768]{2,1,0:T(8,128)(2,1)S(1)}, bf16[4,48,768]{2,1,0:T(8,128)(2,1)S(1)}, u32[]{:S(2)}, u32[]{:S(2)}) collective-permute-start(bf16[4,48,768]{2,1,0:T(8,128)(2,1)S(1)} %pad_maximum_fusion.3), channel_id=1, source_target_pairs={{0,8},{8,0},{16,24},{24,16},{1,9},{9,1},{17,25},{25,17},{2,10},{10... | collective-permute-start | bytes 884744 | tf_op jit(solution)/shard_map/ppermute | solution.py:182
  4.5 1.6 %collective-permute-start.2 = (bf16[4,48,768]{2,1,0:T(8,128)(2,1)S(1)}, bf16[4,48,768]{2,1,0:T(8,128)(2,1)S(1)}, u32[]{:S(2)}, u32[]{:S(2)}) collective-permute-start(bf16[4,48,768]{2,1,0:T(8,128)(2,1)S(1)} %pad_maximum_fusion.3), channel_id=1, source_target_pairs={{0,24},{8,16},{16,8},{24,0},{1,25},{9,17},{17,9},{25,1},{2,26},{10... | collective-permute-start | bytes 884744 | tf_op jit(solution)/shard_map/ppermute | solution.py:182
  6.1 9.3 %collective-permute-done.12 = bf16[4,48,768]{2,1,0:T(8,128)(2,1)S(1)} collective-permute-done((bf16[4,48,768]{2,1,0:T(8,128)(2,1)S(1)}, bf16[4,48,768]{2,1,0:T(8,128)(2,1)S(1)}, u32[]{:S(2)}, u32[]{:S(2)}) %collective-permute-start.12) | collective-permute-done | bytes 294944 | tf_op jit(solution)/shard_map/ppermute | solution.py:182
  15.4 1.5 %collective-permute-start.13 = (bf16[4,48,768]{2,1,0:T(8,128)(2,1)S(1)}, bf16[4,48,768]{2,1,0:T(8,128)(2,1)S(1)}, u32[]{:S(2)}, u32[]{:S(2)}) collective-permute-start(bf16[4,48,768]{2,1,0:T(8,128)(2,1)S(1)} %collective-permute-done.12), channel_id=1, source_target_pairs={{0,2},{1,5},{2,0},{3,7},{4,6},{5,1},{6,4},{7,3},{8,10},{9,13},{10,... | collective-permute-start | bytes 884744 | tf_op jit(solution)/shard_map/ppermute | solution.py:183
  16.9 7.7 %collective-permute-done.7 = bf16[4,48,768]{2,1,0:T(8,128)(2,1)S(1)} collective-permute-done((bf16[4,48,768]{2,1,0:T(8,128)(2,1)S(1)}, bf16[4,48,768]{2,1,0:T(8,128)(2,1)S(1)}, u32[]{:S(2)}, u32[]{:S(2)}) %collective-permute-start.7) | collective-permute-done | bytes 294944 | tf_op jit(solution)/shard_map/ppermute | solution.py:182
  24.6 1.5 %collective-permute-start.8 = (bf16[4,48,768]{2,1,0:T(8,128)(2,1)S(1)}, bf16[4,48,768]{2,1,0:T(8,128)(2,1)S(1)}, u32[]{:S(2)}, u32[]{:S(2)}) collective-permute-start(bf16[4,48,768]{2,1,0:T(8,128)(2,1)S(1)} %collective-permute-done.7), channel_id=1, source_target_pairs={{0,2},{1,5},{2,0},{3,7},{4,6},{5,1},{6,4},{7,3},{8,10},{9,13},{10,... | collective-permute-start | bytes 884744 | tf_op jit(solution)/shard_map/ppermute | solution.py:183
  26.1 5.4 %collective-permute-done.2 = bf16[4,48,768]{2,1,0:T(8,128)(2,1)S(1)} collective-permute-done((bf16[4,48,768]{2,1,0:T(8,128)(2,1)S(1)}, bf16[4,48,768]{2,1,0:T(8,128)(2,1)S(1)}, u32[]{:S(2)}, u32[]{:S(2)}) %collective-permute-start.2) | collective-permute-done | bytes 294944 | tf_op jit(solution)/shard_map/ppermute | solution.py:182
  31.5 1.5 %collective-permute-start.3 = (bf16[4,48,768]{2,1,0:T(8,128)(2,1)S(1)}, bf16[4,48,768]{2,1,0:T(8,128)(2,1)S(1)}, u32[]{:S(2)}, u32[]{:S(2)}) collective-permute-start(bf16[4,48,768]{2,1,0:T(8,128)(2,1)S(1)} %collective-permute-done.2), channel_id=1, source_target_pairs={{0,2},{1,5},{2,0},{3,7},{4,6},{5,1},{6,4},{7,3},{8,10},{9,13},{10,... | collective-permute-start | bytes 884744 | tf_op jit(solution)/shard_map/ppermute | solution.py:183
  33.0 1.3 %fusion.7 = (f32[2,128,1536]{2,1,0:T(8,128)S(1)}, bf16[2,128,1536]{2,1,0:T(8,128)(2,1)S(1)}) fusion(bf16[2,128,1536]{2,1,0:T(8,128)(2,1)S(1)} %copy-done.2), kind=kLoop, calls=%fused_computation.13 | loop fusion | flops 9437184 | bytes 3145728 | tf_op jit(solution)/shard_map/add | solution.py:24
  35.1 3.8 %collective-permute-done.3 = bf16[4,48,768]{2,1,0:T(8,128)(2,1)S(1)} collective-permute-done((bf16[4,48,768]{2,1,0:T(8,128)(2,1)S(1)}, bf16[4,48,768]{2,1,0:T(8,128)(2,1)S(1)}, u32[]{:S(2)}, u32[]{:S(2)}) %collective-permute-start.3) | collective-permute-done | bytes 294944 | tf_op jit(solution)/shard_map/ppermute | solution.py:183
  39.6 1.6 %collective-permute-start.9 = (bf16[2,4,48,768]{3,2,1,0:T(8,128)(2,1)S(1)}, bf16[2,4,48,768]{3,2,1,0:T(8,128)(2,1)S(1)}, u32[]{:S(2)}, u32[]{:S(2)}) collective-permute-start(bf16[2,4,48,768]{3,2,1,0:T(8,128)(2,1)S(1)} %pad_maximum_fusion.1.own), channel_id=1, source_target_pairs={{0,4},{1,3},{2,6},{3,1},{4,0},{5,7},{6,2},{7,5},{8,12},{9,11},{10,... | collective-permute-start | bytes 1769480 | tf_op jit(solution)/shard_map/ppermute | solution.py:185
  41.2 1.9 %collective-permute-start.1 = (bf16[2,32,1536]{2,1,0:T(8,128)(2,1)S(1)}, bf16[2,32,1536]{2,1,0:T(8,128)(2,1)S(1)}, u32[]{:S(2)}, u32[]{:S(2)}) collective-permute-start(bf16[2,32,1536]{2,1,0:T(8,128)(2,1)S(1)} %get-tuple-element.40), channel_id=1, source_target_pairs={{1,0},{2,1},{3,2},{4,3},{5,4},{6,5},{7,6},{9,8},{10,9},{11,10},{12... | collective-permute-start | bytes 589832 | tf_op jit(solution)/shard_map/ppermute | solution.py:40
  43.1 5.3 %collective-permute-done.1.high = bf16[2,32,1536]{2,1,0:T(8,128)(2,1)S(1)} collective-permute-done((bf16[2,32,1536]{2,1,0:T(8,128)(2,1)S(1)}, bf16[2,32,1536]{2,1,0:T(8,128)(2,1)S(1)}, u32[]{:S(2)}, u32[]{:S(2)}) %collective-permute-start.1) | collective-permute-done | bytes 196640 | tf_op jit(solution)/shard_map/ppermute | solution.py:40
  48.5 4.9 %collective-permute-start = (bf16[2,32,1536]{2,1,0:T(8,128)(2,1)S(1)}, bf16[2,32,1536]{2,1,0:T(8,128)(2,1)S(1)}, u32[]{:S(2)}, u32[]{:S(2)}) collective-permute-start(bf16[2,32,1536]{2,1,0:T(8,128)(2,1)S(1)} %get-tuple-element.41), channel_id=1, source_target_pairs={{0,1},{1,2},{2,3},{3,4},{4,5},{5,6},{6,7},{8,9},{9,10},{10,11},{11... | collective-permute-start | bytes 589832 | tf_op jit(solution)/shard_map/ppermute | solution.py:39
  53.5 7.9 %collective-permute-done.low = bf16[2,32,1536]{2,1,0:T(8,128)(2,1)S(1)} collective-permute-done((bf16[2,32,1536]{2,1,0:T(8,128)(2,1)S(1)}, bf16[2,32,1536]{2,1,0:T(8,128)(2,1)S(1)}, u32[]{:S(2)}, u32[]{:S(2)}) %collective-permute-start) | collective-permute-done | bytes 196640 | tf_op jit(solution)/shard_map/ppermute | solution.py:39
  62.4 1.0 %shard_map.59 = (f32[256,768]{1,0:T(8,128)S(1)}, f32[256,768]{1,0:T(8,128)S(1)}) custom-call(bf16[2,128,1536]{2,1,0:T(8,128)(2,1)S(1)} %get-tuple-element.39.act, bf16[2,32,1536]{2,1,0:T(8,128)(2,1)S(1)} %collective-permute-done.low, bf16[2,32,1536]{2,1,0:T(8,128)(2,1)S(1)} %collective-permute-done.1.high, bf16[2,128,1536]{2,1,0:T(8,128)(2,1)S(1)} %copy-done, ...), custom_call_target="tpu_custom_call" | custom-call | tf_op jit(solution)/shard_map/pallas_call | solution.py:198
  63.4 2.4 %shard_map.60 = (f32[256,768]{1,0:T(8,128)S(1)}, f32[256,768]{1,0:T(8,128)S(1)}, bf16[3,384,768]{2,1,0:T(8,128)(2,1)S(1)}, bf16[768,384]{1,0:T(8,128)(2,1)S(1)}) custom-call(bf16[2,128,1536]{2,1,0:T(8,128)(2,1)S(1)} %get-tuple-element.39.act, bf16[2,32,1536]{2,1,0:T(8,128)(2,1)S(1)} %collective-permute-done.low, ...), custom_call_target="tpu_custom_call", output_to_operand_aliasing={{0}: (8, {}), {1}: (9, {})} | custom-call | tf_op jit(solution)/shard_map/pallas_call | solution.py:203
  65.8 2.4 %shard_map.61 = (f32[256,768]{1,0:T(8,128)S(1)}, f32[256,768]{1,0:T(8,128)S(1)}, bf16[3,384,768]{2,1,0:T(8,128)(2,1)S(1)}, bf16[768,384]{1,0:T(8,128)(2,1)S(1)}) custom-call(bf16[2,128,1536]{2,1,0:T(8,128)(2,1)S(1)} %get-tuple-element.39.act, bf16[2,32,1536]{2,1,0:T(8,128)(2,1)S(1)} %collective-permute-done.low, ...), custom_call_target="tpu_custom_call", output_to_operand_aliasing={{0}: (8, {}), {1}: (9, {})} | custom-call | tf_op jit(solution)/shard_map/pallas_call | solution.py:203
  68.2 2.4 %shard_map.62 = (f32[256,768]{1,0:T(8,128)S(1)}, f32[256,768]{1,0:T(8,128)S(1)}, bf16[3,384,768]{2,1,0:T(8,128)(2,1)S(1)}, bf16[768,384]{1,0:T(8,128)(2,1)S(1)}) custom-call(bf16[2,128,1536]{2,1,0:T(8,128)(2,1)S(1)} %get-tuple-element.39.act, bf16[2,32,1536]{2,1,0:T(8,128)(2,1)S(1)} %collective-permute-done.low, ...), custom_call_target="tpu_custom_call", output_to_operand_aliasing={{0}: (8, {}), {1}: (9, {})} | custom-call | tf_op jit(solution)/shard_map/pallas_call | solution.py:203
  71.2 1.9 %collective-permute-start.18 = (bf16[2,32,768]{2,1,0:T(8,128)(2,1)S(1)}, bf16[2,32,768]{2,1,0:T(8,128)(2,1)S(1)}, u32[]{:S(2)}, u32[]{:S(2)}) collective-permute-start(bf16[2,32,768]{2,1,0:T(8,128)(2,1)S(1)} %get-tuple-element.44), channel_id=1, source_target_pairs={{1,0},{2,1},{3,2},{4,3},{5,4},{6,5},{7,6},{9,8},{10,9},{11,10},{12... | collective-permute-start | bytes 294920 | tf_op jit(solution)/shard_map/ppermute | solution.py:40
  73.1 2.4 %collective-permute-start.17 = (bf16[2,32,768]{2,1,0:T(8,128)(2,1)S(1)}, bf16[2,32,768]{2,1,0:T(8,128)(2,1)S(1)}, u32[]{:S(2)}, u32[]{:S(2)}) collective-permute-start(bf16[2,32,768]{2,1,0:T(8,128)(2,1)S(1)} %get-tuple-element.45), channel_id=1, source_target_pairs={{0,1},{1,2},{2,3},{3,4},{4,5},{5,6},{6,7},{8,9},{9,10},{10,11},{11... | collective-permute-start | bytes 294920 | tf_op jit(solution)/shard_map/ppermute | solution.py:39
  75.5 2.5 %shard_map.64 = (bf16[2,128,1536]{2,1,0:T(8,128)(2,1)}, f32[2,128,1536]{2,1,0:T(8,128)S(1)}) custom-call(bf16[2,128,1536]{2,1,0:T(8,128)(2,1)S(1)} %copy-done.2, bf16[256,768]{1,0:T(8,128)(2,1)S(1)} %get-tuple-element.28.refs_1_, bf16[2,128,768]{2,1,0:T(8,128)(2,1)S(1)} %get-tuple-element.29.refs_2_.refs_3_, bf16[3,384,768]{2,1,0:T(8,128)(2,1)S(1)} %copy-done.1, ...), custom_call_target="tpu_custom_call" | custom-call | tf_op jit(solution)/shard_map/pallas_call | solution.py:222
  78.0 1.9 %collective-permute-done.17.refs_4_ = bf16[2,32,768]{2,1,0:T(8,128)(2,1)S(1)} collective-permute-done((bf16[2,32,768]{2,1,0:T(8,128)(2,1)S(1)}, bf16[2,32,768]{2,1,0:T(8,128)(2,1)S(1)}, u32[]{:S(2)}, u32[]{:S(2)}) %collective-permute-start.17) | collective-permute-done | bytes 98336 | tf_op jit(solution)/shard_map/ppermute | solution.py:39
  79.9 2.8 %shard_map.65 = bf16[2,128,1536]{2,1,0:T(8,128)(2,1)} custom-call(bf16[2,128,1536]{2,1,0:T(8,128)(2,1)S(1)} %copy-done, f32[2,128,1536]{2,1,0:T(8,128)S(1)} %get-tuple-element.38.refs_1_, f32[2,128,1536]{2,1,0:T(8,128)S(1)} %get-tuple-element.37.refs_2_, bf16[2,128,768]{2,1,0:T(8,128)(2,1)S(1)} %get-tuple-element.29.refs_2_.refs_3_, ...), custom_call_target="tpu_custom_call" | custom-call | tf_op jit(solution)/shard_map/pallas_call | solution.py:229
  (39 shorter events, 5.3 us)
Async XLA Ops:
  0.6 32.4 %copy-start.2 = (bf16[2,128,1536]{2,1,0:T(8,128)(2,1)S(1)}, bf16[2,128,1536]{2,1,0:T(8,128)(2,1)}, u32[]{:S(2)}) copy-start(bf16[2,128,1536]{2,1,0:T(8,128)(2,1)} %refs_0_.2) | copy-start | bytes 2359300
  2.5 12.9 %collective-permute-start.12 = (bf16[4,48,768]{2,1,0:T(8,128)(2,1)S(1)}, bf16[4,48,768]{2,1,0:T(8,128)(2,1)S(1)}, u32[]{:S(2)}, u32[]{:S(2)}) collective-permute-start(bf16[4,48,768]{2,1,0:T(8,128)(2,1)S(1)} %pad_maximum_fusion.3), channel_id=1, source_target_pairs={{0,8},{8,0},{16,24},{24,16},{1,9},{9,1},{17,25},{25,17},{2,10},{10... | collective-permute-start | bytes 884744 | tf_op jit(solution)/shard_map/ppermute | solution.py:182
  4.2 20.4 %collective-permute-start.7 = (bf16[4,48,768]{2,1,0:T(8,128)(2,1)S(1)}, bf16[4,48,768]{2,1,0:T(8,128)(2,1)S(1)}, u32[]{:S(2)}, u32[]{:S(2)}) collective-permute-start(bf16[4,48,768]{2,1,0:T(8,128)(2,1)S(1)} %pad_maximum_fusion.3), channel_id=1, source_target_pairs={{0,16},{8,24},{16,0},{24,8},{1,17},{9,25},{17,1},{25,9},{2,18},{10... | collective-permute-start | bytes 884744 | tf_op jit(solution)/shard_map/ppermute | solution.py:182
  4.5 27.0 %collective-permute-start.2 = (bf16[4,48,768]{2,1,0:T(8,128)(2,1)S(1)}, bf16[4,48,768]{2,1,0:T(8,128)(2,1)S(1)}, u32[]{:S(2)}, u32[]{:S(2)}) collective-permute-start(bf16[4,48,768]{2,1,0:T(8,128)(2,1)S(1)} %pad_maximum_fusion.3), channel_id=1, source_target_pairs={{0,24},{8,16},{16,8},{24,0},{1,25},{9,17},{17,9},{25,1},{2,26},{10... | collective-permute-start | bytes 884744 | tf_op jit(solution)/shard_map/ppermute | solution.py:182
  15.4 18.9 %collective-permute-start.13 = (bf16[4,48,768]{2,1,0:T(8,128)(2,1)S(1)}, bf16[4,48,768]{2,1,0:T(8,128)(2,1)S(1)}, u32[]{:S(2)}, u32[]{:S(2)}) collective-permute-start(bf16[4,48,768]{2,1,0:T(8,128)(2,1)S(1)} %collective-permute-done.12), channel_id=1, source_target_pairs={{0,2},{1,5},{2,0},{3,7},{4,6},{5,1},{6,4},{7,3},{8,10},{9,13},{10,... | collective-permute-start | bytes 884744 | tf_op jit(solution)/shard_map/ppermute | solution.py:183
  24.6 14.9 %collective-permute-start.8 = (bf16[4,48,768]{2,1,0:T(8,128)(2,1)S(1)}, bf16[4,48,768]{2,1,0:T(8,128)(2,1)S(1)}, u32[]{:S(2)}, u32[]{:S(2)}) collective-permute-start(bf16[4,48,768]{2,1,0:T(8,128)(2,1)S(1)} %collective-permute-done.7), channel_id=1, source_target_pairs={{0,2},{1,5},{2,0},{3,7},{4,6},{5,1},{6,4},{7,3},{8,10},{9,13},{10,... | collective-permute-start | bytes 884744 | tf_op jit(solution)/shard_map/ppermute | solution.py:183
  31.5 7.3 %collective-permute-start.3 = (bf16[4,48,768]{2,1,0:T(8,128)(2,1)S(1)}, bf16[4,48,768]{2,1,0:T(8,128)(2,1)S(1)}, u32[]{:S(2)}, u32[]{:S(2)}) collective-permute-start(bf16[4,48,768]{2,1,0:T(8,128)(2,1)S(1)} %collective-permute-done.2), channel_id=1, source_target_pairs={{0,2},{1,5},{2,0},{3,7},{4,6},{5,1},{6,4},{7,3},{8,10},{9,13},{10,... | collective-permute-start | bytes 884744 | tf_op jit(solution)/shard_map/ppermute | solution.py:183
  34.4 27.6 %collective-permute-start.15 = (bf16[2,4,48,768]{3,2,1,0:T(8,128)(2,1)S(1)}, bf16[2,4,48,768]{3,2,1,0:T(8,128)(2,1)S(1)}, u32[]{:S(2)}, u32[]{:S(2)}) collective-permute-start(bf16[2,4,48,768]{3,2,1,0:T(8,128)(2,1)S(1)} %pad_maximum_fusion.2.own), channel_id=1, source_target_pairs={{0,1},{1,0},{2,3},{3,2},{4,5},{5,4},{6,7},{7,6},{8,9},{9,8},{10,11... | collective-permute-start | bytes 1769480 | tf_op jit(solution)/shard_map/ppermute | solution.py:186
  34.5 18.9 %collective-permute-start.14 = (bf16[2,4,48,768]{3,2,1,0:T(8,128)(2,1)S(1)}, bf16[2,4,48,768]{3,2,1,0:T(8,128)(2,1)S(1)}, u32[]{:S(2)}, u32[]{:S(2)}) collective-permute-start(bf16[2,4,48,768]{3,2,1,0:T(8,128)(2,1)S(1)} %pad_maximum_fusion.2.own), channel_id=1, source_target_pairs={{0,4},{1,3},{2,6},{3,1},{4,0},{5,7},{6,2},{7,5},{8,12},{9,11},{10,... | collective-permute-start | bytes 1769480 | tf_op jit(solution)/shard_map/ppermute | solution.py:185
  38.9 23.5 %copy-start = (bf16[2,128,1536]{2,1,0:T(8,128)(2,1)S(1)}, bf16[2,128,1536]{2,1,0:T(8,128)(2,1)}, u32[]{:S(2)}) copy-start(bf16[2,128,1536]{2,1,0:T(8,128)(2,1)} %refs_0_.3) | copy-start | bytes 2359300
  38.9 23.5 %copy-start.1 = (bf16[3,384,768]{2,1,0:T(8,128)(2,1)S(1)}, bf16[3,384,768]{2,1,0:T(8,128)(2,1)}, u32[]{:S(2)}) copy-start(bf16[3,384,768]{2,1,0:T(8,128)(2,1)} %refs_6_.1) | copy-start | bytes 5308420
  38.9 23.5 %copy-start.3 = (bf16[768,384]{1,0:T(8,128)(2,1)S(1)}, bf16[768,384]{1,0:T(8,128)(2,1)}, u32[]{:S(2)}) copy-start(bf16[768,384]{1,0:T(8,128)(2,1)} %refs_7_.1) | copy-start | bytes 1769476
  38.9 23.0 %collective-permute-start.4 = (bf16[2,4,48,768]{3,2,1,0:T(8,128)(2,1)S(1)}, bf16[2,4,48,768]{3,2,1,0:T(8,128)(2,1)S(1)}, u32[]{:S(2)}, u32[]{:S(2)}) collective-permute-start(bf16[2,4,48,768]{3,2,1,0:T(8,128)(2,1)S(1)} %pad_maximum_fusion.own), channel_id=1, source_target_pairs={{0,4},{1,3},{2,6},{3,1},{4,0},{5,7},{6,2},{7,5},{8,12},{9,11},{10,... | collective-permute-start | bytes 1769480 | tf_op jit(solution)/shard_map/ppermute | solution.py:185
  39.6 21.8 %collective-permute-start.9 = (bf16[2,4,48,768]{3,2,1,0:T(8,128)(2,1)S(1)}, bf16[2,4,48,768]{3,2,1,0:T(8,128)(2,1)S(1)}, u32[]{:S(2)}, u32[]{:S(2)}) collective-permute-start(bf16[2,4,48,768]{3,2,1,0:T(8,128)(2,1)S(1)} %pad_maximum_fusion.1.own), channel_id=1, source_target_pairs={{0,4},{1,3},{2,6},{3,1},{4,0},{5,7},{6,2},{7,5},{8,12},{9,11},{10,... | collective-permute-start | bytes 1769480 | tf_op jit(solution)/shard_map/ppermute | solution.py:185
  41.2 7.3 %collective-permute-start.1 = (bf16[2,32,1536]{2,1,0:T(8,128)(2,1)S(1)}, bf16[2,32,1536]{2,1,0:T(8,128)(2,1)S(1)}, u32[]{:S(2)}, u32[]{:S(2)}) collective-permute-start(bf16[2,32,1536]{2,1,0:T(8,128)(2,1)S(1)} %get-tuple-element.40), channel_id=1, source_target_pairs={{1,0},{2,1},{3,2},{4,3},{5,4},{6,5},{7,6},{9,8},{10,9},{11,10},{12... | collective-permute-start | bytes 589832 | tf_op jit(solution)/shard_map/ppermute | solution.py:40
  48.5 12.9 %collective-permute-start = (bf16[2,32,1536]{2,1,0:T(8,128)(2,1)S(1)}, bf16[2,32,1536]{2,1,0:T(8,128)(2,1)S(1)}, u32[]{:S(2)}, u32[]{:S(2)}) collective-permute-start(bf16[2,32,1536]{2,1,0:T(8,128)(2,1)S(1)} %get-tuple-element.41), channel_id=1, source_target_pairs={{0,1},{1,2},{2,3},{3,4},{4,5},{5,6},{6,7},{8,9},{9,10},{10,11},{11... | collective-permute-start | bytes 589832 | tf_op jit(solution)/shard_map/ppermute | solution.py:39
  53.4 10.0 %collective-permute-start.16 = (bf16[2,4,48,768]{3,2,1,0:T(8,128)(2,1)S(1)}, bf16[2,4,48,768]{3,2,1,0:T(8,128)(2,1)S(1)}, u32[]{:S(2)}, u32[]{:S(2)}) collective-permute-start(bf16[2,4,48,768]{3,2,1,0:T(8,128)(2,1)S(1)} %collective-permute-done.14.own_far), channel_id=1, source_target_pairs={{0,1},{1,0},{2,3},{3,2},{4,5},{5,4},{6,7},{7,6},{8,9},{9,8},{10,11... | collective-permute-start | bytes 1769480 | tf_op jit(solution)/shard_map/ppermute | solution.py:187
  61.4 4.4 %collective-permute-start.10 = (bf16[2,4,48,768]{3,2,1,0:T(8,128)(2,1)S(1)}, bf16[2,4,48,768]{3,2,1,0:T(8,128)(2,1)S(1)}, u32[]{:S(2)}, u32[]{:S(2)}) collective-permute-start(bf16[2,4,48,768]{3,2,1,0:T(8,128)(2,1)S(1)} %pad_maximum_fusion.1.own), channel_id=1, source_target_pairs={{0,1},{1,0},{2,3},{3,2},{4,5},{5,4},{6,7},{7,6},{8,9},{9,8},{10,11... | collective-permute-start | bytes 1769480 | tf_op jit(solution)/shard_map/ppermute | solution.py:186
  61.4 4.4 %collective-permute-start.11 = (bf16[2,4,48,768]{3,2,1,0:T(8,128)(2,1)S(1)}, bf16[2,4,48,768]{3,2,1,0:T(8,128)(2,1)S(1)}, u32[]{:S(2)}, u32[]{:S(2)}) collective-permute-start(bf16[2,4,48,768]{3,2,1,0:T(8,128)(2,1)S(1)} %collective-permute-done.9.own_far), channel_id=1, source_target_pairs={{0,1},{1,0},{2,3},{3,2},{4,5},{5,4},{6,7},{7,6},{8,9},{9,8},{10,11... | collective-permute-start | bytes 1769480 | tf_op jit(solution)/shard_map/ppermute | solution.py:187
  61.9 6.3 %collective-permute-start.5 = (bf16[2,4,48,768]{3,2,1,0:T(8,128)(2,1)S(1)}, bf16[2,4,48,768]{3,2,1,0:T(8,128)(2,1)S(1)}, u32[]{:S(2)}, u32[]{:S(2)}) collective-permute-start(bf16[2,4,48,768]{3,2,1,0:T(8,128)(2,1)S(1)} %pad_maximum_fusion.own), channel_id=1, source_target_pairs={{0,1},{1,0},{2,3},{3,2},{4,5},{5,4},{6,7},{7,6},{8,9},{9,8},{10,11... | collective-permute-start | bytes 1769480 | tf_op jit(solution)/shard_map/ppermute | solution.py:186
  62.0 6.2 %collective-permute-start.6 = (bf16[2,4,48,768]{3,2,1,0:T(8,128)(2,1)S(1)}, bf16[2,4,48,768]{3,2,1,0:T(8,128)(2,1)S(1)}, u32[]{:S(2)}, u32[]{:S(2)}) collective-permute-start(bf16[2,4,48,768]{3,2,1,0:T(8,128)(2,1)S(1)} %collective-permute-done.4.own_far), channel_id=1, source_target_pairs={{0,1},{1,0},{2,3},{3,2},{4,5},{5,4},{6,7},{7,6},{8,9},{9,8},{10,11... | collective-permute-start | bytes 1769480 | tf_op jit(solution)/shard_map/ppermute | solution.py:187
  71.2 6.8 %collective-permute-start.18 = (bf16[2,32,768]{2,1,0:T(8,128)(2,1)S(1)}, bf16[2,32,768]{2,1,0:T(8,128)(2,1)S(1)}, u32[]{:S(2)}, u32[]{:S(2)}) collective-permute-start(bf16[2,32,768]{2,1,0:T(8,128)(2,1)S(1)} %get-tuple-element.44), channel_id=1, source_target_pairs={{1,0},{2,1},{3,2},{4,3},{5,4},{6,5},{7,6},{9,8},{10,9},{11,10},{12... | collective-permute-start | bytes 294920 | tf_op jit(solution)/shard_map/ppermute | solution.py:40
  73.1 6.8 %collective-permute-start.17 = (bf16[2,32,768]{2,1,0:T(8,128)(2,1)S(1)}, bf16[2,32,768]{2,1,0:T(8,128)(2,1)S(1)}, u32[]{:S(2)}, u32[]{:S(2)}) collective-permute-start(bf16[2,32,768]{2,1,0:T(8,128)(2,1)S(1)} %get-tuple-element.45), channel_id=1, source_target_pairs={{0,1},{1,2},{2,3},{3,4},{4,5},{5,6},{6,7},{8,9},{9,10},{10,11},{11... | collective-permute-start | bytes 294920 | tf_op jit(solution)/shard_map/ppermute | solution.py:39

commit v2 on v1

v2 whole, which is shorter than its diff:
```python
import functools
import jax
import jax.numpy as jnp
from jax import lax
from jax.experimental import pallas as pl
from jax.experimental.pallas import tpu as pltpu
from jax.sharding import PartitionSpec as P

DILATION_STEP = 32
PLANE = 8
F32 = jnp.float32
BF16 = jnp.bfloat16
ROOT = 0.7978845608028654
CUBIC = 0.044715


def gelu(v):
    return 0.5 * v * (1.0 + jnp.tanh(ROOT * (v + CUBIC * (v * v * v))))


def gelu_slope(v):
    square = v * v
    t = jnp.tanh(ROOT * v * (1.0 + CUBIC * square))
    return 0.5 * (1.0 + t) + (0.5 * ROOT) * v * (1.0 - t * t) * (1.0 + 3.0 * CUBIC * square)


def flip(index, bit):
    return index + bit - 2 * bit * ((index // bit) % 2)


def halo(block, width):
    count = lax.axis_size("seq")
    forward = [(i, i + 1) for i in range(count - 1)]
    backward = [(target, source) for source, target in forward]
    low = lax.ppermute(block[:, -width:], "seq", forward)
    high = lax.ppermute(block[:, :width], "seq", backward)
    return low, high


def plane_pairs(count, bit_even, bit_odd):
    return [(i, i ^ (bit_odd if i % 2 else bit_even)) for i in range(count)]


def slot_columns(slot, width):
    z = lax.axis_index("dp")
    upper = z // 2
    shard = (z, flip(z, 1), 2 - upper, 3 - 3 * upper)[slot]
    return pl.ds(pl.multiple_of(shard * width, 128), width)


def held(name):
    s = lax.axis_index("seq") % PLANE

    def moved(index, step):
        return index + step - 2 * step * ((index // step) % 2)

    first = 2 + 2 * (s % 2)
    second = 6 - first
    mate = flip(s, 1)
    return {
        "near": (s, moved(s, first)),
        "far": (moved(s, second), flip(flip(s, 2), 4)),
        "mate_near": (mate, moved(mate, second)),
        "mate_far": (moved(mate, first), flip(flip(mate, 2), 4)),
    }[name]


def slice_kernel(tap, out, piece, stage, sem):
    s = lax.axis_index("seq") % PLANE
    matrix, half = s // 2, s % 2
    size = piece.shape[0]
    part = pl.ds(pl.multiple_of(half * size, 128), size)

    @pl.when(matrix < 3)
    def _():
        copy = pltpu.make_async_copy(tap.at[matrix, :, part], piece, sem)
        copy.start()
        copy.wait()

    @pl.when(matrix == 3)
    def _():
        copy = pltpu.make_async_copy(out.at[part, :], stage, sem)
        copy.start()
        copy.wait()
        piece[...] = stage[...].T


def left_kernel(signal, cot, low, high, left, slope):
    reach = 2 * DILATION_STEP
    windows, rows, _ = signal.shape
    for w in range(windows):
        wide = signal[w].astype(F32)
        square = wide * wide
        t = jnp.tanh(ROOT * wide * (1.0 + CUBIC * square))
        left[0, w, reach : reach + rows] = (0.5 * wide * (1.0 + t)).astype(BF16)
        slope[w] = 0.5 * (1.0 + t) + (0.5 * ROOT) * wide * (1.0 - t * t) * (1.0 + 3.0 * CUBIC * square)
        left[0, w, 0:reach] = gelu(low[w, 0:reach].astype(F32)).astype(BF16)
        left[0, w, reach + rows :] = gelu(high[w, DILATION_STEP:].astype(F32)).astype(BF16)
        left[1, w, 0:DILATION_STEP] = low[w, reach:]
        left[1, w, DILATION_STEP : DILATION_STEP + rows] = cot[w]
        left[1, w, DILATION_STEP + rows : reach + rows] = high[w, 0:DILATION_STEP]
        left[1, w, reach + rows :] = jnp.zeros_like(left[1, w, reach + rows :])


def rows_of(left, which, offset, rows, columns):
    return jnp.concatenate([left[which, w, pl.ds(offset, rows), columns] for w in range(left.shape[1])], axis=0)


LAST = (((1,), (1,)), ((), ()))


def own_kernel(left, tap, out, sums):
    rows = left.shape[2] - 2 * DILATION_STEP
    columns = slot_columns(0, tap.shape[1])
    inner = None
    for k in range(3):
        term = jnp.dot(rows_of(left, 0, k * DILATION_STEP, rows, columns), tap[k], preferred_element_type=F32)
        inner = term if inner is None else inner + term
    sums[0] = inner
    sums[1] = lax.dot_general(rows_of(left, 1, 0, rows, columns), out[...], LAST, preferred_element_type=F32)


def slot_kernel(slot, names, fresh, *refs):
    count = len(names)
    left, sums_in = refs[0], refs[1]
    buffers = refs[2 : 2 + count]
    sums, whole, sems = refs[-3:]
    rows = left.shape[2] - 2 * DILATION_STEP
    size = buffers[0].shape[1]
    columns = slot_columns(slot, size)
    pieces = [(b, i, q) for b, name in zip(buffers, names) for i, q in enumerate(held(name))]
    copies = []
    for n, (buffer, i, q) in enumerate(pieces):
        half = pl.ds(pl.multiple_of((q % 2) * size, 128), size)
        copies.append(pltpu.make_async_copy(buffer.at[i], whole.at[q // 2, :, half], sems.at[n]))
        copies[-1].start()
    for buffer, name in zip(buffers, names):
        terms = []
        for i, q in enumerate(held(name)):
            matrix = q // 2
            offset = pl.multiple_of((matrix % 3) * DILATION_STEP, DILATION_STEP)
            lhs = rows_of(left, matrix // 3, offset, rows, columns)
            terms.append((matrix // 3, jnp.dot(lhs, buffer[i], preferred_element_type=F32)))
        half = pl.ds(pl.multiple_of((held(name)[0] % 2) * size, 128), size)
        for which in range(2):
            total = sums_in[which, :, half]
            for place, term in terms:
                total = total + jnp.where(place == which, term, 0.0)
            sums[which, :, half] = total
    for copy in copies:
        copy.wait()


def middle_kernel(sums, right):
    windows, rows = right.shape[1:3]
    v = sums[0]
    square = v * v
    t = jnp.tanh(ROOT * v * (1.0 + CUBIC * square))
    slope = 0.5 * (1.0 + t) + (0.5 * ROOT) * v * (1.0 - t * t) * (1.0 + 3.0 * CUBIC * square)
    right[0] = (sums[1] * slope).astype(BF16).reshape(right.shape[1:])
    active = (0.5 * v * (1.0 + t)).astype(BF16).reshape(right.shape[1:])
    right[1, :, 2 * DILATION_STEP :] = active[:, DILATION_STEP : rows - DILATION_STEP]


def back_kernel(signal, cot, slope, right, tap, out, *refs):
    wholes, (result, grad) = refs[:3], refs[3:]
    windows, rows, _ = signal.shape
    width = tap.shape[1]
    step = DILATION_STEP
    everything = slice(None)
    shifted = [rows_of(right, 0, (2 - k) * step, rows, everything) for k in range(3)]
    active = rows_of(right, 1, 2 * step, rows, everything)
    for slot in range(4):
        columns = slot_columns(slot, width)
        matrices = tap if slot == 0 else wholes[slot - 1]
        total = None
        for k in range(3):
            term = lax.dot_general(shifted[k], matrices[k], LAST, preferred_element_type=F32)
            total = term if total is None else total + term
        if slot == 0:
            more = jnp.dot(active, out[...], preferred_element_type=F32)
        else:
            more = lax.dot_general(active, matrices[3], LAST, preferred_element_type=F32)
        for w in range(windows):
            at = slice(w * rows, (w + 1) * rows)
            grad[w, :, columns] = (cot[w, :, columns].astype(F32) + total[at] * slope[w, :, columns]).astype(BF16)
            result[w, :, columns] = (signal[w, :, columns].astype(F32) + more[at]).astype(BF16)


def cost(microseconds):
    return pl.CostEstimate(flops=int(microseconds * 9e8), bytes_accessed=int(microseconds * 3e6), transcendentals=0)


def params(mib):
    return pltpu.CompilerParams(vmem_limit_bytes=mib << 20)


def tie(*values):
    return lax.optimization_barrier(values)


def per_device(signal, tap, out, cot):
    windows, rows, channels = signal.shape
    hidden = tap.shape[2]
    width = tap.shape[1]
    wide_rows = rows + 2 * DILATION_STEP
    vmem = pl.BlockSpec(memory_space=pltpu.VMEM)
    hbm = pl.BlockSpec(memory_space=pl.ANY)
    count = lax.axis_size("seq")
    z = lax.axis_index("dp")
    middle = (z == 1) | (z == 2)

    mine = pl.pallas_call(
        slice_kernel,
        out_shape=jax.ShapeDtypeStruct((width, width), BF16),
        in_specs=[hbm] * 2,
        out_specs=vmem,
        scratch_shapes=[pltpu.VMEM((width, width), BF16), pltpu.SemaphoreType.DMA],
        compiler_params=params(60),
    )(tap, out)

    def across(block, even, odd):
        return lax.ppermute(block, "seq", plane_pairs(count, even, odd))

    outward = [(1, 0), (2, 3)]
    inward = [(1, 2), (2, 1)]
    sums_shape = jax.ShapeDtypeStruct((2, windows * wide_rows, hidden), F32)
    whole_shape = jax.ShapeDtypeStruct((4, width, hidden), BF16)

    def add_slot(slot, names, buffers, left, sums, whole=None):
        fresh = whole is None
        given = [left, sums, *buffers] + ([] if fresh else [whole])
        aliases = {1: 0}
        if not fresh:
            aliases[len(given) - 1] = 1
        return pl.pallas_call(
            functools.partial(slot_kernel, slot, names, fresh),
            out_shape=[sums_shape, whole_shape],
            in_specs=[vmem] * len(given),
            out_specs=[vmem] * 2,
            scratch_shapes=[pltpu.SemaphoreType.DMA((2 * len(names),))],
            input_output_aliases=aliases,
            compiler_params=params(16),
            cost_estimate=cost(0.5 * len(names)),
        )(*given)

    p1 = lax.ppermute(mine, "dp", [(0, 1), (1, 0), (2, 3), (3, 2)])
    reach = 2 * DILATION_STEP
    low, high = (
        jnp.concatenate([signal[:, -reach:], cot[:, -DILATION_STEP:]], axis=1),
        jnp.concatenate([cot[:, :DILATION_STEP], signal[:, :reach]], axis=1),
    )
    low, high, mine = tie(low, high, mine)
    p2 = lax.ppermute(mine, "dp", inward)
    low = lax.ppermute(low, "seq", [(i, i + 1) for i in range(count - 1)])
    high = lax.ppermute(high, "seq", [(i + 1, i) for i in range(count - 1)])

    near1 = across(p1, 2, 4)
    p4 = lax.ppermute(p1, "dp", inward)
    p3 = lax.ppermute(p2, "dp", outward)
    left, slope = pl.pallas_call(
        left_kernel,
        out_shape=[
            jax.ShapeDtypeStruct((2, windows, rows + 2 * reach, channels), BF16),
            jax.ShapeDtypeStruct(signal.shape, F32),
        ],
        in_specs=[vmem] * 4,
        out_specs=[vmem] * 2,
        compiler_params=params(16),
        cost_estimate=cost(2.5),
    )(signal, cot, low, high)
    sums = pl.pallas_call(
        own_kernel,
        out_shape=sums_shape,
        in_specs=[vmem] * 3,
        out_specs=vmem,
        compiler_params=params(16),
        cost_estimate=cost(1.5),
    )(left, tap, out)
    own1 = jnp.stack([p1, near1])
    far1 = across(own1, 4, 2)
    mate1 = across(own1, 1, 1)
    got2 = jnp.where(middle, p2, p3)
    near2 = across(got2, 2, 4)
    p5 = lax.ppermute(p4, "dp", outward)
    near_names, far_names = ("near", "mate_near"), ("far", "mate_far")
    own2 = jnp.stack([got2, near2])
    own2, sums = tie(own2, sums)
    far2 = across(own2, 4, 2)
    mate2 = across(own2, 1, 1)
    far_mate1 = across(far1, 1, 1)
    sums, whole1 = add_slot(1, near_names, (own1, mate1), left, sums)
    got3 = jnp.where(middle, p4, p5)
    got3, sums = tie(got3, sums)
    near3 = across(got3, 2, 4)
    own3 = jnp.stack([got3, near3])
    sums, whole1 = add_slot(1, far_names, (far1, far_mate1), left, sums, whole1)
    own3, sums = tie(own3, sums)
    far3 = across(own3, 4, 2)
    mate3 = across(own3, 1, 1)
    far_mate2 = across(far2, 1, 1)
    sums, whole2 = add_slot(2, near_names, (own2, mate2), left, sums)
    sums, whole2 = add_slot(2, far_names, (far2, far_mate2), left, sums, whole2)
    sums, whole3 = add_slot(3, near_names, (own3, mate3), left, sums)
    far3, sums = tie(far3, sums)
    far_mate3 = across(far3, 1, 1)
    sums, whole3 = add_slot(3, far_names, (far3, far_mate3), left, sums, whole3)

    right = pl.pallas_call(
        middle_kernel,
        out_shape=jax.ShapeDtypeStruct((2, windows, wide_rows, hidden), BF16),
        in_specs=[vmem],
        out_specs=vmem,
        compiler_params=params(16),
        cost_estimate=cost(0.8),
    )(sums)
    result, grad_signal = pl.pallas_call(
        back_kernel,
        out_shape=[jax.ShapeDtypeStruct(signal.shape, BF16)] * 2,
        in_specs=[vmem] * 9,
        out_specs=[vmem] * 2,
        compiler_params=params(24),
        cost_estimate=cost(4.5),
    )(signal, cot, slope, right, tap, out, whole1, whole2, whole3)
    return result, grad_signal


def extended(block, width):
    low, high = halo(block, width)
    return jnp.concatenate([low, block, high], axis=1)


def per_device_general(signal, tap, out, cot):
    tap = lax.all_gather(tap, "dp", axis=1, tiled=True)
    out = lax.all_gather(out, "dp", axis=1, tiled=True)
    rows = signal.shape[1]
    wide = signal.astype(F32)
    act = extended(gelu(wide).astype(BF16), DILATION_STEP)

    def contract(rule, a, b):
        return jnp.einsum(rule, a, b, preferred_element_type=F32)

    def window(block, k):
        return block[:, k * DILATION_STEP : k * DILATION_STEP + rows]

    inner = sum(contract("wtc,ch->wth", window(act, k), tap[k]) for k in range(3))
    active = gelu(inner).astype(BF16)
    result = wide + contract("wth,hc->wtc", active, out)
    grad_inner = (contract("wtc,hc->wth", cot, out) * gelu_slope(inner)).astype(BF16)
    grad_inner = extended(grad_inner, DILATION_STEP)
    grad_act = sum(contract("wth,ch->wtc", window(grad_inner, 2 - k), tap[k]) for k in range(3))
    grad_signal = cot.astype(F32) + grad_act * gelu_slope(wide)
    return result.astype(BF16), grad_signal.astype(BF16)


def solution(mesh):
    dp, seq = mesh.shape["dp"], mesh.shape["seq"]

    def run(signal, tap, out, cot):
        width = tap.shape[1] // dp
        hidden = tap.shape[2]
        sliced = dp == 4 and seq % PLANE == 0 and width % 128 == 0 and 2 * width == hidden
        body = per_device if sliced else per_device_general
        return jax.shard_map(
            body,
            mesh=mesh,
            in_specs=(P("dp", "seq", None), P(None, "dp", None), P(None, "dp"), P("dp", "seq", None)),
            out_specs=(P("dp", "seq", None), P("dp", "seq", None)),
            check_vma=False,
        )(signal, tap, out, cot)

    return run
```

time: 83 us -> 75.9 us (0.914)
  the two profiles are of different devices: /device:TPU:20 before, /device:TPU:0 now
where the time goes in v2:
time: 75.9 us; the launch traced here: 75.5 us
  waiting for transfers between devices  26.4 us (35%)
  starting transfers between devices  25.9 us (34%)
  Pallas kernels  18.9 us (25%)
  other arithmetic  3.19 us (4%)
  between operations  0.92 us (1%)
    ppermute x12, waiting for transfers between devices, across(): return lax.ppermute(block, 'seq', plane_pairs(count, even, odd))  17.8 us
    ppermute x12, starting transfers between devices, across(): return lax.ppermute(block, 'seq', plane_pairs(count, even, odd))  15.6 us
    pallas_call x6, Pallas kernels, add_slot(): pl.pallas_call(functools.partial(slot_kernel, slot, names, fresh), out_sh...  8.9 us
    ppermute x1, waiting for transfers between devices, per_device(): p1 = lax.ppermute(mine, 'dp', [(0, 1), (1, 0), (2, 3), (3, 2)])  4.95 us
    pallas_call x1, Pallas kernels, per_device(): pl.pallas_call(back_kernel, out_shape=[jax.ShapeDtypeStruct(signal.shape,...  4.43 us
    ppermute x1, starting transfers between devices, per_device(): p1 = lax.ppermute(mine, 'dp', [(0, 1), (1, 0), (2, 3), (3, 2)])  3.09 us
    ppermute x1, waiting for transfers between devices, per_device(): p3 = lax.ppermute(p2, 'dp', outward)  2.7 us
    pallas_call x1, Pallas kernels, per_device(): pl.pallas_call(slice_kernel, out_shape=jax.ShapeDtypeStruct((width, width...  1.82 us
  transfers between devices with their start and end apart: 19, of which 8 were waited for; matrix products, arithmetic and copies ran while one was open for 4% of the time, Pallas kernels for 14%

profile of v2, /device:TPU:0, one launch (start us, length us, event | category | flops | bytes accessed | tf_op | source)
XLA Modules:
  0.0 75.5 jit_solution(8867809700503152696)
XLA Ops:
  0.6 1.8 %shard_map.59 = bf16[384,384]{1,0:T(8,128)(2,1)} custom-call(bf16[3,384,768]{2,1,0:T(8,128)(2,1)} %tap.5, bf16[768,384]{1,0:T(8,128)(2,1)} %out.5), custom_call_target="tpu_custom_call" | custom-call | tf_op jit(solution)/shard_map/pallas_call | solution.py:213
  2.5 3.1 %collective-permute-start.2 = (bf16[384,384]{1,0:T(8,128)(2,1)}, bf16[384,384]{1,0:T(8,128)(2,1)}, u32[]{:S(2)}, u32[]{:S(2)}) collective-permute-start(bf16[384,384]{1,0:T(8,128)(2,1)} %shard_map.59), channel_id=1, source_target_pairs={{0,8},{8,0},{16,24},{24,16},{1,9},{9,1},{17,25},{25,17},{2,10},{10... | collective-permute-start | bytes 884744 | tf_op jit(solution)/shard_map/ppermute | solution.py:247
  6.6 1.4 %collective-permute-start.5 = (bf16[384,384]{1,0:T(8,128)(2,1)S(1)}, bf16[384,384]{1,0:T(8,128)(2,1)}, u32[]{:S(2)}, u32[]{:S(2)}) collective-permute-start(bf16[384,384]{1,0:T(8,128)(2,1)S(1)} %copy-done.4), channel_id=1, source_target_pairs={{8,16},{16,8},{9,17},{17,9},{10,18},{18,10},{11,19},{19,11},{12,20... | collective-permute-start | bytes 884744 | tf_op jit(solution)/shard_map/ppermute | solution.py:254
  8.0 4.9 %collective-permute-done.2 = bf16[384,384]{1,0:T(8,128)(2,1)} collective-permute-done((bf16[384,384]{1,0:T(8,128)(2,1)}, bf16[384,384]{1,0:T(8,128)(2,1)}, u32[]{:S(2)}, u32[]{:S(2)}) %collective-permute-start.2) | collective-permute-done | bytes 294944 | tf_op jit(solution)/shard_map/ppermute | solution.py:247
  12.9 1.7 %collective-permute-start.8 = (bf16[384,384]{1,0:T(8,128)(2,1)}, bf16[384,384]{1,0:T(8,128)(2,1)}, u32[]{:S(2)}, u32[]{:S(2)}) collective-permute-start(bf16[384,384]{1,0:T(8,128)(2,1)} %collective-permute-done.2), channel_id=1, source_target_pairs={{0,2},{1,5},{2,0},{3,7},{4,6},{5,1},{6,4},{7,3},{8,10},{9,13},{10,... | collective-permute-start | bytes 884744 | tf_op jit(solution)/shard_map/ppermute | solution.py:223
  14.6 1.3 %collective-permute-start = (bf16[2,96,1536]{2,1,0:T(8,128)(2,1)}, bf16[2,96,1536]{2,1,0:T(8,128)(2,1)S(1)}, u32[]{:S(2)}, u32[]{:S(2)}) collective-permute-start(bf16[2,96,1536]{2,1,0:T(8,128)(2,1)} %get-tuple-element.27), channel_id=1, source_target_pairs={{0,1},{1,2},{2,3},{3,4},{4,5},{5,6},{6,7},{8,9},{9,10},{10,11},{11... | collective-permute-start | bytes 1769480 | tf_op jit(solution)/shard_map/ppermute | solution.py:255
  19.2 1.3 %collective-permute-done.8 = bf16[384,384]{1,0:T(8,128)(2,1)} collective-permute-done((bf16[384,384]{1,0:T(8,128)(2,1)}, bf16[384,384]{1,0:T(8,128)(2,1)}, u32[]{:S(2)}, u32[]{:S(2)}) %collective-permute-start.8) | collective-permute-done | bytes 294944 | tf_op jit(solution)/shard_map/ppermute | solution.py:223
  21.6 4.2 %collective-permute-start.11 = (bf16[2,384,384]{2,1,0:T(8,128)(2,1)S(1)}, bf16[2,384,384]{2,1,0:T(8,128)(2,1)S(1)}, u32[]{:S(2)}, u32[]{:S(2)}) collective-permute-start(bf16[2,384,384]{2,1,0:T(8,128)(2,1)S(1)} %pad_maximum_fusion.3.refs_2_), channel_id=1, source_target_pairs={{0,4},{1,3},{2,6},{3,1},{4,0},{5,7},{6,2},{7,5},{8,12},{9,11},{10,... | collective-permute-start | bytes 1769480 | tf_op jit(solution)/shard_map/ppermute | solution.py:223
  25.9 2.7 %collective-permute-done.6 = bf16[384,384]{1,0:T(8,128)(2,1)} collective-permute-done((bf16[384,384]{1,0:T(8,128)(2,1)}, bf16[384,384]{1,0:T(8,128)(2,1)}, u32[]{:S(2)}, u32[]{:S(2)}) %collective-permute-start.6) | collective-permute-done | bytes 294944 | tf_op jit(solution)/shard_map/ppermute | solution.py:260
  30.3 3.4 %collective-permute-start.7 = (bf16[384,384]{1,0:T(8,128)(2,1)S(1)}, bf16[384,384]{1,0:T(8,128)(2,1)S(1)}, u32[]{:S(2)}, u32[]{:S(2)}) collective-permute-start(bf16[384,384]{1,0:T(8,128)(2,1)S(1)} %broadcast_select_fusion), channel_id=1, source_target_pairs={{0,2},{1,5},{2,0},{3,7},{4,6},{5,1},{6,4},{7,3},{8,10},{9,13},{10,... | collective-permute-start | bytes 884744 | tf_op jit(solution)/shard_map/ppermute | solution.py:223
  35.0 1.6 %shard_map.60 = (bf16[2,2,256,1536]{3,2,1,0:T(8,128)(2,1)S(1)}, f32[2,128,1536]{2,1,0:T(8,128)S(1)}) custom-call(bf16[2,128,1536]{2,1,0:T(8,128)(2,1)S(1)} %copy-done.2, bf16[2,128,1536]{2,1,0:T(8,128)(2,1)S(1)} %copy-done.3, bf16[2,96,1536]{2,1,0:T(8,128)(2,1)S(1)} %collective-permute-done.low, bf16[2,96,1536]{2,1,0:T(8,128)(2,1)S(1)} %collective-permute-done.1.high), custom_call_target="tpu_custom_call" | custom-call | flops 2249999872 | bytes 7500000 | tf_op jit(solution)/shard_map/pallas_call | solution.py:261
  36.7 1.4 %shard_map.61.refs_1_ = f32[2,384,768]{2,1,0:T(8,128)S(1)} custom-call(bf16[2,2,256,1536]{3,2,1,0:T(8,128)(2,1)S(1)} %get-tuple-element.30.left.refs_0_, bf16[3,384,768]{2,1,0:T(8,128)(2,1)S(1)} %copy-done, bf16[768,384]{1,0:T(8,128)(2,1)S(1)} %copy-done.1), custom_call_target="tpu_custom_call" | custom-call | flops 1350000000 | bytes 4500000 | tf_op jit(solution)/shard_map/pallas_call | solution.py:272
  38.0 3.6 %collective-permute-done.7 = bf16[384,384]{1,0:T(8,128)(2,1)S(1)} collective-permute-done((bf16[384,384]{1,0:T(8,128)(2,1)S(1)}, bf16[384,384]{1,0:T(8,128)(2,1)S(1)}, u32[]{:S(2)}, u32[]{:S(2)}) %collective-permute-start.7) | collective-permute-done | bytes 294944 | tf_op jit(solution)/shard_map/ppermute | solution.py:223
  44.0 1.6 %shard_map.62 = (f32[2,384,768]{2,1,0:T(8,128)S(1)}, bf16[4,384,768]{2,1,0:T(8,128)(2,1)S(1)}) custom-call(bf16[2,2,256,1536]{3,2,1,0:T(8,128)(2,1)S(1)} %get-tuple-element.30.left.refs_0_, f32[2,384,768]{2,1,0:T(8,128)S(1)} %shard_map.61.refs_1_, bf16[2,384,384]{2,1,0:T(8,128)(2,1)S(1)} %pad_maximum_fusion.3.refs_2_, ...), custom_call_target="tpu_custom_call", output_to_operand_aliasing={{0}: (1, {})} | custom-call | flops 900000000 | bytes 3000000 | tf_op jit(solution)/shard_map/pallas_call | solution.py:236
  45.6 2.7 %collective-permute-start.10 = (bf16[384,384]{1,0:T(8,128)(2,1)S(1)}, bf16[384,384]{1,0:T(8,128)(2,1)S(1)}, u32[]{:S(2)}, u32[]{:S(2)}) collective-permute-start(bf16[384,384]{1,0:T(8,128)(2,1)S(1)} %broadcast_select_fusion.1), channel_id=1, source_target_pairs={{0,2},{1,5},{2,0},{3,7},{4,6},{5,1},{6,4},{7,3},{8,10},{9,13},{10,... | collective-permute-start | bytes 884744 | tf_op jit(solution)/shard_map/ppermute | solution.py:223
  48.3 6.5 %collective-permute-done.15.refs_2_ = bf16[2,384,384]{2,1,0:T(8,128)(2,1)S(1)} collective-permute-done((bf16[2,384,384]{2,1,0:T(8,128)(2,1)S(1)}, bf16[2,384,384]{2,1,0:T(8,128)(2,1)S(1)}, u32[]{:S(2)}, u32[]{:S(2)}) %collective-permute-start.15) | collective-permute-done | bytes 589856 | tf_op jit(solution)/shard_map/ppermute | solution.py:223
  54.9 1.5 %shard_map.63 = (f32[2,384,768]{2,1,0:T(8,128)S(1)}, bf16[4,384,768]{2,1,0:T(8,128)(2,1)S(1)}) custom-call(bf16[2,2,256,1536]{3,2,1,0:T(8,128)(2,1)S(1)} %get-tuple-element.30.left.refs_0_, f32[2,384,768]{2,1,0:T(8,128)S(1)} %get-tuple-element.35.refs_1_, ...), custom_call_target="tpu_custom_call", output_to_operand_aliasing={{0}: (1, {}), {1}: (4, {})} | custom-call | flops 900000000 | bytes 3000000 | tf_op jit(solution)/shard_map/pallas_call | solution.py:236
  58.1 1.4 %shard_map.64 = (f32[2,384,768]{2,1,0:T(8,128)S(1)}, bf16[4,384,768]{2,1,0:T(8,128)(2,1)S(1)}) custom-call(bf16[2,2,256,1536]{3,2,1,0:T(8,128)(2,1)S(1)} %get-tuple-element.30.left.refs_0_, f32[2,384,768]{2,1,0:T(8,128)S(1)} %get-tuple-element.39.refs_1_, bf16[2,384,384]{2,1,0:T(8,128)(2,1)S(1)} %pad_maximum_fusion.2.refs_2_, ...), custom_call_target="tpu_custom_call", output_to_operand_aliasing={{0}: (1, {})} | custom-call | flops 900000000 | bytes 3000000 | tf_op jit(solution)/shard_map/pallas_call | solution.py:236
  59.5 1.5 %shard_map.65 = (f32[2,384,768]{2,1,0:T(8,128)S(1)}, bf16[4,384,768]{2,1,0:T(8,128)(2,1)S(1)}) custom-call(bf16[2,2,256,1536]{3,2,1,0:T(8,128)(2,1)S(1)} %get-tuple-element.30.left.refs_0_, f32[2,384,768]{2,1,0:T(8,128)S(1)} %get-tuple-element.41.refs_1_, ...), custom_call_target="tpu_custom_call", output_to_operand_aliasing={{0}: (1, {}), {1}: (4, {})} | custom-call | flops 900000000 | bytes 3000000 | tf_op jit(solution)/shard_map/pallas_call | solution.py:236
  61.1 1.5 %shard_map.66 = (f32[2,384,768]{2,1,0:T(8,128)S(1)}, bf16[4,384,768]{2,1,0:T(8,128)(2,1)S(1)}) custom-call(bf16[2,2,256,1536]{3,2,1,0:T(8,128)(2,1)S(1)} %get-tuple-element.30.left.refs_0_, f32[2,384,768]{2,1,0:T(8,128)S(1)} %get-tuple-element.43.refs_1_, bf16[2,384,384]{2,1,0:T(8,128)(2,1)S(1)} %pad_maximum_fusion.4.refs_2_, ...), custom_call_target="tpu_custom_call", output_to_operand_aliasing={{0}: (1, {})} | custom-call | flops 900000000 | bytes 3000000 | tf_op jit(solution)/shard_map/pallas_call | solution.py:236
  62.5 4.3 %collective-permute-done.13.refs_2_ = bf16[2,384,384]{2,1,0:T(8,128)(2,1)S(1)} collective-permute-done((bf16[2,384,384]{2,1,0:T(8,128)(2,1)S(1)}, bf16[2,384,384]{2,1,0:T(8,128)(2,1)S(1)}, u32[]{:S(2)}, u32[]{:S(2)}) %collective-permute-start.13) | collective-permute-done | bytes 589856 | tf_op jit(solution)/shard_map/ppermute | solution.py:223
  66.9 2.0 %collective-permute-done.18.refs_3_ = bf16[2,384,384]{2,1,0:T(8,128)(2,1)S(1)} collective-permute-done((bf16[2,384,384]{2,1,0:T(8,128)(2,1)S(1)}, bf16[2,384,384]{2,1,0:T(8,128)(2,1)S(1)}, u32[]{:S(2)}, u32[]{:S(2)}) %collective-permute-start.18) | collective-permute-done | bytes 589856 | tf_op jit(solution)/shard_map/ppermute | solution.py:223
  68.9 1.4 %shard_map.67 = (f32[2,384,768]{2,1,0:T(8,128)S(1)}, bf16[4,384,768]{2,1,0:T(8,128)(2,1)S(1)}) custom-call(bf16[2,2,256,1536]{3,2,1,0:T(8,128)(2,1)S(1)} %get-tuple-element.30.left.refs_0_, f32[2,384,768]{2,1,0:T(8,128)S(1)} %get-tuple-element.45.refs_1_, ...), custom_call_target="tpu_custom_call", output_to_operand_aliasing={{0}: (1, {}), {1}: (4, {})} | custom-call | flops 900000000 | bytes 3000000 | tf_op jit(solution)/shard_map/pallas_call | solution.py:236
  71.1 4.4 %shard_map.69 = (bf16[2,128,1536]{2,1,0:T(8,128)(2,1)}, bf16[2,128,1536]{2,1,0:T(8,128)(2,1)}) custom-call(bf16[2,128,1536]{2,1,0:T(8,128)(2,1)S(1)} %copy-done.2, bf16[2,128,1536]{2,1,0:T(8,128)(2,1)S(1)} %copy-done.3, f32[2,128,1536]{2,1,0:T(8,128)S(1)} %get-tuple-element.29.slope, bf16[2,2,192,768]{3,2,1,0:T(8,128)(2,1)S(1)} %shard_map.68.right, ...), custom_call_target="tpu_custom_call" | custom-call | flops 4049999872 | bytes 13500000 | tf_op jit(solution)/shard_map/pallas_call | solution.py:317
  (43 shorter events, 13.3 us)
Async XLA Ops:
  0.6 4.9 %copy-start.3 = (bf16[2,128,1536]{2,1,0:T(8,128)(2,1)S(1)}, bf16[2,128,1536]{2,1,0:T(8,128)(2,1)}, u32[]{:S(2)}) copy-start(bf16[2,128,1536]{2,1,0:T(8,128)(2,1)} %cot.3) | copy-start | bytes 2359300
  0.6 5.0 %copy-start.2 = (bf16[2,128,1536]{2,1,0:T(8,128)(2,1)S(1)}, bf16[2,128,1536]{2,1,0:T(8,128)(2,1)}, u32[]{:S(2)}) copy-start(bf16[2,128,1536]{2,1,0:T(8,128)(2,1)} %signal.3) | copy-start | bytes 2359300
  2.5 4.1 %copy-start.4 = (bf16[384,384]{1,0:T(8,128)(2,1)S(1)}, bf16[384,384]{1,0:T(8,128)(2,1)}, u32[]{:S(2)}) copy-start(bf16[384,384]{1,0:T(8,128)(2,1)} %shard_map.59) | copy-start | bytes 884740
  2.5 10.4 %collective-permute-start.2 = (bf16[384,384]{1,0:T(8,128)(2,1)}, bf16[384,384]{1,0:T(8,128)(2,1)}, u32[]{:S(2)}, u32[]{:S(2)}) collective-permute-start(bf16[384,384]{1,0:T(8,128)(2,1)} %shard_map.59), channel_id=1, source_target_pairs={{0,8},{8,0},{16,24},{24,16},{1,9},{9,1},{17,25},{25,17},{2,10},{10... | collective-permute-start | bytes 884744 | tf_op jit(solution)/shard_map/ppermute | solution.py:247
  6.6 10.6 %collective-permute-start.5 = (bf16[384,384]{1,0:T(8,128)(2,1)S(1)}, bf16[384,384]{1,0:T(8,128)(2,1)}, u32[]{:S(2)}, u32[]{:S(2)}) collective-permute-start(bf16[384,384]{1,0:T(8,128)(2,1)S(1)} %copy-done.4), channel_id=1, source_target_pairs={{8,16},{16,8},{9,17},{17,9},{10,18},{18,10},{11,19},{19,11},{12,20... | collective-permute-start | bytes 884744 | tf_op jit(solution)/shard_map/ppermute | solution.py:254
  12.9 7.6 %collective-permute-start.8 = (bf16[384,384]{1,0:T(8,128)(2,1)}, bf16[384,384]{1,0:T(8,128)(2,1)}, u32[]{:S(2)}, u32[]{:S(2)}) collective-permute-start(bf16[384,384]{1,0:T(8,128)(2,1)} %collective-permute-done.2), channel_id=1, source_target_pairs={{0,2},{1,5},{2,0},{3,7},{4,6},{5,1},{6,4},{7,3},{8,10},{9,13},{10,... | collective-permute-start | bytes 884744 | tf_op jit(solution)/shard_map/ppermute | solution.py:223
  14.6 19.2 %collective-permute-start = (bf16[2,96,1536]{2,1,0:T(8,128)(2,1)}, bf16[2,96,1536]{2,1,0:T(8,128)(2,1)S(1)}, u32[]{:S(2)}, u32[]{:S(2)}) collective-permute-start(bf16[2,96,1536]{2,1,0:T(8,128)(2,1)} %get-tuple-element.27), channel_id=1, source_target_pairs={{0,1},{1,2},{2,3},{3,4},{4,5},{5,6},{6,7},{8,9},{9,10},{10,11},{11... | collective-permute-start | bytes 1769480 | tf_op jit(solution)/shard_map/ppermute | solution.py:255
  15.9 19.1 %collective-permute-start.1 = (bf16[2,96,1536]{2,1,0:T(8,128)(2,1)S(1)}, bf16[2,96,1536]{2,1,0:T(8,128)(2,1)S(1)}, u32[]{:S(2)}, u32[]{:S(2)}) collective-permute-start(bf16[2,96,1536]{2,1,0:T(8,128)(2,1)S(1)} %get-tuple-element.28), channel_id=1, source_target_pairs={{1,0},{2,1},{3,2},{4,3},{5,4},{6,5},{7,6},{9,8},{10,9},{11,10},{12... | collective-permute-start | bytes 1769480 | tf_op jit(solution)/shard_map/ppermute | solution.py:256
  17.2 11.4 %collective-permute-start.6 = (bf16[384,384]{1,0:T(8,128)(2,1)}, bf16[384,384]{1,0:T(8,128)(2,1)}, u32[]{:S(2)}, u32[]{:S(2)}) collective-permute-start(bf16[384,384]{1,0:T(8,128)(2,1)} %collective-permute-done.5), channel_id=1, source_target_pairs={{8,0},{16,24},{9,1},{17,25},{10,2},{18,26},{11,3},{19,27},{12,4},{... | collective-permute-start | bytes 884744 | tf_op jit(solution)/shard_map/ppermute | solution.py:260
  18.5 11.8 %collective-permute-start.3 = (bf16[384,384]{1,0:T(8,128)(2,1)}, bf16[384,384]{1,0:T(8,128)(2,1)S(1)}, u32[]{:S(2)}, u32[]{:S(2)}) collective-permute-start(bf16[384,384]{1,0:T(8,128)(2,1)} %collective-permute-done.2), channel_id=1, source_target_pairs={{8,16},{16,8},{9,17},{17,9},{10,18},{18,10},{11,19},{19,11},{12,20... | collective-permute-start | bytes 884744 | tf_op jit(solution)/shard_map/ppermute | solution.py:259
  21.6 21.3 %collective-permute-start.11 = (bf16[2,384,384]{2,1,0:T(8,128)(2,1)S(1)}, bf16[2,384,384]{2,1,0:T(8,128)(2,1)S(1)}, u32[]{:S(2)}, u32[]{:S(2)}) collective-permute-start(bf16[2,384,384]{2,1,0:T(8,128)(2,1)S(1)} %pad_maximum_fusion.3.refs_2_), channel_id=1, source_target_pairs={{0,4},{1,3},{2,6},{3,1},{4,0},{5,7},{6,2},{7,5},{8,12},{9,11},{10,... | collective-permute-start | bytes 1769480 | tf_op jit(solution)/shard_map/ppermute | solution.py:223
  28.6 15.4 %collective-permute-start.9 = (bf16[2,384,384]{2,1,0:T(8,128)(2,1)S(1)}, bf16[2,384,384]{2,1,0:T(8,128)(2,1)S(1)}, u32[]{:S(2)}, u32[]{:S(2)}) collective-permute-start(bf16[2,384,384]{2,1,0:T(8,128)(2,1)S(1)} %pad_maximum_fusion.3.refs_2_), channel_id=1, source_target_pairs={{0,1},{1,0},{2,3},{3,2},{4,5},{5,4},{6,7},{7,6},{8,9},{9,8},{10,11... | collective-permute-start | bytes 1769480 | tf_op jit(solution)/shard_map/ppermute | solution.py:223
  30.3 6.3 %copy-start = (bf16[3,384,768]{2,1,0:T(8,128)(2,1)S(1)}, bf16[3,384,768]{2,1,0:T(8,128)(2,1)}, u32[]{:S(2)}) copy-start(bf16[3,384,768]{2,1,0:T(8,128)(2,1)} %tap.5) | copy-start | bytes 5308420
  30.3 6.3 %copy-start.1 = (bf16[768,384]{1,0:T(8,128)(2,1)S(1)}, bf16[768,384]{1,0:T(8,128)(2,1)}, u32[]{:S(2)}) copy-start(bf16[768,384]{1,0:T(8,128)(2,1)} %out.5) | copy-start | bytes 1769476
  30.3 11.3 %collective-permute-start.7 = (bf16[384,384]{1,0:T(8,128)(2,1)S(1)}, bf16[384,384]{1,0:T(8,128)(2,1)S(1)}, u32[]{:S(2)}, u32[]{:S(2)}) collective-permute-start(bf16[384,384]{1,0:T(8,128)(2,1)S(1)} %broadcast_select_fusion), channel_id=1, source_target_pairs={{0,2},{1,5},{2,0},{3,7},{4,6},{5,1},{6,4},{7,3},{8,10},{9,13},{10,... | collective-permute-start | bytes 884744 | tf_op jit(solution)/shard_map/ppermute | solution.py:223
  33.7 10.2 %collective-permute-start.4 = (bf16[384,384]{1,0:T(8,128)(2,1)S(1)}, bf16[384,384]{1,0:T(8,128)(2,1)S(1)}, u32[]{:S(2)}, u32[]{:S(2)}) collective-permute-start(bf16[384,384]{1,0:T(8,128)(2,1)S(1)} %collective-permute-done.3), channel_id=1, source_target_pairs={{8,0},{16,24},{9,1},{17,25},{10,2},{18,26},{11,3},{19,27},{12,4},{... | collective-permute-start | bytes 884744 | tf_op jit(solution)/shard_map/ppermute | solution.py:285
  41.7 13.1 %collective-permute-start.15 = (bf16[2,384,384]{2,1,0:T(8,128)(2,1)S(1)}, bf16[2,384,384]{2,1,0:T(8,128)(2,1)S(1)}, u32[]{:S(2)}, u32[]{:S(2)}) collective-permute-start(bf16[2,384,384]{2,1,0:T(8,128)(2,1)S(1)} %pad_maximum_fusion.2.refs_2_), channel_id=1, source_target_pairs={{0,4},{1,3},{2,6},{3,1},{4,0},{5,7},{6,2},{7,5},{8,12},{9,11},{10,... | collective-permute-start | bytes 1769480 | tf_op jit(solution)/shard_map/ppermute | solution.py:223
  42.9 12.0 %collective-permute-start.12 = (bf16[2,384,384]{2,1,0:T(8,128)(2,1)S(1)}, bf16[2,384,384]{2,1,0:T(8,128)(2,1)S(1)}, u32[]{:S(2)}, u32[]{:S(2)}) collective-permute-start(bf16[2,384,384]{2,1,0:T(8,128)(2,1)S(1)} %collective-permute-done.11.refs_2_), channel_id=1, source_target_pairs={{0,1},{1,0},{2,3},{3,2},{4,5},{5,4},{6,7},{7,6},{8,9},{9,8},{10,11... | collective-permute-start | bytes 1769480 | tf_op jit(solution)/shard_map/ppermute | solution.py:223
  45.6 9.2 %collective-permute-start.10 = (bf16[384,384]{1,0:T(8,128)(2,1)S(1)}, bf16[384,384]{1,0:T(8,128)(2,1)S(1)}, u32[]{:S(2)}, u32[]{:S(2)}) collective-permute-start(bf16[384,384]{1,0:T(8,128)(2,1)S(1)} %broadcast_select_fusion.1), channel_id=1, source_target_pairs={{0,2},{1,5},{2,0},{3,7},{4,6},{5,1},{6,4},{7,3},{8,10},{9,13},{10,... | collective-permute-start | bytes 884744 | tf_op jit(solution)/shard_map/ppermute | solution.py:223
  48.3 9.8 %collective-permute-start.14 = (bf16[2,384,384]{2,1,0:T(8,128)(2,1)S(1)}, bf16[2,384,384]{2,1,0:T(8,128)(2,1)S(1)}, u32[]{:S(2)}, u32[]{:S(2)}) collective-permute-start(bf16[2,384,384]{2,1,0:T(8,128)(2,1)S(1)} %pad_maximum_fusion.2.refs_2_), channel_id=1, source_target_pairs={{0,1},{1,0},{2,3},{3,2},{4,5},{5,4},{6,7},{7,6},{8,9},{9,8},{10,11... | collective-permute-start | bytes 1769480 | tf_op jit(solution)/shard_map/ppermute | solution.py:223
  54.8 4.7 %collective-permute-start.16 = (bf16[2,384,384]{2,1,0:T(8,128)(2,1)S(1)}, bf16[2,384,384]{2,1,0:T(8,128)(2,1)S(1)}, u32[]{:S(2)}, u32[]{:S(2)}) collective-permute-start(bf16[2,384,384]{2,1,0:T(8,128)(2,1)S(1)} %collective-permute-done.15.refs_2_), channel_id=1, source_target_pairs={{0,1},{1,0},{2,3},{3,2},{4,5},{5,4},{6,7},{7,6},{8,9},{9,8},{10,11... | collective-permute-start | bytes 1769480 | tf_op jit(solution)/shard_map/ppermute | solution.py:223
  56.4 4.6 %collective-permute-start.17 = (bf16[2,384,384]{2,1,0:T(8,128)(2,1)S(1)}, bf16[2,384,384]{2,1,0:T(8,128)(2,1)S(1)}, u32[]{:S(2)}, u32[]{:S(2)}) collective-permute-start(bf16[2,384,384]{2,1,0:T(8,128)(2,1)S(1)} %pad_maximum_fusion.4.refs_2_), channel_id=1, source_target_pairs={{0,1},{1,0},{2,3},{3,2},{4,5},{5,4},{6,7},{7,6},{8,9},{9,8},{10,11... | collective-permute-start | bytes 1769480 | tf_op jit(solution)/shard_map/ppermute | solution.py:223
  57.0 9.9 %collective-permute-start.13 = (bf16[2,384,384]{2,1,0:T(8,128)(2,1)S(1)}, bf16[2,384,384]{2,1,0:T(8,128)(2,1)S(1)}, u32[]{:S(2)}, u32[]{:S(2)}) collective-permute-start(bf16[2,384,384]{2,1,0:T(8,128)(2,1)S(1)} %pad_maximum_fusion.4.refs_2_), channel_id=1, source_target_pairs={{0,4},{1,3},{2,6},{3,1},{4,0},{5,7},{6,2},{7,5},{8,12},{9,11},{10,... | collective-permute-start | bytes 1769480 | tf_op jit(solution)/shard_map/ppermute | solution.py:223
  66.9 2.0 %collective-permute-start.18 = (bf16[2,384,384]{2,1,0:T(8,128)(2,1)S(1)}, bf16[2,384,384]{2,1,0:T(8,128)(2,1)S(1)}, u32[]{:S(2)}, u32[]{:S(2)}) collective-permute-start(bf16[2,384,384]{2,1,0:T(8,128)(2,1)S(1)} %collective-permute-done.13.refs_2_), channel_id=1, source_target_pairs={{0,1},{1,0},{2,3},{3,2},{4,5},{5,4},{6,7},{7,6},{8,9},{9,8},{10,11... | collective-permute-start | bytes 1769480 | tf_op jit(solution)/shard_map/ppermute | solution.py:223

commit v3 on v2

--- a/solution.py
+++ b/solution.py
@@ -43,9 +43,10 @@
 
 def slot_columns(slot, width):
     z = lax.axis_index("dp")
-    upper = z // 2
-    shard = (z, flip(z, 1), 2 - upper, 3 - 3 * upper)[slot]
-    return pl.ds(pl.multiple_of(shard * width, 128), width)
+    for bit in (1, 2):
+        if slot & bit:
+            z = flip(z, bit)
+    return pl.ds(pl.multiple_of(z * width, 128), width)
 
 
 def held(name):
@@ -62,30 +63,64 @@
         "far": (moved(s, second), flip(flip(s, 2), 4)),
         "mate_near": (mate, moved(mate, second)),
         "mate_far": (moved(mate, first), flip(flip(mate, 2), 4)),
+        "first": (s % 2,),
+        "last": (2 + s % 2, 4 + s % 2, 6 + s % 2),
+        "mate_first": (mate % 2,),
+        "mate_last": (2 + mate % 2, 4 + mate % 2, 6 + mate % 2),
     }[name]
 
 
-def slice_kernel(tap, out, piece, stage, sem):
+def prepare_kernel(signal, cot, tap, out, piece, first, to_next, to_previous, stage, sem, sems):
     s = lax.axis_index("seq") % PLANE
     matrix, half = s // 2, s % 2
     size = piece.shape[0]
+    rows = signal.shape[1]
+    step = DILATION_STEP
     part = pl.ds(pl.multiple_of(half * size, 128), size)
+    copies = [
+        (tap.at[0:1, :, part], first),
+        (signal.at[:, rows - 2 * step :], to_next.at[:, 0 : 2 * step]),
+        (cot.at[:, rows - step :], to_next.at[:, 2 * step :]),
+        (cot.at[:, 0:step], to_previous.at[:, 0:step]),
+        (signal.at[:, 0 : 2 * step], to_previous.at[:, step:]),
+    ]
+    copies = [pltpu.make_async_copy(a, b, sems.at[n]) for n, (a, b) in enumerate(copies)]
 
     @pl.when(matrix < 3)
     def _():
         copy = pltpu.make_async_copy(tap.at[matrix, :, part], piece, sem)
         copy.start()
+        for other in copies:
+            other.start()
         copy.wait()
 
     @pl.when(matrix == 3)
     def _():
         copy = pltpu.make_async_copy(out.at[part, :], stage, sem)
         copy.start()
+        for other in copies:
+            other.start()
         copy.wait()
         piece[...] = stage[...].T
 
-
-def left_kernel(signal, cot, low, high, left, slope):
+    for other in copies:
+        other.wait()
+
+
+def half_kernel(tap, out, last, stage, sems):
+    half = lax.axis_index("seq") % 2
+    size = last.shape[1]
+    part = pl.ds(pl.multiple_of(half * size, 128), size)
+    copies = [(out.at[part, :], stage), (tap.at[1:3, :, part], last.at[0:2])]
+    copies = [pltpu.make_async_copy(a, b, sems.at[n]) for n, (a, b) in enumerate(copies)]
+    for copy in copies:
+        copy.start()
+    copies[0].wait()
+    last[2] = stage[...].T
+    copies[1].wait()
+
+
+def left_kernel(signal, cot, left, slope):
     reach = 2 * DILATION_STEP
     windows, rows, _ = signal.shape
     for w in range(windows):
@@ -94,12 +129,34 @@
         t = jnp.tanh(ROOT * wide * (1.0 + CUBIC * square))
         left[0, w, reach : reach + rows] = (0.5 * wide * (1.0 + t)).astype(BF16)
         slope[w] = 0.5 * (1.0 + t) + (0.5 * ROOT) * wide * (1.0 - t * t) * (1.0 + 3.0 * CUBIC * square)
+        left[1, w, DILATION_STEP : DILATION_STEP + rows] = cot[w]
+        left[1, w, reach + rows :] = jnp.zeros_like(left[1, w, reach + rows :])
+
+
+def pair_kernel(first, second, both, sems):
+    copies = [pltpu.make_async_copy(a, both.at[n], sems.at[n]) for n, a in enumerate((first, second))]
+    for copy in copies:
+        copy.start()
+    for copy in copies:
+        copy.wait()
+
+
+def edge_kernel(low, high, left_in, left, sems):
+    reach = 2 * DILATION_STEP
+    windows = low.shape[0]
+    rows = left.shape[2] - 2 * reach
+    copies = [
+        (low.at[:, reach:], left.at[1, :, 0:DILATION_STEP]),
+        (high.at[:, 0:DILATION_STEP], left.at[1, :, DILATION_STEP + rows : reach + rows]),
+    ]
+    copies = [pltpu.make_async_copy(a, b, sems.at[n]) for n, (a, b) in enumerate(copies)]
+    for copy in copies:
+        copy.start()
+    for w in range(windows):
         left[0, w, 0:reach] = gelu(low[w, 0:reach].astype(F32)).astype(BF16)
         left[0, w, reach + rows :] = gelu(high[w, DILATION_STEP:].astype(F32)).astype(BF16)
-        left[1, w, 0:DILATION_STEP] = low[w, reach:]
-        left[1, w, DILATION_STEP : DILATION_STEP + rows] = cot[w]
-        left[1, w, DILATION_STEP + rows : reach + rows] = high[w, 0:DILATION_STEP]
-        left[1, w, reach + rows :] = jnp.zeros_like(left[1, w, reach + rows :])
+    for copy in copies:
+        copy.wait()
 
 
 def rows_of(left, which, offset, rows, columns):
@@ -188,7 +245,7 @@
 
 
 def cost(microseconds):
-    return pl.CostEstimate(flops=int(microseconds * 9e8), bytes_accessed=int(microseconds * 3e6), transcendentals=0)
+    return pl.CostEstimate(flops=1000, bytes_accessed=1000, transcendentals=0)
 
 
 def params(mib):
@@ -207,23 +264,47 @@
     vmem = pl.BlockSpec(memory_space=pltpu.VMEM)
     hbm = pl.BlockSpec(memory_space=pl.ANY)
     count = lax.axis_size("seq")
-    z = lax.axis_index("dp")
-    middle = (z == 1) | (z == 2)
-
-    mine = pl.pallas_call(
-        slice_kernel,
-        out_shape=jax.ShapeDtypeStruct((width, width), BF16),
-        in_specs=[hbm] * 2,
-        out_specs=vmem,
-        scratch_shapes=[pltpu.VMEM((width, width), BF16), pltpu.SemaphoreType.DMA],
-        compiler_params=params(60),
-    )(tap, out)
+
+    def stay(array):
+        return pltpu.with_memory_space_constraint(array, pltpu.HBM)
+
+    reach = 2 * DILATION_STEP
+    edge = jax.ShapeDtypeStruct((windows, reach + DILATION_STEP, channels), BF16)
+    mine, first, low, high = pl.pallas_call(
+        prepare_kernel,
+        out_shape=[
+            jax.ShapeDtypeStruct((width, width), BF16),
+            jax.ShapeDtypeStruct((1, width, width), BF16),
+            edge,
+            edge,
+        ],
+        in_specs=[hbm] * 4,
+        out_specs=[vmem] * 4,
+        scratch_shapes=[
+            pltpu.VMEM((width, width), BF16),
+            pltpu.SemaphoreType.DMA,
+            pltpu.SemaphoreType.DMA((5,)),
+        ],
+        compiler_params=params(8),
+    )(stay(signal), stay(cot), stay(tap), stay(out))
 
     def across(block, even, odd):
         return lax.ppermute(block, "seq", plane_pairs(count, even, odd))
 
-    outward = [(1, 0), (2, 3)]
-    inward = [(1, 2), (2, 1)]
+    def over(block, bits):
+        return lax.ppermute(block, "dp", [(i, i ^ bits) for i in range(4)])
+
+    def pair(first, second):
+        return pl.pallas_call(
+            pair_kernel,
+            out_shape=jax.ShapeDtypeStruct((2, width, width), BF16),
+            in_specs=[hbm] * 2,
+            out_specs=vmem,
+            scratch_shapes=[pltpu.SemaphoreType.DMA((2,))],
+            compiler_params=params(2),
+            cost_estimate=cost(0.3),
+        )(first, second)
+
     sums_shape = jax.ShapeDtypeStruct((2, windows * wide_rows, hidden), F32)
     whole_shape = jax.ShapeDtypeStruct((4, width, hidden), BF16)
 
@@ -238,80 +319,88 @@
             out_shape=[sums_shape, whole_shape],
             in_specs=[vmem] * len(given),
             out_specs=[vmem] * 2,
-            scratch_shapes=[pltpu.SemaphoreType.DMA((2 * len(names),))],
+            scratch_shapes=[pltpu.SemaphoreType.DMA((sum(b.shape[0] for b in buffers),))],
             input_output_aliases=aliases,
-            compiler_params=params(16),
-            cost_estimate=cost(0.5 * len(names)),
+            compiler_params=params(4),
+            cost_estimate=cost(0.7 * len(names)),
         )(*given)
 
-    p1 = lax.ppermute(mine, "dp", [(0, 1), (1, 0), (2, 3), (3, 2)])
-    reach = 2 * DILATION_STEP
-    low, high = (
-        jnp.concatenate([signal[:, -reach:], cot[:, -DILATION_STEP:]], axis=1),
-        jnp.concatenate([cot[:, :DILATION_STEP], signal[:, :reach]], axis=1),
-    )
-    low, high, mine = tie(low, high, mine)
-    p2 = lax.ppermute(mine, "dp", inward)
+    p2 = over(mine, 2)
+    first = over(first, 1)
     low = lax.ppermute(low, "seq", [(i, i + 1) for i in range(count - 1)])
     high = lax.ppermute(high, "seq", [(i + 1, i) for i in range(count - 1)])
-
-    near1 = across(p1, 2, 4)
-    p4 = lax.ppermute(p1, "dp", inward)
-    p3 = lax.ppermute(p2, "dp", outward)
+    left_shape = jax.ShapeDtypeStruct((2, windows, rows + 2 * reach, channels), BF16)
     left, slope = pl.pallas_call(
         left_kernel,
-        out_shape=[
-            jax.ShapeDtypeStruct((2, windows, rows + 2 * reach, channels), BF16),
-            jax.ShapeDtypeStruct(signal.shape, F32),
-        ],
-        in_specs=[vmem] * 4,
+        out_shape=[left_shape, jax.ShapeDtypeStruct(signal.shape, F32)],
+        in_specs=[vmem] * 2,
         out_specs=[vmem] * 2,
-        compiler_params=params(16),
-        cost_estimate=cost(2.5),
-    )(signal, cot, low, high)
+        compiler_params=params(4),
+        cost_estimate=cost(1.3),
+    )(signal, cot)
+    last = pl.pallas_call(
+        half_kernel,
+        out_shape=jax.ShapeDtypeStruct((3, width, width), BF16),
+        in_specs=[hbm] * 2,
+        out_specs=vmem,
+        scratch_shapes=[pltpu.VMEM((width, width), BF16), pltpu.SemaphoreType.DMA((2,))],
+        compiler_params=params(4),
+        cost_estimate=cost(1.5),
+    )(stay(tap), stay(out))
+    p2, first, left, last = tie(p2, first, left, last)
+    near2 = across(p2, 2, 4)
+    p3 = over(p2, 1)
+    left = pl.pallas_call(
+        edge_kernel,
+        out_shape=left_shape,
+        in_specs=[vmem] * 3,
+        out_specs=vmem,
+        scratch_shapes=[pltpu.SemaphoreType.DMA((2,))],
+        input_output_aliases={2: 0},
+        compiler_params=params(4),
+        cost_estimate=cost(0.5),
+    )(low, high, left)
     sums = pl.pallas_call(
         own_kernel,
         out_shape=sums_shape,
         in_specs=[vmem] * 3,
         out_specs=vmem,
-        compiler_params=params(16),
-        cost_estimate=cost(1.5),
+        compiler_params=params(4),
+        cost_estimate=cost(1.4),
     )(left, tap, out)
-    own1 = jnp.stack([p1, near1])
-    far1 = across(own1, 4, 2)
-    mate1 = across(own1, 1, 1)
-    got2 = jnp.where(middle, p2, p3)
-    near2 = across(got2, 2, 4)
-    p5 = lax.ppermute(p4, "dp", outward)
     near_names, far_names = ("near", "mate_near"), ("far", "mate_far")
-    own2 = jnp.stack([got2, near2])
-    own2, sums = tie(own2, sums)
+    mate_first = across(first, 1, 1)
+    own2 = pair(p2, near2)
+    own2, left = tie(own2, left)
     far2 = across(own2, 4, 2)
     mate2 = across(own2, 1, 1)
-    far_mate1 = across(far1, 1, 1)
-    sums, whole1 = add_slot(1, near_names, (own1, mate1), left, sums)
-    got3 = jnp.where(middle, p4, p5)
-    got3, sums = tie(got3, sums)
-    near3 = across(got3, 2, 4)
-    own3 = jnp.stack([got3, near3])
-    sums, whole1 = add_slot(1, far_names, (far1, far_mate1), left, sums, whole1)
+    p3, last = tie(p3, last)
+    near3 = across(p3, 2, 4)
+    last = over(last, 1)
+    far_mate2 = across(far2, 1, 1)
+    own3 = pair(p3, near3)
     own3, sums = tie(own3, sums)
     far3 = across(own3, 4, 2)
     mate3 = across(own3, 1, 1)
-    far_mate2 = across(far2, 1, 1)
     sums, whole2 = add_slot(2, near_names, (own2, mate2), left, sums)
+    sums, whole1 = add_slot(1, ("first", "mate_first"), (first, mate_first), left, sums)
+    sums, whole3 = add_slot(3, near_names, (own3, mate3), left, sums)
+    last, sums = tie(last, sums)
+    mate_last = across(last, 1, 1)
     sums, whole2 = add_slot(2, far_names, (far2, far_mate2), left, sums, whole2)
-    sums, whole3 = add_slot(3, near_names, (own3, mate3), left, sums)
     far3, sums = tie(far3, sums)
     far_mate3 = across(far3, 1, 1)
-    sums, whole3 = add_slot(3, far_names, (far3, far_mate3), left, sums, whole3)
+    sums, whole3 = add_slot(3, ("far",), (far3,), left, sums, whole3)
+    sums, whole3 = add_slot(3, ("mate_far",), (far_mate3,), left, sums, whole3)
+    sums, whole1 = add_slot(1, ("last",), (last,), left, sums, whole1)
+    sums, whole1 = add_slot(1, ("mate_last",), (mate_last,), left, sums, whole1)
 
     right = pl.pallas_call(
         middle_kernel,
         out_shape=jax.ShapeDtypeStruct((2, windows, wide_rows, hidden), BF16),
         in_specs=[vmem],
         out_specs=vmem,
-        compiler_params=params(16),
+        compiler_params=params(4),
         cost_estimate=cost(0.8),
     )(sums)
     result, grad_signal = pl.pallas_call(
@@ -319,7 +408,7 @@
         out_shape=[jax.ShapeDtypeStruct(signal.shape, BF16)] * 2,
         in_specs=[vmem] * 9,
         out_specs=[vmem] * 2,
-        compiler_params=params(24),
+        compiler_params=params(8),
         cost_estimate=cost(4.5),
     )(signal, cot, slope, right, tap, out, whole1, whole2, whole3)
     return result, grad_signal

time: 75.9 us -> 66.4 us (0.87)
  starting transfers between devices: 25.9 us -> 15.3 us
  other arithmetic: 3.19 us -> 0 us
  waiting for transfers between devices: 26.4 us -> 29.5 us
  Pallas kernels: 18.9 us -> 20.5 us
    ppermute x12 -> x10, starting transfers between devices: 15.6 us -> 5.13 us  [across(): return lax.ppermute(block, 'seq', plane_pairs(count, even, odd))]
    ppermute x5 -> x4, waiting for transfers between devices: 8.63 us -> 13.1 us  [over(): return lax.ppermute(block, 'dp', [(i, i ^ bits) for i in range(4)])]
    pallas_call x2 -> x6, Pallas kernels: 3.43 us -> 4.86 us  [the longest x1 1.49 us: per_device(): pl.pallas_call(prepare_kernel, out_shape=[jax.ShapeDtypeStruct((width, wi...]
    ppermute x12 -> x10, waiting for transfers between devices: 17.8 us -> 16.4 us  [across(): return lax.ppermute(block, 'seq', plane_pairs(count, even, odd))]
    another operation x3 -> x0, other arithmetic: 1.25 us -> none  [the longest x1 1.12 us: per_device(): own1 = jnp.stack([p1, near1])]
    select_n x2 -> x0, other arithmetic: 1.04 us -> none  [the longest x1 1 us: per_device(): got2 = jnp.where(middle, p2, p3)]
    concatenate x1 -> x0, other arithmetic: 0.9 us -> none  [per_device(): jnp.concatenate([signal[:, -reach:], cot[:, -DILATION_STEP:]], axis=1)]
    ppermute x5 -> x4, starting transfers between devices: 7.71 us -> 7.57 us  [over(): return lax.ppermute(block, 'dp', [(i, i ^ bits) for i in range(4)])]
  transfers between devices with their start and end apart: 19 -> 16, of which waited for: 8 -> 8; matrix products, arithmetic and copies ran while one was open for 4% -> 0% of each run, Pallas kernels for 14% -> 19%
where the time goes in v3:
time: 66.4 us; the launch traced here: 66.2 us
  waiting for transfers between devices  29.5 us (44%)
  Pallas kernels  20.5 us (31%)
  starting transfers between devices  15.3 us (23%)
  between operations  0.89 us (1%)
    ppermute x10, waiting for transfers between devices, across(): return lax.ppermute(block, 'seq', plane_pairs(count, even, odd))  16.4 us
    ppermute x4, waiting for transfers between devices, over(): return lax.ppermute(block, 'dp', [(i, i ^ bits) for i in range(4)])  13.1 us
    pallas_call x8, Pallas kernels, add_slot(): pl.pallas_call(functools.partial(slot_kernel, slot, names, fresh), out_sh...  9.02 us
    ppermute x4, starting transfers between devices, over(): return lax.ppermute(block, 'dp', [(i, i ^ bits) for i in range(4)])  7.57 us
    ppermute x10, starting transfers between devices, across(): return lax.ppermute(block, 'seq', plane_pairs(count, even, odd))  5.13 us
    pallas_call x1, Pallas kernels, per_device(): pl.pallas_call(back_kernel, out_shape=[jax.ShapeDtypeStruct(signal.shape,...  4.43 us
    pallas_call x1, Pallas kernels, per_device(): pl.pallas_call(prepare_kernel, out_shape=[jax.ShapeDtypeStruct((width, wi...  1.49 us
    pallas_call x1, Pallas kernels, per_device(): pl.pallas_call(own_kernel, out_shape=sums_shape, in_specs=[vmem] * 3, out...  1.38 us
  transfers between devices with their start and end apart: 16, of which 8 were waited for; matrix products, arithmetic and copies ran while one was open for 0% of the time, Pallas kernels for 19%

profile of v3, /device:TPU:0, one launch (start us, length us, event | category | flops | bytes accessed | tf_op | source)
XLA Modules:
  0.0 66.2 jit_solution(8688605828993915306)
XLA Ops:
  0.6 1.5 %shard_map.60 = (bf16[384,384]{1,0:T(8,128)(2,1)S(1)}, bf16[1,384,384]{2,1,0:T(8,128)(2,1)S(1)}, bf16[2,96,1536]{2,1,0:T(8,128)(2,1)S(1)}, bf16[2,96,1536]{2,1,0:T(8,128)(2,1)S(1)}) custom-call(bf16[2,128,1536]{2,1,0:T(8,128)(2,1)} %signal.5, bf16[2,128,1536]{2,1,0:T(8,128)(2,1)} %cot.5, bf16[3,384,768]{2,1,0:T(8,128)(2,1)} %tap.7, bf16[768,384]{1,0:T(8,128)(2,1)} %out.7), custom_call_target="tpu_custom_call" | custom-call | tf_op jit(solution)/shard_map/pallas_call | solution.py:273
  2.1 4.1 %collective-permute-start = (bf16[384,384]{1,0:T(8,128)(2,1)S(1)}, bf16[384,384]{1,0:T(8,128)(2,1)S(1)}, u32[]{:S(2)}, u32[]{:S(2)}) collective-permute-start(bf16[384,384]{1,0:T(8,128)(2,1)S(1)} %get-tuple-element.39), channel_id=1, source_target_pairs={{0,16},{8,24},{16,0},{24,8},{1,17},{9,25},{17,1},{25,9},{2,18},{10... | collective-permute-start | bytes 884744 | tf_op jit(solution)/shard_map/ppermute | solution.py:295
  6.2 1.6 %collective-permute-start.1 = (bf16[1,384,384]{2,1,0:T(8,128)(2,1)S(1)}, bf16[1,384,384]{2,1,0:T(8,128)(2,1)S(1)}, u32[]{:S(2)}, u32[]{:S(2)}) collective-permute-start(bf16[1,384,384]{2,1,0:T(8,128)(2,1)S(1)} %get-tuple-element.40), channel_id=1, source_target_pairs={{0,8},{8,0},{16,24},{24,16},{1,9},{9,1},{17,25},{25,17},{2,10},{10... | collective-permute-start | bytes 884744 | tf_op jit(solution)/shard_map/ppermute | solution.py:295
  7.8 1.3 %collective-permute-start.3 = (bf16[2,96,1536]{2,1,0:T(8,128)(2,1)S(1)}, bf16[2,96,1536]{2,1,0:T(8,128)(2,1)S(1)}, u32[]{:S(2)}, u32[]{:S(2)}) collective-permute-start(bf16[2,96,1536]{2,1,0:T(8,128)(2,1)S(1)} %get-tuple-element.43), channel_id=1, source_target_pairs={{0,1},{1,2},{2,3},{3,4},{4,5},{5,6},{6,7},{8,9},{9,10},{10,11},{11... | collective-permute-start | bytes 1769480 | tf_op jit(solution)/shard_map/ppermute | solution.py:330
  9.1 1.3 %collective-permute-start.4 = (bf16[2,96,1536]{2,1,0:T(8,128)(2,1)S(1)}, bf16[2,96,1536]{2,1,0:T(8,128)(2,1)S(1)}, u32[]{:S(2)}, u32[]{:S(2)}) collective-permute-start(bf16[2,96,1536]{2,1,0:T(8,128)(2,1)S(1)} %get-tuple-element.44), channel_id=1, source_target_pairs={{1,0},{2,1},{3,2},{4,3},{5,4},{6,5},{7,6},{9,8},{10,9},{11,10},{12... | collective-permute-start | bytes 1769480 | tf_op jit(solution)/shard_map/ppermute | solution.py:331
  10.4 1.2 %shard_map.61 = bf16[3,384,384]{2,1,0:T(8,128)(2,1)S(1)} custom-call(bf16[3,384,768]{2,1,0:T(8,128)(2,1)} %tap.7, bf16[768,384]{1,0:T(8,128)(2,1)} %out.7), custom_call_target="tpu_custom_call" | custom-call | flops 1000 | bytes 1000 | tf_op jit(solution)/shard_map/pallas_call | solution.py:341
  11.7 1.1 %shard_map.59 = (bf16[2,2,256,1536]{3,2,1,0:T(8,128)(2,1)S(1)}, f32[2,128,1536]{2,1,0:T(8,128)S(1)}) custom-call(bf16[2,128,1536]{2,1,0:T(8,128)(2,1)S(1)} %copy-done.2, bf16[2,128,1536]{2,1,0:T(8,128)(2,1)S(1)} %copy-done.3), custom_call_target="tpu_custom_call" | custom-call | flops 1000 | bytes 1000 | tf_op jit(solution)/shard_map/pallas_call | solution.py:333
  12.8 6.9 %collective-permute-done.first = bf16[384,384]{1,0:T(8,128)(2,1)S(1)} collective-permute-done((bf16[384,384]{1,0:T(8,128)(2,1)S(1)}, bf16[384,384]{1,0:T(8,128)(2,1)S(1)}, u32[]{:S(2)}, u32[]{:S(2)}) %collective-permute-start) | collective-permute-done | bytes 294944 | tf_op jit(solution)/shard_map/ppermute | solution.py:295
  19.9 1.5 %collective-permute-start.2 = (bf16[384,384]{1,0:T(8,128)(2,1)S(1)}, bf16[384,384]{1,0:T(8,128)(2,1)S(1)}, u32[]{:S(2)}, u32[]{:S(2)}) collective-permute-start(bf16[384,384]{1,0:T(8,128)(2,1)S(1)} %collective-permute-done.first), channel_id=1, source_target_pairs={{0,2},{1,5},{2,0},{3,7},{4,6},{5,1},{6,4},{7,3},{8,10},{9,13},{10,... | collective-permute-start | bytes 884744 | tf_op jit(solution)/shard_map/ppermute | solution.py:292
  21.4 1.4 %collective-permute-start.5 = (bf16[384,384]{1,0:T(8,128)(2,1)S(1)}, bf16[384,384]{1,0:T(8,128)(2,1)S(1)}, u32[]{:S(2)}, u32[]{:S(2)}) collective-permute-start(bf16[384,384]{1,0:T(8,128)(2,1)S(1)} %collective-permute-done.first), channel_id=1, source_target_pairs={{0,8},{8,0},{16,24},{24,16},{1,9},{9,1},{17,25},{25,17},{2,10},{10... | collective-permute-start | bytes 884744 | tf_op jit(solution)/shard_map/ppermute | solution.py:295
  22.9 6.6 %collective-permute-done.2.second = bf16[384,384]{1,0:T(8,128)(2,1)S(1)} collective-permute-done((bf16[384,384]{1,0:T(8,128)(2,1)S(1)}, bf16[384,384]{1,0:T(8,128)(2,1)S(1)}, u32[]{:S(2)}, u32[]{:S(2)}) %collective-permute-start.2) | collective-permute-done | bytes 294944 | tf_op jit(solution)/shard_map/ppermute | solution.py:292
  31.2 1.6 %collective-permute-start.6 = (bf16[384,384]{1,0:T(8,128)(2,1)S(1)}, bf16[384,384]{1,0:T(8,128)(2,1)S(1)}, u32[]{:S(2)}, u32[]{:S(2)}) collective-permute-start(bf16[384,384]{1,0:T(8,128)(2,1)S(1)} %collective-permute-done.5.first), channel_id=1, source_target_pairs={{0,2},{1,5},{2,0},{3,7},{4,6},{5,1},{6,4},{7,3},{8,10},{9,13},{10,... | collective-permute-start | bytes 884744 | tf_op jit(solution)/shard_map/ppermute | solution.py:292
  33.2 1.4 %shard_map.65.refs_1_ = f32[2,384,768]{2,1,0:T(8,128)S(1)} custom-call(bf16[2,2,256,1536]{3,2,1,0:T(8,128)(2,1)S(1)} %shard_map.63.left.refs_0_, bf16[3,384,768]{2,1,0:T(8,128)(2,1)S(1)} %copy-done, bf16[768,384]{1,0:T(8,128)(2,1)S(1)} %copy-done.1), custom_call_target="tpu_custom_call" | custom-call | flops 1000 | bytes 1000 | tf_op jit(solution)/shard_map/pallas_call | solution.py:363
  34.6 6.5 %collective-permute-done.6.second = bf16[384,384]{1,0:T(8,128)(2,1)S(1)} collective-permute-done((bf16[384,384]{1,0:T(8,128)(2,1)S(1)}, bf16[384,384]{1,0:T(8,128)(2,1)S(1)}, u32[]{:S(2)}, u32[]{:S(2)}) %collective-permute-start.6) | collective-permute-done | bytes 294944 | tf_op jit(solution)/shard_map/ppermute | solution.py:292
  41.4 2.0 %collective-permute-done.12.refs_2_ = bf16[2,384,384]{2,1,0:T(8,128)(2,1)S(1)} collective-permute-done((bf16[2,384,384]{2,1,0:T(8,128)(2,1)S(1)}, bf16[2,384,384]{2,1,0:T(8,128)(2,1)S(1)}, u32[]{:S(2)}, u32[]{:S(2)}) %collective-permute-start.12) | collective-permute-done | bytes 589856 | tf_op jit(solution)/shard_map/ppermute | solution.py:292
  44.0 1.4 %shard_map.66 = (f32[2,384,768]{2,1,0:T(8,128)S(1)}, bf16[4,384,768]{2,1,0:T(8,128)(2,1)S(1)}) custom-call(bf16[2,2,256,1536]{3,2,1,0:T(8,128)(2,1)S(1)} %shard_map.63.left.refs_0_, f32[2,384,768]{2,1,0:T(8,128)S(1)} %shard_map.65.refs_1_, bf16[2,384,384]{2,1,0:T(8,128)(2,1)S(1)} %shard_map.62.refs_2_, ...), custom_call_target="tpu_custom_call", output_to_operand_aliasing={{0}: (1, {})} | custom-call | flops 1000 | bytes 1000 | tf_op jit(solution)/shard_map/pallas_call | solution.py:317
  45.8 1.1 %shard_map.67 = (f32[2,384,768]{2,1,0:T(8,128)S(1)}, bf16[4,384,768]{2,1,0:T(8,128)(2,1)S(1)}) custom-call(bf16[2,2,256,1536]{3,2,1,0:T(8,128)(2,1)S(1)} %shard_map.63.left.refs_0_, f32[2,384,768]{2,1,0:T(8,128)S(1)} %get-tuple-element.53.refs_1_, bf16[1,384,384]{2,1,0:T(8,128)(2,1)S(1)} %collective-permute-done.1.refs_2_, ...), custom_call_target="tpu_custom_call", output_to_operand_aliasing={{0}: (1, {})} | custom-call | flops 1000 | bytes 1000 | tf_op jit(solution)/shard_map/pallas_call | solution.py:317
  46.9 1.5 %shard_map.68 = (f32[2,384,768]{2,1,0:T(8,128)S(1)}, bf16[4,384,768]{2,1,0:T(8,128)(2,1)S(1)}) custom-call(bf16[2,2,256,1536]{3,2,1,0:T(8,128)(2,1)S(1)} %shard_map.63.left.refs_0_, f32[2,384,768]{2,1,0:T(8,128)S(1)} %get-tuple-element.55.refs_1_, bf16[2,384,384]{2,1,0:T(8,128)(2,1)S(1)} %shard_map.64.refs_2_, ...), custom_call_target="tpu_custom_call", output_to_operand_aliasing={{0}: (1, {})} | custom-call | flops 1000 | bytes 1000 | tf_op jit(solution)/shard_map/pallas_call | solution.py:317
  48.4 6.0 %collective-permute-done.8.refs_2_ = bf16[3,384,384]{2,1,0:T(8,128)(2,1)S(1)} collective-permute-done((bf16[3,384,384]{2,1,0:T(8,128)(2,1)S(1)}, bf16[3,384,384]{2,1,0:T(8,128)(2,1)S(1)}, u32[]{:S(2)}, u32[]{:S(2)}) %collective-permute-start.8) | collective-permute-done | bytes 884768 | tf_op jit(solution)/shard_map/ppermute | solution.py:295
  54.4 1.4 %shard_map.69 = (f32[2,384,768]{2,1,0:T(8,128)S(1)}, bf16[4,384,768]{2,1,0:T(8,128)(2,1)S(1)}) custom-call(bf16[2,2,256,1536]{3,2,1,0:T(8,128)(2,1)S(1)} %shard_map.63.left.refs_0_, f32[2,384,768]{2,1,0:T(8,128)S(1)} %get-tuple-element.57.refs_1_, ...), custom_call_target="tpu_custom_call", output_to_operand_aliasing={{0}: (1, {}), {1}: (4, {})} | custom-call | flops 1000 | bytes 1000 | tf_op jit(solution)/shard_map/pallas_call | solution.py:317
  57.1 0.9 %collective-permute-done.14.refs_2_ = bf16[2,384,384]{2,1,0:T(8,128)(2,1)S(1)} collective-permute-done((bf16[2,384,384]{2,1,0:T(8,128)(2,1)S(1)}, bf16[2,384,384]{2,1,0:T(8,128)(2,1)S(1)}, u32[]{:S(2)}, u32[]{:S(2)}) %collective-permute-start.14) | collective-permute-done | bytes 589856 | tf_op jit(solution)/shard_map/ppermute | solution.py:292
  58.8 1.0 %shard_map.72 = (f32[2,384,768]{2,1,0:T(8,128)S(1)}, bf16[4,384,768]{2,1,0:T(8,128)(2,1)S(1)}) custom-call(bf16[2,2,256,1536]{3,2,1,0:T(8,128)(2,1)S(1)} %shard_map.63.left.refs_0_, f32[2,384,768]{2,1,0:T(8,128)S(1)} %get-tuple-element.65.refs_1_, ...), custom_call_target="tpu_custom_call", output_to_operand_aliasing={{0}: (1, {}), {1}: (3, {})} | custom-call | flops 1000 | bytes 1000 | tf_op jit(solution)/shard_map/pallas_call | solution.py:317
  59.8 1.2 %shard_map.73 = (f32[2,384,768]{2,1,0:T(8,128)S(1)}, bf16[4,384,768]{2,1,0:T(8,128)(2,1)S(1)}) custom-call(bf16[2,2,256,1536]{3,2,1,0:T(8,128)(2,1)S(1)} %shard_map.63.left.refs_0_, f32[2,384,768]{2,1,0:T(8,128)S(1)} %get-tuple-element.68.refs_1_, ...), custom_call_target="tpu_custom_call", output_to_operand_aliasing={{0}: (1, {}), {1}: (3, {})} | custom-call | flops 1000 | bytes 1000 | tf_op jit(solution)/shard_map/pallas_call | solution.py:317
  61.7 4.4 %shard_map.75 = (bf16[2,128,1536]{2,1,0:T(8,128)(2,1)}, bf16[2,128,1536]{2,1,0:T(8,128)(2,1)}) custom-call(bf16[2,128,1536]{2,1,0:T(8,128)(2,1)S(1)} %copy-done.2, bf16[2,128,1536]{2,1,0:T(8,128)(2,1)S(1)} %copy-done.3, f32[2,128,1536]{2,1,0:T(8,128)S(1)} %get-tuple-element.38.slope, bf16[2,2,192,768]{3,2,1,0:T(8,128)(2,1)S(1)} %shard_map.74.right, ...), custom_call_target="tpu_custom_call" | custom-call | flops 1000 | bytes 1000 | tf_op jit(solution)/shard_map/pallas_call | solution.py:406
  (33 shorter events, 6.4 us)
Async XLA Ops:
  2.1 9.5 %copy-start.2 = (bf16[2,128,1536]{2,1,0:T(8,128)(2,1)S(1)}, bf16[2,128,1536]{2,1,0:T(8,128)(2,1)}, u32[]{:S(2)}) copy-start(bf16[2,128,1536]{2,1,0:T(8,128)(2,1)} %signal.5) | copy-start | bytes 2359300
  2.1 9.5 %copy-start.3 = (bf16[2,128,1536]{2,1,0:T(8,128)(2,1)S(1)}, bf16[2,128,1536]{2,1,0:T(8,128)(2,1)}, u32[]{:S(2)}) copy-start(bf16[2,128,1536]{2,1,0:T(8,128)(2,1)} %cot.5) | copy-start | bytes 2359300
  2.1 17.5 %collective-permute-start = (bf16[384,384]{1,0:T(8,128)(2,1)S(1)}, bf16[384,384]{1,0:T(8,128)(2,1)S(1)}, u32[]{:S(2)}, u32[]{:S(2)}) collective-permute-start(bf16[384,384]{1,0:T(8,128)(2,1)S(1)} %get-tuple-element.39), channel_id=1, source_target_pairs={{0,16},{8,24},{16,0},{24,8},{1,17},{9,25},{17,1},{25,9},{2,18},{10... | collective-permute-start | bytes 884744 | tf_op jit(solution)/shard_map/ppermute | solution.py:295
  6.2 13.6 %collective-permute-start.1 = (bf16[1,384,384]{2,1,0:T(8,128)(2,1)S(1)}, bf16[1,384,384]{2,1,0:T(8,128)(2,1)S(1)}, u32[]{:S(2)}, u32[]{:S(2)}) collective-permute-start(bf16[1,384,384]{2,1,0:T(8,128)(2,1)S(1)} %get-tuple-element.40), channel_id=1, source_target_pairs={{0,8},{8,0},{16,24},{24,16},{1,9},{9,1},{17,25},{25,17},{2,10},{10... | collective-permute-start | bytes 884744 | tf_op jit(solution)/shard_map/ppermute | solution.py:295
  7.8 21.8 %collective-permute-start.3 = (bf16[2,96,1536]{2,1,0:T(8,128)(2,1)S(1)}, bf16[2,96,1536]{2,1,0:T(8,128)(2,1)S(1)}, u32[]{:S(2)}, u32[]{:S(2)}) collective-permute-start(bf16[2,96,1536]{2,1,0:T(8,128)(2,1)S(1)} %get-tuple-element.43), channel_id=1, source_target_pairs={{0,1},{1,2},{2,3},{3,4},{4,5},{5,6},{6,7},{8,9},{9,10},{10,11},{11... | collective-permute-start | bytes 1769480 | tf_op jit(solution)/shard_map/ppermute | solution.py:330
  9.1 20.5 %collective-permute-start.4 = (bf16[2,96,1536]{2,1,0:T(8,128)(2,1)S(1)}, bf16[2,96,1536]{2,1,0:T(8,128)(2,1)S(1)}, u32[]{:S(2)}, u32[]{:S(2)}) collective-permute-start(bf16[2,96,1536]{2,1,0:T(8,128)(2,1)S(1)} %get-tuple-element.44), channel_id=1, source_target_pairs={{1,0},{2,1},{3,2},{4,3},{5,4},{6,5},{7,6},{9,8},{10,9},{11,10},{12... | collective-permute-start | bytes 1769480 | tf_op jit(solution)/shard_map/ppermute | solution.py:331
  19.9 9.6 %collective-permute-start.2 = (bf16[384,384]{1,0:T(8,128)(2,1)S(1)}, bf16[384,384]{1,0:T(8,128)(2,1)S(1)}, u32[]{:S(2)}, u32[]{:S(2)}) collective-permute-start(bf16[384,384]{1,0:T(8,128)(2,1)S(1)} %collective-permute-done.first), channel_id=1, source_target_pairs={{0,2},{1,5},{2,0},{3,7},{4,6},{5,1},{6,4},{7,3},{8,10},{9,13},{10,... | collective-permute-start | bytes 884744 | tf_op jit(solution)/shard_map/ppermute | solution.py:292
  21.4 9.8 %collective-permute-start.5 = (bf16[384,384]{1,0:T(8,128)(2,1)S(1)}, bf16[384,384]{1,0:T(8,128)(2,1)S(1)}, u32[]{:S(2)}, u32[]{:S(2)}) collective-permute-start(bf16[384,384]{1,0:T(8,128)(2,1)S(1)} %collective-permute-done.first), channel_id=1, source_target_pairs={{0,8},{8,0},{16,24},{24,16},{1,9},{9,1},{17,25},{25,17},{2,10},{10... | collective-permute-start | bytes 884744 | tf_op jit(solution)/shard_map/ppermute | solution.py:295
  29.6 3.6 %copy-start = (bf16[3,384,768]{2,1,0:T(8,128)(2,1)S(1)}, bf16[3,384,768]{2,1,0:T(8,128)(2,1)}, u32[]{:S(2)}) copy-start(bf16[3,384,768]{2,1,0:T(8,128)(2,1)} %tap.7) | copy-start | bytes 5308420
  29.6 3.6 %copy-start.1 = (bf16[768,384]{1,0:T(8,128)(2,1)S(1)}, bf16[768,384]{1,0:T(8,128)(2,1)}, u32[]{:S(2)}) copy-start(bf16[768,384]{1,0:T(8,128)(2,1)} %out.7) | copy-start | bytes 1769476
  30.5 12.9 %collective-permute-start.12 = (bf16[2,384,384]{2,1,0:T(8,128)(2,1)S(1)}, bf16[2,384,384]{2,1,0:T(8,128)(2,1)S(1)}, u32[]{:S(2)}, u32[]{:S(2)}) collective-permute-start(bf16[2,384,384]{2,1,0:T(8,128)(2,1)S(1)} %shard_map.62.refs_2_), channel_id=1, source_target_pairs={{0,4},{1,3},{2,6},{3,1},{4,0},{5,7},{6,2},{7,5},{8,12},{9,11},{10,... | collective-permute-start | bytes 1769480 | tf_op jit(solution)/shard_map/ppermute | solution.py:292
  30.5 13.0 %collective-permute-start.9 = (bf16[2,384,384]{2,1,0:T(8,128)(2,1)S(1)}, bf16[2,384,384]{2,1,0:T(8,128)(2,1)S(1)}, u32[]{:S(2)}, u32[]{:S(2)}) collective-permute-start(bf16[2,384,384]{2,1,0:T(8,128)(2,1)S(1)} %shard_map.62.refs_2_), channel_id=1, source_target_pairs={{0,1},{1,0},{2,3},{3,2},{4,5},{5,4},{6,7},{7,6},{8,9},{9,8},{10,11... | collective-permute-start | bytes 1769480 | tf_op jit(solution)/shard_map/ppermute | solution.py:292
  31.2 9.9 %collective-permute-start.6 = (bf16[384,384]{1,0:T(8,128)(2,1)S(1)}, bf16[384,384]{1,0:T(8,128)(2,1)S(1)}, u32[]{:S(2)}, u32[]{:S(2)}) collective-permute-start(bf16[384,384]{1,0:T(8,128)(2,1)S(1)} %collective-permute-done.5.first), channel_id=1, source_target_pairs={{0,2},{1,5},{2,0},{3,7},{4,6},{5,1},{6,4},{7,3},{8,10},{9,13},{10,... | collective-permute-start | bytes 884744 | tf_op jit(solution)/shard_map/ppermute | solution.py:292
  32.8 21.6 %collective-permute-start.8 = (bf16[3,384,384]{2,1,0:T(8,128)(2,1)S(1)}, bf16[3,384,384]{2,1,0:T(8,128)(2,1)S(1)}, u32[]{:S(2)}, u32[]{:S(2)}) collective-permute-start(bf16[3,384,384]{2,1,0:T(8,128)(2,1)S(1)} %shard_map.61), channel_id=1, source_target_pairs={{0,8},{8,0},{16,24},{24,16},{1,9},{9,1},{17,25},{25,17},{2,10},{10... | collective-permute-start | bytes 2654216 | tf_op jit(solution)/shard_map/ppermute | solution.py:295
  41.3 5.6 %collective-permute-start.11 = (bf16[2,384,384]{2,1,0:T(8,128)(2,1)S(1)}, bf16[2,384,384]{2,1,0:T(8,128)(2,1)S(1)}, u32[]{:S(2)}, u32[]{:S(2)}) collective-permute-start(bf16[2,384,384]{2,1,0:T(8,128)(2,1)S(1)} %shard_map.64.refs_2_), channel_id=1, source_target_pairs={{0,1},{1,0},{2,3},{3,2},{4,5},{5,4},{6,7},{7,6},{8,9},{9,8},{10,11... | collective-permute-start | bytes 1769480 | tf_op jit(solution)/shard_map/ppermute | solution.py:292
  43.4 10.9 %collective-permute-start.13 = (bf16[2,384,384]{2,1,0:T(8,128)(2,1)S(1)}, bf16[2,384,384]{2,1,0:T(8,128)(2,1)S(1)}, u32[]{:S(2)}, u32[]{:S(2)}) collective-permute-start(bf16[2,384,384]{2,1,0:T(8,128)(2,1)S(1)} %collective-permute-done.12.refs_2_), channel_id=1, source_target_pairs={{0,1},{1,0},{2,3},{3,2},{4,5},{5,4},{6,7},{7,6},{8,9},{9,8},{10,11... | collective-permute-start | bytes 1769480 | tf_op jit(solution)/shard_map/ppermute | solution.py:292
  43.4 12.4 %collective-permute-start.7 = (bf16[2,384,384]{2,1,0:T(8,128)(2,1)S(1)}, bf16[2,384,384]{2,1,0:T(8,128)(2,1)S(1)}, u32[]{:S(2)}, u32[]{:S(2)}) collective-permute-start(bf16[2,384,384]{2,1,0:T(8,128)(2,1)S(1)} %shard_map.64.refs_2_), channel_id=1, source_target_pairs={{0,4},{1,3},{2,6},{3,1},{4,0},{5,7},{6,2},{7,5},{8,12},{9,11},{10,... | collective-permute-start | bytes 1769480 | tf_op jit(solution)/shard_map/ppermute | solution.py:292
  43.6 2.2 %collective-permute-start.10 = (bf16[1,384,384]{2,1,0:T(8,128)(2,1)S(1)}, bf16[1,384,384]{2,1,0:T(8,128)(2,1)S(1)}, u32[]{:S(2)}, u32[]{:S(2)}) collective-permute-start(bf16[1,384,384]{2,1,0:T(8,128)(2,1)S(1)} %collective-permute-done.1.refs_2_), channel_id=1, source_target_pairs={{0,1},{1,0},{2,3},{3,2},{4,5},{5,4},{6,7},{7,6},{8,9},{9,8},{10,11... | collective-permute-start | bytes 884744 | tf_op jit(solution)/shard_map/ppermute | solution.py:292
  54.3 5.4 %collective-permute-start.15 = (bf16[3,384,384]{2,1,0:T(8,128)(2,1)S(1)}, bf16[3,384,384]{2,1,0:T(8,128)(2,1)S(1)}, u32[]{:S(2)}, u32[]{:S(2)}) collective-permute-start(bf16[3,384,384]{2,1,0:T(8,128)(2,1)S(1)} %collective-permute-done.8.refs_2_), channel_id=1, source_target_pairs={{0,1},{1,0},{2,3},{3,2},{4,5},{5,4},{6,7},{7,6},{8,9},{9,8},{10,11... | collective-permute-start | bytes 2654216 | tf_op jit(solution)/shard_map/ppermute | solution.py:292
  55.8 2.2 %collective-permute-start.14 = (bf16[2,384,384]{2,1,0:T(8,128)(2,1)S(1)}, bf16[2,384,384]{2,1,0:T(8,128)(2,1)S(1)}, u32[]{:S(2)}, u32[]{:S(2)}) collective-permute-start(bf16[2,384,384]{2,1,0:T(8,128)(2,1)S(1)} %collective-permute-done.7.refs_2_), channel_id=1, source_target_pairs={{0,1},{1,0},{2,3},{3,2},{4,5},{5,4},{6,7},{7,6},{8,9},{9,8},{10,11... | collective-permute-start | bytes 1769480 | tf_op jit(solution)/shard_map/ppermute | solution.py:292

commit v4 on v3

--- a/solution.py
+++ b/solution.py
@@ -55,19 +55,15 @@
     def moved(index, step):
         return index + step - 2 * step * ((index // step) % 2)
 
-    first = 2 + 2 * (s % 2)
-    second = 6 - first
-    mate = flip(s, 1)
-    return {
-        "near": (s, moved(s, first)),
-        "far": (moved(s, second), flip(flip(s, 2), 4)),
-        "mate_near": (mate, moved(mate, second)),
-        "mate_far": (moved(mate, first), flip(flip(mate, 2), 4)),
-        "first": (s % 2,),
-        "last": (2 + s % 2, 4 + s % 2, 6 + s % 2),
-        "mate_first": (mate % 2,),
-        "mate_last": (2 + mate % 2, 4 + mate % 2, 6 + mate % 2),
-    }[name]
+    mine, mate = s, flip(s, 1)
+    first, second = 2 + 2 * (s % 2), 4 - 2 * (s % 2)
+    if name.startswith("mate_"):
+        mine, first, second = mate, second, first
+    name = name.removeprefix("mate_")
+    if name in ("first", "last"):
+        return [(matrix, mine % 2, None) for matrix in ((1,) if name == "first" else (2, 3))]
+    pair = (mine, moved(mine, first)) if name == "near" else (moved(mine, second), flip(flip(mine, 2), 4))
+    return [(q // 2, mine % 2, q) for q in pair]
 
 
 def prepare_kernel(signal, cot, tap, out, piece, first, to_next, to_previous, stage, sem, sems):
@@ -77,8 +73,11 @@
     rows = signal.shape[1]
     step = DILATION_STEP
     part = pl.ds(pl.multiple_of(half * size, 128), size)
+    eighth = pl.ds(pl.multiple_of(s * (size // PLANE), 16), size // PLANE)
     copies = [
-        (tap.at[0:1, :, part], first),
+        (tap.at[1, :, part], first.at[0, 0:size]),
+        (tap.at[0, eighth, 0:size], first.at[0, pl.ds(size, size // PLANE)]),
+        (tap.at[0, eighth, size : 2 * size], first.at[0, pl.ds(size + size // PLANE, size // PLANE)]),
         (signal.at[:, rows - 2 * step :], to_next.at[:, 0 : 2 * step]),
         (cot.at[:, rows - step :], to_next.at[:, 2 * step :]),
         (cot.at[:, 0:step], to_previous.at[:, 0:step]),
@@ -111,12 +110,12 @@
     half = lax.axis_index("seq") % 2
     size = last.shape[1]
     part = pl.ds(pl.multiple_of(half * size, 128), size)
-    copies = [(out.at[part, :], stage), (tap.at[1:3, :, part], last.at[0:2])]
+    copies = [(out.at[part, :], stage), (tap.at[2, :, part], last.at[0])]
     copies = [pltpu.make_async_copy(a, b, sems.at[n]) for n, (a, b) in enumerate(copies)]
     for copy in copies:
         copy.start()
     copies[0].wait()
-    last[2] = stage[...].T
+    last[1] = stage[...].T
     copies[1].wait()
 
 
@@ -141,6 +140,16 @@
         copy.wait()
 
 
+def join_kernel(piece, first, both, sems):
+    size = piece.shape[0]
+    copies = [(piece, both.at[0:size]), (first.at[0, size:], both.at[size:])]
+    copies = [pltpu.make_async_copy(a, b, sems.at[n]) for n, (a, b) in enumerate(copies)]
+    for copy in copies:
+        copy.start()
+    for copy in copies:
+        copy.wait()
+
+
 def edge_kernel(low, high, left_in, left, sems):
     reach = 2 * DILATION_STEP
     windows = low.shape[0]
@@ -166,82 +175,134 @@
 LAST = (((1,), (1,)), ((), ()))
 
 
-def own_kernel(left, tap, out, sums):
+def own_kernel(left, tap, out, *sums):
+    sums, out_t = sums[:2], sums[2]
+    out_t[...] = out[...].T
     rows = left.shape[2] - 2 * DILATION_STEP
-    columns = slot_columns(0, tap.shape[1])
-    inner = None
-    for k in range(3):
-        term = jnp.dot(rows_of(left, 0, k * DILATION_STEP, rows, columns), tap[k], preferred_element_type=F32)
-        inner = term if inner is None else inner + term
-    sums[0] = inner
-    sums[1] = lax.dot_general(rows_of(left, 1, 0, rows, columns), out[...], LAST, preferred_element_type=F32)
-
-
-def slot_kernel(slot, names, fresh, *refs):
+    size = tap.shape[1]
+    columns = slot_columns(0, size)
+    core = lax.axis_index("seq") % 2
+    for side, half in zip(sums, (core, 1 - core)):
+        part = pl.ds(pl.multiple_of(half * size, 128), size)
+        inner = None
+        for k in range(3):
+            lhs = rows_of(left, 0, k * DILATION_STEP, rows, columns)
+            term = jnp.dot(lhs, tap[k, :, part], preferred_element_type=F32)
+            inner = term if inner is None else inner + term
+        side[0] = inner
+        lhs = rows_of(left, 1, 0, rows, columns)
+        side[1] = lax.dot_general(lhs, out[part, :], LAST, preferred_element_type=F32)
+
+
+def slot_kernel(slot, names, sides, fresh, carries, *refs):
     count = len(names)
-    left, sums_in = refs[0], refs[1]
-    buffers = refs[2 : 2 + count]
-    sums, whole, sems = refs[-3:]
+    left, refs = refs[0], refs[1:]
+    sums_in, refs = refs[:sides], refs[sides:]
+    buffers, refs = refs[:count], refs[count:]
+    refs = refs[0 if fresh else (2 if carries else 1) :]
+    sums, whole, sems = refs[:sides], refs[sides], refs[-1]
     rows = left.shape[2] - 2 * DILATION_STEP
-    size = buffers[0].shape[1]
+    size = buffers[0].shape[2]
+    eighth = size // PLANE
     columns = slot_columns(slot, size)
-    pieces = [(b, i, q) for b, name in zip(buffers, names) for i, q in enumerate(held(name))]
     copies = []
-    for n, (buffer, i, q) in enumerate(pieces):
-        half = pl.ds(pl.multiple_of((q % 2) * size, 128), size)
-        copies.append(pltpu.make_async_copy(buffer.at[i], whole.at[q // 2, :, half], sems.at[n]))
-        copies[-1].start()
     for buffer, name in zip(buffers, names):
-        terms = []
-        for i, q in enumerate(held(name)):
-            matrix = q // 2
-            offset = pl.multiple_of((matrix % 3) * DILATION_STEP, DILATION_STEP)
-            lhs = rows_of(left, matrix // 3, offset, rows, columns)
-            terms.append((matrix // 3, jnp.dot(lhs, buffer[i], preferred_element_type=F32)))
-        half = pl.ds(pl.multiple_of((held(name)[0] % 2) * size, 128), size)
-        for which in range(2):
-            total = sums_in[which, :, half]
-            for place, term in terms:
-                total = total + jnp.where(place == which, term, 0.0)
-            sums[which, :, half] = total
-    for copy in copies:
-        copy.wait()
-
-
-def middle_kernel(sums, right):
+        for i, (matrix, half, q) in enumerate(held(name)):
+            part = pl.ds(pl.multiple_of(half * size, 128), size)
+            copies.append((buffer.at[i, 0:size], whole.at[matrix, :, part]))
+            if carries:
+                at = pl.ds(pl.multiple_of(q * eighth, 16), eighth)
+                for h in range(2):
+                    source = buffer.at[i, pl.ds(size + h * eighth, eighth)]
+                    copies.append((source, refs[sides + 1].at[at, pl.ds(h * size, size)]))
+    copies = [pltpu.make_async_copy(a, b, sems.at[n]) for n, (a, b) in enumerate(copies)]
+    for copy in copies:
+        copy.start()
+    for n, (side_in, side) in enumerate(zip(sums_in, sums)):
+        totals = [side_in[0], side_in[1]]
+        for buffer, name in zip(buffers, names):
+            if sides == 2 and name.startswith("mate_") != (n == 1):
+                continue
+            for i, (matrix, _, _) in enumerate(held(name)):
+                offset = (matrix % 3) * DILATION_STEP
+                if not isinstance(matrix, int):
+                    offset = pl.multiple_of(offset, DILATION_STEP)
+                lhs = rows_of(left, matrix // 3, offset, rows, columns)
+                term = jnp.dot(lhs, buffer[i, 0:size], preferred_element_type=F32)
+                for which in range(2):
+                    if not isinstance(matrix, int):
+                        totals[which] = totals[which] + jnp.where(matrix // 3 == which, term, 0.0)
+                    elif matrix // 3 == which:
+                        totals[which] = totals[which] + term
+        side[0], side[1] = totals
+    for copy in copies:
+        copy.wait()
+
+
+def tap_kernel(left, tap, *sums):
+    rows = left.shape[2] - 2 * DILATION_STEP
+    size = tap.shape[0]
+    core = lax.axis_index("seq") % 2
+    lhs = rows_of(left, 0, 0, rows, slot_columns(1, size))
+    for side_in, side, half in zip(sums[:2], sums[2:], (core, 1 - core)):
+        part = pl.ds(pl.multiple_of(half * size, 128), size)
+        side[0] = side_in[0] + jnp.dot(lhs, tap[:, part], preferred_element_type=F32)
+        side[1] = side_in[1]
+
+
+def middle_kernel(own, mate, right):
     windows, rows = right.shape[1:3]
-    v = sums[0]
-    square = v * v
-    t = jnp.tanh(ROOT * v * (1.0 + CUBIC * square))
-    slope = 0.5 * (1.0 + t) + (0.5 * ROOT) * v * (1.0 - t * t) * (1.0 + 3.0 * CUBIC * square)
-    right[0] = (sums[1] * slope).astype(BF16).reshape(right.shape[1:])
-    active = (0.5 * v * (1.0 + t)).astype(BF16).reshape(right.shape[1:])
-    right[1, :, 2 * DILATION_STEP :] = active[:, DILATION_STEP : rows - DILATION_STEP]
-
-
-def back_kernel(signal, cot, slope, right, tap, out, *refs):
-    wholes, (result, grad) = refs[:3], refs[3:]
+    size = own.shape[2]
+    core = lax.axis_index("seq") % 2
+    for sums, half in ((own, core), (mate, 1 - core)):
+        part = pl.ds(pl.multiple_of(half * size, 128), size)
+        v = sums[0]
+        square = v * v
+        t = jnp.tanh(ROOT * v * (1.0 + CUBIC * square))
+        slope = 0.5 * (1.0 + t) + (0.5 * ROOT) * v * (1.0 - t * t) * (1.0 + 3.0 * CUBIC * square)
+        right[0, :, :, part] = (sums[1] * slope).astype(BF16).reshape(windows, rows, size)
+        active = (0.5 * v * (1.0 + t)).astype(BF16).reshape(windows, rows, size)
+        right[1, :, 2 * DILATION_STEP :, part] = active[:, DILATION_STEP : rows - DILATION_STEP]
+
+
+def back_kernel(signal, cot, slope, right, tap, out_t, pair_tap, *refs):
+    wholes, (result, grad), (result_part, grad_part, sems) = refs[:3], refs[3:5], refs[5:]
     windows, rows, _ = signal.shape
     width = tap.shape[1]
     step = DILATION_STEP
     everything = slice(None)
     shifted = [rows_of(right, 0, (2 - k) * step, rows, everything) for k in range(3)]
     active = rows_of(right, 1, 2 * step, rows, everything)
-    for slot in range(4):
-        columns = slot_columns(slot, width)
-        matrices = tap if slot == 0 else wholes[slot - 1]
+
+    def matrix(slot, k):
+        if slot == 0:
+            return tap[k] if k < 3 else out_t[...]
+        return pair_tap[...] if (slot, k) == (1, 0) else wholes[slot - 1][k]
+
+    copies = []
+    for slots in ((0, 1), (2, 3)):
         total = None
-        for k in range(3):
-            term = lax.dot_general(shifted[k], matrices[k], LAST, preferred_element_type=F32)
-            total = term if total is None else total + term
-        if slot == 0:
-            more = jnp.dot(active, out[...], preferred_element_type=F32)
-        else:
-            more = lax.dot_general(active, matrices[3], LAST, preferred_element_type=F32)
-        for w in range(windows):
-            at = slice(w * rows, (w + 1) * rows)
-            grad[w, :, columns] = (cot[w, :, columns].astype(F32) + total[at] * slope[w, :, columns]).astype(BF16)
-            result[w, :, columns] = (signal[w, :, columns].astype(F32) + more[at]).astype(BF16)
+        for k in range(4):
+            both = jnp.concatenate([matrix(slot, k) for slot in slots], axis=0)
+            term = lax.dot_general(shifted[k] if k < 3 else active, both, LAST, preferred_element_type=F32)
+            if k == 3:
+                more = term
+            else:
+                total = term if total is None else total + term
+        for n, slot in enumerate(slots):
+            columns = slot_columns(slot, width)
+            here = slice(n * width, (n + 1) * width)
+            for w in range(windows):
+                at = slice(w * rows, (w + 1) * rows)
+                change = total[at, here] * slope[w, :, columns]
+                grad_part[w, :, columns] = (cot[w, :, columns].astype(F32) + change).astype(BF16)
+                result_part[w, :, columns] = (signal[w, :, columns].astype(F32) + more[at, here]).astype(BF16)
+            for m, (part, whole) in enumerate(((result_part, result), (grad_part, grad))):
+                copy = pltpu.make_async_copy(part.at[:, :, columns], whole.at[:, :, columns], sems.at[2 * slot + m])
+                copy.start()
+                copies.append(copy)
+    for copy in copies:
+        copy.wait()
 
 
 def cost(microseconds):
@@ -274,7 +335,7 @@
         prepare_kernel,
         out_shape=[
             jax.ShapeDtypeStruct((width, width), BF16),
-            jax.ShapeDtypeStruct((1, width, width), BF16),
+            jax.ShapeDtypeStruct((1, width + 2 * (width // PLANE), width), BF16),
             edge,
             edge,
         ],
@@ -283,7 +344,7 @@
         scratch_shapes=[
             pltpu.VMEM((width, width), BF16),
             pltpu.SemaphoreType.DMA,
-            pltpu.SemaphoreType.DMA((5,)),
+            pltpu.SemaphoreType.DMA((7,)),
         ],
         compiler_params=params(8),
     )(stay(signal), stay(cot), stay(tap), stay(out))
@@ -294,36 +355,43 @@
     def over(block, bits):
         return lax.ppermute(block, "dp", [(i, i ^ bits) for i in range(4)])
 
-    def pair(first, second):
+    def moved_by(kernel, shape, *given):
         return pl.pallas_call(
-            pair_kernel,
-            out_shape=jax.ShapeDtypeStruct((2, width, width), BF16),
+            kernel,
+            out_shape=jax.ShapeDtypeStruct(shape, BF16),
             in_specs=[hbm] * 2,
             out_specs=vmem,
             scratch_shapes=[pltpu.SemaphoreType.DMA((2,))],
             compiler_params=params(2),
             cost_estimate=cost(0.3),
-        )(first, second)
-
-    sums_shape = jax.ShapeDtypeStruct((2, windows * wide_rows, hidden), F32)
+        )(*given)
+
+    def pair(first, second):
+        return moved_by(pair_kernel, (2, *first.shape), first, second)
+
+    side_shape = jax.ShapeDtypeStruct((2, windows * wide_rows, width), F32)
     whole_shape = jax.ShapeDtypeStruct((4, width, hidden), BF16)
-
-    def add_slot(slot, names, buffers, left, sums, whole=None):
-        fresh = whole is None
-        given = [left, sums, *buffers] + ([] if fresh else [whole])
-        aliases = {1: 0}
-        if not fresh:
-            aliases[len(given) - 1] = 1
-        return pl.pallas_call(
-            functools.partial(slot_kernel, slot, names, fresh),
-            out_shape=[sums_shape, whole_shape],
-            in_specs=[vmem] * len(given),
-            out_specs=[vmem] * 2,
-            scratch_shapes=[pltpu.SemaphoreType.DMA((sum(b.shape[0] for b in buffers),))],
+    tap_shape = jax.ShapeDtypeStruct((width, hidden), BF16)
+
+    def add_slot(slot, names, buffers, left, sums, *wholes, carries=False):
+        given = [left, *sums, *buffers, *wholes]
+        sides = len(sums)
+        aliases = {1 + n: n for n in range(sides)}
+        for n in range(len(wholes)):
+            aliases[1 + sides + len(buffers) + n] = sides + n
+        shapes = [side_shape] * sides + [whole_shape] + [tap_shape] * carries
+        copies = sum(b.shape[0] for b in buffers) * (3 if carries else 1)
+        done = pl.pallas_call(
+            functools.partial(slot_kernel, slot, names, sides, not wholes, carries),
+            out_shape=shapes,
+            in_specs=[vmem] * (1 + sides + len(buffers)) + [hbm] * len(wholes),
+            out_specs=[vmem] * sides + [hbm] * (1 + carries),
+            scratch_shapes=[pltpu.SemaphoreType.DMA((copies,))],
             input_output_aliases=aliases,
             compiler_params=params(4),
             cost_estimate=cost(0.7 * len(names)),
         )(*given)
+        return done[:sides], *done[sides:]
 
     p2 = over(mine, 2)
     first = over(first, 1)
@@ -340,7 +408,7 @@
     )(signal, cot)
     last = pl.pallas_call(
         half_kernel,
-        out_shape=jax.ShapeDtypeStruct((3, width, width), BF16),
+        out_shape=jax.ShapeDtypeStruct((2, width, width), BF16),
         in_specs=[hbm] * 2,
         out_specs=vmem,
         scratch_shapes=[pltpu.VMEM((width, width), BF16), pltpu.SemaphoreType.DMA((2,))],
@@ -348,8 +416,9 @@
         cost_estimate=cost(1.5),
     )(stay(tap), stay(out))
     p2, first, left, last = tie(p2, first, left, last)
-    near2 = across(p2, 2, 4)
     p3 = over(p2, 1)
+    got2 = moved_by(join_kernel, (first.shape[1], width), p2, first)
+    near2 = across(got2, 2, 4)
     left = pl.pallas_call(
         edge_kernel,
         out_shape=left_shape,
@@ -360,17 +429,17 @@
         compiler_params=params(4),
         cost_estimate=cost(0.5),
     )(low, high, left)
-    sums = pl.pallas_call(
+    *sums, out_t = pl.pallas_call(
         own_kernel,
-        out_shape=sums_shape,
+        out_shape=[side_shape] * 2 + [tap_shape],
         in_specs=[vmem] * 3,
-        out_specs=vmem,
+        out_specs=[vmem] * 3,
         compiler_params=params(4),
         cost_estimate=cost(1.4),
     )(left, tap, out)
     near_names, far_names = ("near", "mate_near"), ("far", "mate_far")
     mate_first = across(first, 1, 1)
-    own2 = pair(p2, near2)
+    own2 = pair(got2, near2)
     own2, left = tie(own2, left)
     far2 = across(own2, 4, 2)
     mate2 = across(own2, 1, 1)
@@ -379,38 +448,46 @@
     last = over(last, 1)
     far_mate2 = across(far2, 1, 1)
     own3 = pair(p3, near3)
-    own3, sums = tie(own3, sums)
+    own3, *sums = tie(own3, *sums)
     far3 = across(own3, 4, 2)
     mate3 = across(own3, 1, 1)
-    sums, whole2 = add_slot(2, near_names, (own2, mate2), left, sums)
+    mate_last = across(last, 1, 1)
+    sums, whole2, pair_tap = add_slot(2, near_names, (own2, mate2), left, sums, carries=True)
     sums, whole1 = add_slot(1, ("first", "mate_first"), (first, mate_first), left, sums)
     sums, whole3 = add_slot(3, near_names, (own3, mate3), left, sums)
-    last, sums = tie(last, sums)
-    mate_last = across(last, 1, 1)
-    sums, whole2 = add_slot(2, far_names, (far2, far_mate2), left, sums, whole2)
-    far3, sums = tie(far3, sums)
+    sums, whole1 = add_slot(1, ("last", "mate_last"), (last, mate_last), left, sums, whole1)
+    far3, *sums = tie(far3, *sums)
     far_mate3 = across(far3, 1, 1)
-    sums, whole3 = add_slot(3, ("far",), (far3,), left, sums, whole3)
-    sums, whole3 = add_slot(3, ("mate_far",), (far_mate3,), left, sums, whole3)
-    sums, whole1 = add_slot(1, ("last",), (last,), left, sums, whole1)
-    sums, whole1 = add_slot(1, ("mate_last",), (mate_last,), left, sums, whole1)
+    sums, whole2, pair_tap = add_slot(2, far_names, (far2, far_mate2), left, sums, whole2, pair_tap, carries=True)
+    sums = pl.pallas_call(
+        tap_kernel,
+        out_shape=[side_shape] * 2,
+        in_specs=[vmem] * 4,
+        out_specs=[vmem] * 2,
+        input_output_aliases={2: 0, 3: 1},
+        compiler_params=params(4),
+        cost_estimate=cost(0.5),
+    )(left, pair_tap, *sums)
+    (own_sums,), whole3 = add_slot(3, ("far",), (far3,), left, sums[:1], whole3)
+    (mate_sums,), whole3 = add_slot(3, ("mate_far",), (far_mate3,), left, sums[1:], whole3)
 
     right = pl.pallas_call(
         middle_kernel,
         out_shape=jax.ShapeDtypeStruct((2, windows, wide_rows, hidden), BF16),
-        in_specs=[vmem],
+        in_specs=[vmem] * 2,
         out_specs=vmem,
         compiler_params=params(4),
         cost_estimate=cost(0.8),
-    )(sums)
+    )(own_sums, mate_sums)
     result, grad_signal = pl.pallas_call(
         back_kernel,
         out_shape=[jax.ShapeDtypeStruct(signal.shape, BF16)] * 2,
-        in_specs=[vmem] * 9,
-        out_specs=[vmem] * 2,
+        in_specs=[vmem] * 10,
+        out_specs=[hbm] * 2,
+        scratch_shapes=[pltpu.VMEM(signal.shape, BF16)] * 2 + [pltpu.SemaphoreType.DMA((8,))],
         compiler_params=params(8),
         cost_estimate=cost(4.5),
-    )(signal, cot, slope, right, tap, out, whole1, whole2, whole3)
+    )(signal, cot, slope, right, tap, out_t, pair_tap, whole1, whole2, whole3)
     return result, grad_signal
 
 

time: 66.4 us -> 63 us (0.949)
  waiting for transfers between devices: 29.5 us -> 21.5 us
  starting transfers between devices: 15.3 us -> 20.4 us
    ppermute x10, waiting for transfers between devices: 16.4 us -> 7.84 us  [across(): return lax.ppermute(block, 'seq', plane_pairs(count, even, odd))]
    ppermute x10, starting transfers between devices: 5.13 us -> 7.75 us  [across(): return lax.ppermute(block, 'seq', plane_pairs(count, even, odd))]
    ppermute x4, starting transfers between devices: 7.57 us -> 10 us  [over(): return lax.ppermute(block, 'dp', [(i, i ^ bits) for i in range(4)])]
    pallas_call x1, Pallas kernels: 4.43 us -> 3.54 us  [per_device(): pl.pallas_call(back_kernel, out_shape=[jax.ShapeDtypeStruct(signal.shape,...]
    pallas_call x12 -> x13, Pallas kernels: 11.9 us -> 12 us  [the longest x7 7.82 us: add_slot(): pl.pallas_call(functools.partial(slot_kernel, slot, names, sides, not who...]
  transfers between devices with their start and end apart: 16 -> 16, of which waited for: 8 -> 7; matrix products, arithmetic and copies ran while one was open for 0% -> 0% of each run, Pallas kernels for 19% -> 21%
where the time goes in v4:
time: 63 us; the launch traced here: 62.8 us
  waiting for transfers between devices  21.5 us (34%)
  starting transfers between devices  20.4 us (32%)
  Pallas kernels  19.9 us (32%)
  between operations  1.05 us (2%)
    ppermute x4, waiting for transfers between devices, over(): return lax.ppermute(block, 'dp', [(i, i ^ bits) for i in range(4)])  13.7 us
    ppermute x4, starting transfers between devices, over(): return lax.ppermute(block, 'dp', [(i, i ^ bits) for i in range(4)])  10 us
    ppermute x10, waiting for transfers between devices, across(): return lax.ppermute(block, 'seq', plane_pairs(count, even, odd))  7.84 us
    pallas_call x7, Pallas kernels, add_slot(): pl.pallas_call(functools.partial(slot_kernel, slot, names, sides, not who...  7.82 us
    ppermute x10, starting transfers between devices, across(): return lax.ppermute(block, 'seq', plane_pairs(count, even, odd))  7.75 us
    pallas_call x1, Pallas kernels, per_device(): pl.pallas_call(back_kernel, out_shape=[jax.ShapeDtypeStruct(signal.shape,...  3.54 us
    pallas_call x1, Pallas kernels, per_device(): pl.pallas_call(prepare_kernel, out_shape=[jax.ShapeDtypeStruct((width, wi...  1.65 us
    pallas_call x1, Pallas kernels, per_device(): pl.pallas_call(own_kernel, out_shape=[side_shape] * 2 + [tap_shape], in_s...  1.63 us
  transfers between devices with their start and end apart: 16, of which 7 were waited for; matrix products, arithmetic and copies ran while one was open for 0% of the time, Pallas kernels for 21%

profile of v4, /device:TPU:0, one launch (start us, length us, event | category | flops | bytes accessed | tf_op | source)
XLA Modules:
  0.0 62.8 jit_solution(16955540399498878781)
XLA Ops:
  0.6 1.6 %shard_map.60 = (bf16[384,384]{1,0:T(8,128)(2,1)S(1)}, bf16[1,480,384]{2,1,0:T(8,128)(2,1)S(1)}, bf16[2,96,1536]{2,1,0:T(8,128)(2,1)S(1)}, bf16[2,96,1536]{2,1,0:T(8,128)(2,1)S(1)}) custom-call(bf16[2,128,1536]{2,1,0:T(8,128)(2,1)} %signal.5, bf16[2,128,1536]{2,1,0:T(8,128)(2,1)} %cot.5, bf16[3,384,768]{2,1,0:T(8,128)(2,1)} %tap.7, bf16[768,384]{1,0:T(8,128)(2,1)} %out.5), custom_call_target="tpu_custom_call" | custom-call | tf_op jit(solution)/shard_map/pallas_call | solution.py:334
  2.3 3.1 %collective-permute-start.1 = (bf16[1,480,384]{2,1,0:T(8,128)(2,1)S(1)}, bf16[1,480,384]{2,1,0:T(8,128)(2,1)S(1)}, u32[]{:S(2)}, u32[]{:S(2)}) collective-permute-start(bf16[1,480,384]{2,1,0:T(8,128)(2,1)S(1)} %get-tuple-element.50), channel_id=1, source_target_pairs={{0,8},{8,0},{16,24},{24,16},{1,9},{9,1},{17,25},{25,17},{2,10},{10... | collective-permute-start | bytes 1105928 | tf_op jit(solution)/shard_map/ppermute | solution.py:356
  5.4 2.6 %collective-permute-start = (bf16[384,384]{1,0:T(8,128)(2,1)S(1)}, bf16[384,384]{1,0:T(8,128)(2,1)S(1)}, u32[]{:S(2)}, u32[]{:S(2)}) collective-permute-start(bf16[384,384]{1,0:T(8,128)(2,1)S(1)} %get-tuple-element.49), channel_id=1, source_target_pairs={{0,16},{8,24},{16,0},{24,8},{1,17},{9,25},{17,1},{25,9},{2,18},{10... | collective-permute-start | bytes 884744 | tf_op jit(solution)/shard_map/ppermute | solution.py:356
  8.0 1.3 %collective-permute-start.3 = (bf16[2,96,1536]{2,1,0:T(8,128)(2,1)S(1)}, bf16[2,96,1536]{2,1,0:T(8,128)(2,1)S(1)}, u32[]{:S(2)}, u32[]{:S(2)}) collective-permute-start(bf16[2,96,1536]{2,1,0:T(8,128)(2,1)S(1)} %get-tuple-element.54), channel_id=1, source_target_pairs={{0,1},{1,2},{2,3},{3,4},{4,5},{5,6},{6,7},{8,9},{9,10},{10,11},{11... | collective-permute-start | bytes 1769480 | tf_op jit(solution)/shard_map/ppermute | solution.py:398
  9.3 1.3 %collective-permute-start.4 = (bf16[2,96,1536]{2,1,0:T(8,128)(2,1)S(1)}, bf16[2,96,1536]{2,1,0:T(8,128)(2,1)S(1)}, u32[]{:S(2)}, u32[]{:S(2)}) collective-permute-start(bf16[2,96,1536]{2,1,0:T(8,128)(2,1)S(1)} %get-tuple-element.55), channel_id=1, source_target_pairs={{1,0},{2,1},{3,2},{4,3},{5,4},{6,5},{7,6},{9,8},{10,9},{11,10},{12... | collective-permute-start | bytes 1769480 | tf_op jit(solution)/shard_map/ppermute | solution.py:399
  10.6 1.1 %shard_map.59 = (bf16[2,2,256,1536]{3,2,1,0:T(8,128)(2,1)S(1)}, f32[2,128,1536]{2,1,0:T(8,128)S(1)}) custom-call(bf16[2,128,1536]{2,1,0:T(8,128)(2,1)S(1)} %copy-done.1, bf16[2,128,1536]{2,1,0:T(8,128)(2,1)S(1)} %copy-done.2), custom_call_target="tpu_custom_call" | custom-call | flops 1000 | bytes 1000 | tf_op jit(solution)/shard_map/pallas_call | solution.py:401
  11.7 1.1 %shard_map.61 = bf16[2,384,384]{2,1,0:T(8,128)(2,1)S(1)} custom-call(bf16[3,384,768]{2,1,0:T(8,128)(2,1)} %tap.7, bf16[768,384]{1,0:T(8,128)(2,1)} %out.5), custom_call_target="tpu_custom_call" | custom-call | flops 1000 | bytes 1000 | tf_op jit(solution)/shard_map/pallas_call | solution.py:409
  12.9 6.7 %collective-permute-done.piece = bf16[384,384]{1,0:T(8,128)(2,1)S(1)} collective-permute-done((bf16[384,384]{1,0:T(8,128)(2,1)S(1)}, bf16[384,384]{1,0:T(8,128)(2,1)S(1)}, u32[]{:S(2)}, u32[]{:S(2)}) %collective-permute-start) | collective-permute-done | bytes 294944 | tf_op jit(solution)/shard_map/ppermute | solution.py:356
  20.5 1.7 %collective-permute-start.2 = (bf16[480,384]{1,0:T(8,128)(2,1)S(1)}, bf16[480,384]{1,0:T(8,128)(2,1)S(1)}, u32[]{:S(2)}, u32[]{:S(2)}) collective-permute-start(bf16[480,384]{1,0:T(8,128)(2,1)S(1)} %shard_map.62.first), channel_id=1, source_target_pairs={{0,2},{1,5},{2,0},{3,7},{4,6},{5,1},{6,4},{7,3},{8,10},{9,13},{10,... | collective-permute-start | bytes 1105928 | tf_op jit(solution)/shard_map/ppermute | solution.py:353
  22.2 2.6 %collective-permute-start.5 = (bf16[384,384]{1,0:T(8,128)(2,1)S(1)}, bf16[384,384]{1,0:T(8,128)(2,1)S(1)}, u32[]{:S(2)}, u32[]{:S(2)}) collective-permute-start(bf16[384,384]{1,0:T(8,128)(2,1)S(1)} %collective-permute-done.piece), channel_id=1, source_target_pairs={{0,8},{8,0},{16,24},{24,16},{1,9},{9,1},{17,25},{25,17},{2,10},{10... | collective-permute-start | bytes 884744 | tf_op jit(solution)/shard_map/ppermute | solution.py:356
  24.8 5.9 %collective-permute-done.5.first = bf16[384,384]{1,0:T(8,128)(2,1)S(1)} collective-permute-done((bf16[384,384]{1,0:T(8,128)(2,1)S(1)}, bf16[384,384]{1,0:T(8,128)(2,1)S(1)}, u32[]{:S(2)}, u32[]{:S(2)}) %collective-permute-start.5) | collective-permute-done | bytes 294944 | tf_op jit(solution)/shard_map/ppermute | solution.py:356
  30.7 1.7 %collective-permute-start.11 = (bf16[2,384,384]{2,1,0:T(8,128)(2,1)S(1)}, bf16[2,384,384]{2,1,0:T(8,128)(2,1)S(1)}, u32[]{:S(2)}, u32[]{:S(2)}) collective-permute-start(bf16[2,384,384]{2,1,0:T(8,128)(2,1)S(1)} %shard_map.61), channel_id=1, source_target_pairs={{0,8},{8,0},{16,24},{24,16},{1,9},{9,1},{17,25},{25,17},{2,10},{10... | collective-permute-start | bytes 1769480 | tf_op jit(solution)/shard_map/ppermute | solution.py:356
  33.7 1.6 %collective-permute-start.6 = (bf16[384,384]{1,0:T(8,128)(2,1)S(1)}, bf16[384,384]{1,0:T(8,128)(2,1)S(1)}, u32[]{:S(2)}, u32[]{:S(2)}) collective-permute-start(bf16[384,384]{1,0:T(8,128)(2,1)S(1)} %collective-permute-done.5.first), channel_id=1, source_target_pairs={{0,2},{1,5},{2,0},{3,7},{4,6},{5,1},{6,4},{7,3},{8,10},{9,13},{10,... | collective-permute-start | bytes 884744 | tf_op jit(solution)/shard_map/ppermute | solution.py:353
  35.8 1.6 %shard_map.66 = (f32[2,384,384]{2,1,0:T(8,128)S(1)}, f32[2,384,384]{2,1,0:T(8,128)S(1)}, bf16[384,768]{1,0:T(8,128)(2,1)S(1)}) custom-call(bf16[2,2,256,1536]{3,2,1,0:T(8,128)(2,1)S(1)} %shard_map.64.left.refs_0_, bf16[3,384,768]{2,1,0:T(8,128)(2,1)S(1)} %copy-done, bf16[768,384]{1,0:T(8,128)(2,1)S(1)} %copy-done.3), custom_call_target="tpu_custom_call" | custom-call | flops 1000 | bytes 1000 | tf_op jit(solution)/shard_map/pallas_call | solution.py:432
  37.4 6.0 %collective-permute-done.6.second = bf16[384,384]{1,0:T(8,128)(2,1)S(1)} collective-permute-done((bf16[384,384]{1,0:T(8,128)(2,1)S(1)}, bf16[384,384]{1,0:T(8,128)(2,1)S(1)}, u32[]{:S(2)}, u32[]{:S(2)}) %collective-permute-start.6) | collective-permute-done | bytes 294944 | tf_op jit(solution)/shard_map/ppermute | solution.py:353
  44.1 1.4 %collective-permute-start.7 = (bf16[2,384,384]{2,1,0:T(8,128)(2,1)S(1)}, bf16[2,384,384]{2,1,0:T(8,128)(2,1)S(1)}, u32[]{:S(2)}, u32[]{:S(2)}) collective-permute-start(bf16[2,384,384]{2,1,0:T(8,128)(2,1)S(1)} %shard_map.65.refs_3_), channel_id=1, source_target_pairs={{0,4},{1,3},{2,6},{3,1},{4,0},{5,7},{6,2},{7,5},{8,12},{9,11},{10,... | collective-permute-start | bytes 1769480 | tf_op jit(solution)/shard_map/ppermute | solution.py:353
  45.5 1.3 %collective-permute-start.9 = (bf16[1,480,384]{2,1,0:T(8,128)(2,1)S(1)}, bf16[1,480,384]{2,1,0:T(8,128)(2,1)S(1)}, u32[]{:S(2)}, u32[]{:S(2)}) collective-permute-start(bf16[1,480,384]{2,1,0:T(8,128)(2,1)S(1)} %collective-permute-done.1.first.refs_3_), channel_id=1, source_target_pairs={{0,1},{1,0},{2,3},{3,2},{4,5},{5,4},{6,7},{7,6},{8,9},{9,8},{10,11... | collective-permute-start | bytes 1105928 | tf_op jit(solution)/shard_map/ppermute | solution.py:353
  46.8 1.1 %collective-permute-done.13.refs_3_ = bf16[2,480,384]{2,1,0:T(8,128)(2,1)S(1)} collective-permute-done((bf16[2,480,384]{2,1,0:T(8,128)(2,1)S(1)}, bf16[2,480,384]{2,1,0:T(8,128)(2,1)S(1)}, u32[]{:S(2)}, u32[]{:S(2)}) %collective-permute-start.13) | collective-permute-done | bytes 737312 | tf_op jit(solution)/shard_map/ppermute | solution.py:353
  48.5 1.4 %shard_map.67 = (f32[2,384,384]{2,1,0:T(8,128)S(1)}, f32[2,384,384]{2,1,0:T(8,128)S(1)}, bf16[4,384,768]{2,1,0:T(8,128)(2,1)S(1)}, bf16[384,768]{1,0:T(8,128)(2,1)S(1)}) custom-call(bf16[2,2,256,1536]{3,2,1,0:T(8,128)(2,1)S(1)} %shard_map.64.left.refs_0_, ...), custom_call_target="tpu_custom_call", output_to_operand_aliasing={{0}: (1, {}), {1}: (2, {})} | custom-call | flops 1000 | bytes 1000 | tf_op jit(solution)/shard_map/pallas_call | solution.py:384
  50.8 1.3 %shard_map.69 = (f32[2,384,384]{2,1,0:T(8,128)S(1)}, f32[2,384,384]{2,1,0:T(8,128)S(1)}, bf16[4,384,768]{2,1,0:T(8,128)(2,1)S(1)}) custom-call(bf16[2,2,256,1536]{3,2,1,0:T(8,128)(2,1)S(1)} %shard_map.64.left.refs_0_, f32[2,384,384]{2,1,0:T(8,128)S(1)} %get-tuple-element.68.refs_1_, ...), custom_call_target="tpu_custom_call", output_to_operand_aliasing={{0}: (1, {}), {1}: (2, {})} | custom-call | flops 1000 | bytes 1000 | tf_op jit(solution)/shard_map/pallas_call | solution.py:384
  52.1 1.3 %shard_map.70 = (f32[2,384,384]{2,1,0:T(8,128)S(1)}, f32[2,384,384]{2,1,0:T(8,128)S(1)}, bf16[4,384,768]{2,1,0:T(8,128)(2,1)S(1)}) custom-call(bf16[2,2,256,1536]{3,2,1,0:T(8,128)(2,1)S(1)} %shard_map.64.left.refs_0_, f32[2,384,384]{2,1,0:T(8,128)S(1)} %get-tuple-element.70.refs_1_, ...), custom_call_target="tpu_custom_call", output_to_operand_aliasing={{0}: (1, {}), {1}: (2, {}), {2}: (5, {})} | custom-call | flops 1000 | bytes 1000 | tf_op jit(solution)/shard_map/pallas_call | solution.py:384
  54.5 1.4 %shard_map.71 = (f32[2,384,384]{2,1,0:T(8,128)S(1)}, f32[2,384,384]{2,1,0:T(8,128)S(1)}, bf16[4,384,768]{2,1,0:T(8,128)(2,1)S(1)}, bf16[384,768]{1,0:T(8,128)(2,1)S(1)}) custom-call(bf16[2,2,256,1536]{3,2,1,0:T(8,128)(2,1)S(1)} %shard_map.64.left.refs_0_, ...), custom_call_target="tpu_custom_call", output_to_operand_aliasing={{0}: (1, {}), {1}: (2, {}), {2}: (5, {}), {3}: (6, {})} | custom-call | flops 1000 | bytes 1000 | tf_op jit(solution)/shard_map/pallas_call | solution.py:384
  57.4 0.9 %shard_map.74 = (f32[2,384,384]{2,1,0:T(8,128)S(1)}, bf16[4,384,768]{2,1,0:T(8,128)(2,1)S(1)}) custom-call(bf16[2,2,256,1536]{3,2,1,0:T(8,128)(2,1)S(1)} %shard_map.64.left.refs_0_, f32[2,384,384]{2,1,0:T(8,128)S(1)} %get-tuple-element.87.refs_1_, ...), custom_call_target="tpu_custom_call", output_to_operand_aliasing={{0}: (1, {}), {1}: (3, {})} | custom-call | flops 1000 | bytes 1000 | tf_op jit(solution)/shard_map/pallas_call | solution.py:384
  59.1 3.5 %shard_map.76 = (bf16[2,128,1536]{2,1,0:T(8,128)(2,1)}, bf16[2,128,1536]{2,1,0:T(8,128)(2,1)}) custom-call(bf16[2,128,1536]{2,1,0:T(8,128)(2,1)S(1)} %copy-done.1, bf16[2,128,1536]{2,1,0:T(8,128)(2,1)S(1)} %copy-done.2, f32[2,128,1536]{2,1,0:T(8,128)S(1)} %get-tuple-element.48.slope, bf16[2,2,192,768]{3,2,1,0:T(8,128)(2,1)S(1)} %shard_map.75.right, ...), custom_call_target="tpu_custom_call" | custom-call | flops 1000 | bytes 1000 | tf_op jit(solution)/shard_map/pallas_call | solution.py:482
  (34 shorter events, 8.3 us)
Async XLA Ops:
  0.6 10.0 %copy-start.1 = (bf16[2,128,1536]{2,1,0:T(8,128)(2,1)S(1)}, bf16[2,128,1536]{2,1,0:T(8,128)(2,1)}, u32[]{:S(2)}) copy-start(bf16[2,128,1536]{2,1,0:T(8,128)(2,1)} %signal.5) | copy-start | bytes 2359300
  0.6 10.0 %copy-start.2 = (bf16[2,128,1536]{2,1,0:T(8,128)(2,1)S(1)}, bf16[2,128,1536]{2,1,0:T(8,128)(2,1)}, u32[]{:S(2)}) copy-start(bf16[2,128,1536]{2,1,0:T(8,128)(2,1)} %cot.5) | copy-start | bytes 2359300
  2.3 18.0 %collective-permute-start.1 = (bf16[1,480,384]{2,1,0:T(8,128)(2,1)S(1)}, bf16[1,480,384]{2,1,0:T(8,128)(2,1)S(1)}, u32[]{:S(2)}, u32[]{:S(2)}) collective-permute-start(bf16[1,480,384]{2,1,0:T(8,128)(2,1)S(1)} %get-tuple-element.50), channel_id=1, source_target_pairs={{0,8},{8,0},{16,24},{24,16},{1,9},{9,1},{17,25},{25,17},{2,10},{10... | collective-permute-start | bytes 1105928 | tf_op jit(solution)/shard_map/ppermute | solution.py:356
  5.4 14.2 %collective-permute-start = (bf16[384,384]{1,0:T(8,128)(2,1)S(1)}, bf16[384,384]{1,0:T(8,128)(2,1)S(1)}, u32[]{:S(2)}, u32[]{:S(2)}) collective-permute-start(bf16[384,384]{1,0:T(8,128)(2,1)S(1)} %get-tuple-element.49), channel_id=1, source_target_pairs={{0,16},{8,24},{16,0},{24,8},{1,17},{9,25},{17,1},{25,9},{2,18},{10... | collective-permute-start | bytes 884744 | tf_op jit(solution)/shard_map/ppermute | solution.py:356
  8.0 24.4 %collective-permute-start.3 = (bf16[2,96,1536]{2,1,0:T(8,128)(2,1)S(1)}, bf16[2,96,1536]{2,1,0:T(8,128)(2,1)S(1)}, u32[]{:S(2)}, u32[]{:S(2)}) collective-permute-start(bf16[2,96,1536]{2,1,0:T(8,128)(2,1)S(1)} %get-tuple-element.54), channel_id=1, source_target_pairs={{0,1},{1,2},{2,3},{3,4},{4,5},{5,6},{6,7},{8,9},{9,10},{10,11},{11... | collective-permute-start | bytes 1769480 | tf_op jit(solution)/shard_map/ppermute | solution.py:398
  9.3 23.1 %collective-permute-start.4 = (bf16[2,96,1536]{2,1,0:T(8,128)(2,1)S(1)}, bf16[2,96,1536]{2,1,0:T(8,128)(2,1)S(1)}, u32[]{:S(2)}, u32[]{:S(2)}) collective-permute-start(bf16[2,96,1536]{2,1,0:T(8,128)(2,1)S(1)} %get-tuple-element.55), channel_id=1, source_target_pairs={{1,0},{2,1},{3,2},{4,3},{5,4},{6,5},{7,6},{9,8},{10,9},{11,10},{12... | collective-permute-start | bytes 1769480 | tf_op jit(solution)/shard_map/ppermute | solution.py:399
  20.5 12.8 %collective-permute-start.2 = (bf16[480,384]{1,0:T(8,128)(2,1)S(1)}, bf16[480,384]{1,0:T(8,128)(2,1)S(1)}, u32[]{:S(2)}, u32[]{:S(2)}) collective-permute-start(bf16[480,384]{1,0:T(8,128)(2,1)S(1)} %shard_map.62.first), channel_id=1, source_target_pairs={{0,2},{1,5},{2,0},{3,7},{4,6},{5,1},{6,4},{7,3},{8,10},{9,13},{10,... | collective-permute-start | bytes 1105928 | tf_op jit(solution)/shard_map/ppermute | solution.py:353
  22.2 8.5 %collective-permute-start.5 = (bf16[384,384]{1,0:T(8,128)(2,1)S(1)}, bf16[384,384]{1,0:T(8,128)(2,1)S(1)}, u32[]{:S(2)}, u32[]{:S(2)}) collective-permute-start(bf16[384,384]{1,0:T(8,128)(2,1)S(1)} %collective-permute-done.piece), channel_id=1, source_target_pairs={{0,8},{8,0},{16,24},{24,16},{1,9},{9,1},{17,25},{25,17},{2,10},{10... | collective-permute-start | bytes 884744 | tf_op jit(solution)/shard_map/ppermute | solution.py:356
  30.7 13.3 %collective-permute-start.11 = (bf16[2,384,384]{2,1,0:T(8,128)(2,1)S(1)}, bf16[2,384,384]{2,1,0:T(8,128)(2,1)S(1)}, u32[]{:S(2)}, u32[]{:S(2)}) collective-permute-start(bf16[2,384,384]{2,1,0:T(8,128)(2,1)S(1)} %shard_map.61), channel_id=1, source_target_pairs={{0,8},{8,0},{16,24},{24,16},{1,9},{9,1},{17,25},{25,17},{2,10},{10... | collective-permute-start | bytes 1769480 | tf_op jit(solution)/shard_map/ppermute | solution.py:356
  32.4 3.3 %copy-start = (bf16[3,384,768]{2,1,0:T(8,128)(2,1)S(1)}, bf16[3,384,768]{2,1,0:T(8,128)(2,1)}, u32[]{:S(2)}) copy-start(bf16[3,384,768]{2,1,0:T(8,128)(2,1)} %tap.7) | copy-start | bytes 5308420
  33.3 2.5 %copy-start.3 = (bf16[768,384]{1,0:T(8,128)(2,1)S(1)}, bf16[768,384]{1,0:T(8,128)(2,1)}, u32[]{:S(2)}) copy-start(bf16[768,384]{1,0:T(8,128)(2,1)} %out.5) | copy-start | bytes 1769476
  33.6 11.9 %collective-permute-start.8 = (bf16[2,480,384]{2,1,0:T(8,128)(2,1)S(1)}, bf16[2,480,384]{2,1,0:T(8,128)(2,1)S(1)}, u32[]{:S(2)}, u32[]{:S(2)}) collective-permute-start(bf16[2,480,384]{2,1,0:T(8,128)(2,1)S(1)} %shard_map.63.refs_3_), channel_id=1, source_target_pairs={{0,1},{1,0},{2,3},{3,2},{4,5},{5,4},{6,7},{7,6},{8,9},{9,8},{10,11... | collective-permute-start | bytes 2211848 | tf_op jit(solution)/shard_map/ppermute | solution.py:353
  33.7 9.7 %collective-permute-start.6 = (bf16[384,384]{1,0:T(8,128)(2,1)S(1)}, bf16[384,384]{1,0:T(8,128)(2,1)S(1)}, u32[]{:S(2)}, u32[]{:S(2)}) collective-permute-start(bf16[384,384]{1,0:T(8,128)(2,1)S(1)} %collective-permute-done.5.first), channel_id=1, source_target_pairs={{0,2},{1,5},{2,0},{3,7},{4,6},{5,1},{6,4},{7,3},{8,10},{9,13},{10,... | collective-permute-start | bytes 884744 | tf_op jit(solution)/shard_map/ppermute | solution.py:353
  35.3 12.6 %collective-permute-start.13 = (bf16[2,480,384]{2,1,0:T(8,128)(2,1)S(1)}, bf16[2,480,384]{2,1,0:T(8,128)(2,1)S(1)}, u32[]{:S(2)}, u32[]{:S(2)}) collective-permute-start(bf16[2,480,384]{2,1,0:T(8,128)(2,1)S(1)} %shard_map.63.refs_3_), channel_id=1, source_target_pairs={{0,4},{1,3},{2,6},{3,1},{4,0},{5,7},{6,2},{7,5},{8,12},{9,11},{10,... | collective-permute-start | bytes 2211848 | tf_op jit(solution)/shard_map/ppermute | solution.py:353
  43.5 7.2 %collective-permute-start.10 = (bf16[2,384,384]{2,1,0:T(8,128)(2,1)S(1)}, bf16[2,384,384]{2,1,0:T(8,128)(2,1)S(1)}, u32[]{:S(2)}, u32[]{:S(2)}) collective-permute-start(bf16[2,384,384]{2,1,0:T(8,128)(2,1)S(1)} %shard_map.65.refs_3_), channel_id=1, source_target_pairs={{0,1},{1,0},{2,3},{3,2},{4,5},{5,4},{6,7},{7,6},{8,9},{9,8},{10,11... | collective-permute-start | bytes 1769480 | tf_op jit(solution)/shard_map/ppermute | solution.py:353
  44.0 8.1 %collective-permute-start.12 = (bf16[2,384,384]{2,1,0:T(8,128)(2,1)S(1)}, bf16[2,384,384]{2,1,0:T(8,128)(2,1)S(1)}, u32[]{:S(2)}, u32[]{:S(2)}) collective-permute-start(bf16[2,384,384]{2,1,0:T(8,128)(2,1)S(1)} %collective-permute-done.11.refs_3_), channel_id=1, source_target_pairs={{0,1},{1,0},{2,3},{3,2},{4,5},{5,4},{6,7},{7,6},{8,9},{9,8},{10,11... | collective-permute-start | bytes 1769480 | tf_op jit(solution)/shard_map/ppermute | solution.py:353
  44.1 10.1 %collective-permute-start.7 = (bf16[2,384,384]{2,1,0:T(8,128)(2,1)S(1)}, bf16[2,384,384]{2,1,0:T(8,128)(2,1)S(1)}, u32[]{:S(2)}, u32[]{:S(2)}) collective-permute-start(bf16[2,384,384]{2,1,0:T(8,128)(2,1)S(1)} %shard_map.65.refs_3_), channel_id=1, source_target_pairs={{0,4},{1,3},{2,6},{3,1},{4,0},{5,7},{6,2},{7,5},{8,12},{9,11},{10,... | collective-permute-start | bytes 1769480 | tf_op jit(solution)/shard_map/ppermute | solution.py:353
  45.5 4.4 %collective-permute-start.9 = (bf16[1,480,384]{2,1,0:T(8,128)(2,1)S(1)}, bf16[1,480,384]{2,1,0:T(8,128)(2,1)S(1)}, u32[]{:S(2)}, u32[]{:S(2)}) collective-permute-start(bf16[1,480,384]{2,1,0:T(8,128)(2,1)S(1)} %collective-permute-done.1.first.refs_3_), channel_id=1, source_target_pairs={{0,1},{1,0},{2,3},{3,2},{4,5},{5,4},{6,7},{7,6},{8,9},{9,8},{10,11... | collective-permute-start | bytes 1105928 | tf_op jit(solution)/shard_map/ppermute | solution.py:353
  47.8 6.7 %collective-permute-start.14 = (bf16[2,480,384]{2,1,0:T(8,128)(2,1)S(1)}, bf16[2,480,384]{2,1,0:T(8,128)(2,1)S(1)}, u32[]{:S(2)}, u32[]{:S(2)}) collective-permute-start(bf16[2,480,384]{2,1,0:T(8,128)(2,1)S(1)} %collective-permute-done.13.refs_3_), channel_id=1, source_target_pairs={{0,1},{1,0},{2,3},{3,2},{4,5},{5,4},{6,7},{7,6},{8,9},{9,8},{10,11... | collective-permute-start | bytes 2211848 | tf_op jit(solution)/shard_map/ppermute | solution.py:353
  54.2 3.3 %collective-permute-start.15 = (bf16[2,384,384]{2,1,0:T(8,128)(2,1)S(1)}, bf16[2,384,384]{2,1,0:T(8,128)(2,1)S(1)}, u32[]{:S(2)}, u32[]{:S(2)}) collective-permute-start(bf16[2,384,384]{2,1,0:T(8,128)(2,1)S(1)} %collective-permute-done.7.refs_2_), channel_id=1, source_target_pairs={{0,1},{1,0},{2,3},{3,2},{4,5},{5,4},{6,7},{7,6},{8,9},{9,8},{10,11... | collective-permute-start | bytes 1769480 | tf_op jit(solution)/shard_map/ppermute | solution.py:353

commit v5 on v4

--- a/solution.py
+++ b/solution.py
@@ -66,44 +66,54 @@
     return [(q // 2, mine % 2, q) for q in pair]
 
 
-def prepare_kernel(signal, cot, tap, out, piece, first, to_next, to_previous, stage, sem, sems):
+def prepare_kernel(tap, out, piece, first, stage, sem, sems):
     s = lax.axis_index("seq") % PLANE
     matrix, half = s // 2, s % 2
     size = piece.shape[0]
-    rows = signal.shape[1]
-    step = DILATION_STEP
     part = pl.ds(pl.multiple_of(half * size, 128), size)
     eighth = pl.ds(pl.multiple_of(s * (size // PLANE), 16), size // PLANE)
     copies = [
         (tap.at[1, :, part], first.at[0, 0:size]),
         (tap.at[0, eighth, 0:size], first.at[0, pl.ds(size, size // PLANE)]),
         (tap.at[0, eighth, size : 2 * size], first.at[0, pl.ds(size + size // PLANE, size // PLANE)]),
+    ]
+    copies = [pltpu.make_async_copy(a, b, sems.at[n]) for n, (a, b) in enumerate(copies)]
+
+    @pl.when(matrix < 3)
+    def _():
+        copy = pltpu.make_async_copy(tap.at[matrix, :, part], piece, sem)
+        copy.start()
+        for other in copies:
+            other.start()
+        copy.wait()
+
+    @pl.when(matrix == 3)
+    def _():
+        copy = pltpu.make_async_copy(out.at[part, :], stage, sem)
+        copy.start()
+        for other in copies:
+            other.start()
+        copy.wait()
+        piece[...] = stage[...].T
+
+    for other in copies:
+        other.wait()
+
+
+def bins_kernel(signal, cot, after, to_next, to_previous, sems):
+    rows = signal.shape[1]
+    step = DILATION_STEP
+    copies = [
         (signal.at[:, rows - 2 * step :], to_next.at[:, 0 : 2 * step]),
         (cot.at[:, rows - step :], to_next.at[:, 2 * step :]),
         (cot.at[:, 0:step], to_previous.at[:, 0:step]),
         (signal.at[:, 0 : 2 * step], to_previous.at[:, step:]),
     ]
     copies = [pltpu.make_async_copy(a, b, sems.at[n]) for n, (a, b) in enumerate(copies)]
-
-    @pl.when(matrix < 3)
-    def _():
-        copy = pltpu.make_async_copy(tap.at[matrix, :, part], piece, sem)
-        copy.start()
-        for other in copies:
-            other.start()
-        copy.wait()
-
-    @pl.when(matrix == 3)
-    def _():
-        copy = pltpu.make_async_copy(out.at[part, :], stage, sem)
-        copy.start()
-        for other in copies:
-            other.start()
-        copy.wait()
-        piece[...] = stage[...].T
-
-    for other in copies:
-        other.wait()
+    for copy in copies:
+        copy.start()
+    for copy in copies:
+        copy.wait()
 
 
 def half_kernel(tap, out, last, stage, sems):
@@ -331,23 +341,29 @@
 
     reach = 2 * DILATION_STEP
     edge = jax.ShapeDtypeStruct((windows, reach + DILATION_STEP, channels), BF16)
-    mine, first, low, high = pl.pallas_call(
+    mine, first = pl.pallas_call(
         prepare_kernel,
         out_shape=[
             jax.ShapeDtypeStruct((width, width), BF16),
             jax.ShapeDtypeStruct((1, width + 2 * (width // PLANE), width), BF16),
-            edge,
-            edge,
         ],
-        in_specs=[hbm] * 4,
-        out_specs=[vmem] * 4,
+        in_specs=[hbm] * 2,
+        out_specs=[vmem] * 2,
         scratch_shapes=[
             pltpu.VMEM((width, width), BF16),
             pltpu.SemaphoreType.DMA,
-            pltpu.SemaphoreType.DMA((7,)),
+            pltpu.SemaphoreType.DMA((3,)),
         ],
         compiler_params=params(8),
-    )(stay(signal), stay(cot), stay(tap), stay(out))
+    )(stay(tap), stay(out))
+    low, high = pl.pallas_call(
+        bins_kernel,
+        out_shape=[edge, edge],
+        in_specs=[hbm] * 3,
+        out_specs=[vmem] * 2,
+        scratch_shapes=[pltpu.SemaphoreType.DMA((4,))],
+        compiler_params=params(4),
+    )(stay(signal), stay(cot), mine)
 
     def across(block, even, odd):
         return lax.ppermute(block, "seq", plane_pairs(count, even, odd))
@@ -447,18 +463,25 @@
     near3 = across(p3, 2, 4)
     last = over(last, 1)
     far_mate2 = across(far2, 1, 1)
+    sums, whole1 = add_slot(1, ("first", "mate_first"), (first, mate_first), left, sums)
+    near3, *sums = tie(near3, *sums)
     own3 = pair(p3, near3)
-    own3, *sums = tie(own3, *sums)
     far3 = across(own3, 4, 2)
     mate3 = across(own3, 1, 1)
     mate_last = across(last, 1, 1)
     sums, whole2, pair_tap = add_slot(2, near_names, (own2, mate2), left, sums, carries=True)
-    sums, whole1 = add_slot(1, ("first", "mate_first"), (first, mate_first), left, sums)
     sums, whole3 = add_slot(3, near_names, (own3, mate3), left, sums)
     sums, whole1 = add_slot(1, ("last", "mate_last"), (last, mate_last), left, sums, whole1)
+    (own_sums,), whole2, pair_tap = add_slot(
+        2, ("far",), (far2,), left, sums[:1], whole2, pair_tap, carries=True
+    )
+    sums = [own_sums, sums[1]]
     far3, *sums = tie(far3, *sums)
     far_mate3 = across(far3, 1, 1)
-    sums, whole2, pair_tap = add_slot(2, far_names, (far2, far_mate2), left, sums, whole2, pair_tap, carries=True)
+    (mate_sums,), whole2, pair_tap = add_slot(
+        2, ("mate_far",), (far_mate2,), left, sums[1:], whole2, pair_tap, carries=True
+    )
+    sums = [sums[0], mate_sums]
     sums = pl.pallas_call(
         tap_kernel,
         out_shape=[side_shape] * 2,

time: 63 us -> 60.1 us (0.954)
  waiting for transfers between devices: 21.5 us -> 18.5 us
  starting transfers between devices: 20.4 us -> 19.4 us
  Pallas kernels: 19.9 us -> 20.8 us
    ppermute x10, waiting for transfers between devices: 7.84 us -> 4.2 us  [across(): return lax.ppermute(block, 'seq', plane_pairs(count, even, odd))]
    pallas_call x0 -> x1, Pallas kernels: none -> 1.3 us  [per_device(): pl.pallas_call(bins_kernel, out_shape=[edge, edge], in_specs=[hbm] * 3, o...]
    ppermute x10, starting transfers between devices: 7.75 us -> 6.63 us  [across(): return lax.ppermute(block, 'seq', plane_pairs(count, even, odd))]
    pallas_call x7 -> x8, Pallas kernels: 7.82 us -> 7.96 us  [add_slot(): pl.pallas_call(functools.partial(slot_kernel, slot, names, sides, not who...]
  transfers between devices with their start and end apart: 16 -> 16, of which waited for: 7 -> 7; matrix products, arithmetic and copies ran while one was open for 0% -> 0% of each run, Pallas kernels for 21% -> 24%
where the time goes in v5:
time: 60.1 us; the launch traced here: 59.8 us
  Pallas kernels  20.8 us (35%)
  starting transfers between devices  19.4 us (32%)
  waiting for transfers between devices  18.5 us (31%)
  between operations  1.06 us (2%)
    ppermute x4, waiting for transfers between devices, over(): return lax.ppermute(block, 'dp', [(i, i ^ bits) for i in range(4)])  14.3 us
    ppermute x4, starting transfers between devices, over(): return lax.ppermute(block, 'dp', [(i, i ^ bits) for i in range(4)])  10.2 us
    pallas_call x8, Pallas kernels, add_slot(): pl.pallas_call(functools.partial(slot_kernel, slot, names, sides, not who...  7.96 us
    ppermute x10, starting transfers between devices, across(): return lax.ppermute(block, 'seq', plane_pairs(count, even, odd))  6.63 us
    ppermute x10, waiting for transfers between devices, across(): return lax.ppermute(block, 'seq', plane_pairs(count, even, odd))  4.2 us
    pallas_call x1, Pallas kernels, per_device(): pl.pallas_call(back_kernel, out_shape=[jax.ShapeDtypeStruct(signal.shape,...  3.54 us
    pallas_call x1, Pallas kernels, per_device(): pl.pallas_call(own_kernel, out_shape=[side_shape] * 2 + [tap_shape], in_s...  1.64 us
    ppermute x1, starting transfers between devices, per_device(): low = lax.ppermute(low, 'seq', [(i, i + 1) for i in range(count - 1)])  1.33 us
  transfers between devices with their start and end apart: 16, of which 7 were waited for; matrix products, arithmetic and copies ran while one was open for 0% of the time, Pallas kernels for 24%

profile of v5, /device:TPU:0, one launch (start us, length us, event | category | flops | bytes accessed | tf_op | source)
XLA Modules:
  0.0 59.8 jit_solution(5669491984992705856)
XLA Ops:
  0.6 1.1 %shard_map.60 = (bf16[384,384]{1,0:T(8,128)(2,1)S(1)}, bf16[1,480,384]{2,1,0:T(8,128)(2,1)S(1)}) custom-call(bf16[3,384,768]{2,1,0:T(8,128)(2,1)} %tap.7, bf16[768,384]{1,0:T(8,128)(2,1)} %out.5), custom_call_target="tpu_custom_call" | custom-call | tf_op jit(solution)/shard_map/pallas_call | solution.py:344
  1.8 3.1 %collective-permute-start.1 = (bf16[1,480,384]{2,1,0:T(8,128)(2,1)S(1)}, bf16[1,480,384]{2,1,0:T(8,128)(2,1)S(1)}, u32[]{:S(2)}, u32[]{:S(2)}) collective-permute-start(bf16[1,480,384]{2,1,0:T(8,128)(2,1)S(1)} %get-tuple-element.52), channel_id=1, source_target_pairs={{0,8},{8,0},{16,24},{24,16},{1,9},{9,1},{17,25},{25,17},{2,10},{10... | collective-permute-start | bytes 1105928 | tf_op jit(solution)/shard_map/ppermute | solution.py:372
  4.9 2.6 %collective-permute-start = (bf16[384,384]{1,0:T(8,128)(2,1)S(1)}, bf16[384,384]{1,0:T(8,128)(2,1)S(1)}, u32[]{:S(2)}, u32[]{:S(2)}) collective-permute-start(bf16[384,384]{1,0:T(8,128)(2,1)S(1)} %get-tuple-element.51.after), channel_id=1, source_target_pairs={{0,16},{8,24},{16,0},{24,8},{1,17},{9,25},{17,1},{25,9},{2,18},{10... | collective-permute-start | bytes 884744 | tf_op jit(solution)/shard_map/ppermute | solution.py:372
  7.5 1.3 %shard_map.64 = (bf16[2,96,1536]{2,1,0:T(8,128)(2,1)S(1)}, bf16[2,96,1536]{2,1,0:T(8,128)(2,1)S(1)}) custom-call(bf16[2,128,1536]{2,1,0:T(8,128)(2,1)} %signal.5, bf16[2,128,1536]{2,1,0:T(8,128)(2,1)} %cot.5, bf16[384,384]{1,0:T(8,128)(2,1)S(1)} %get-tuple-element.51.after), custom_call_target="tpu_custom_call" | custom-call | tf_op jit(solution)/shard_map/pallas_call | solution.py:359
  8.8 1.3 %collective-permute-start.3 = (bf16[2,96,1536]{2,1,0:T(8,128)(2,1)S(1)}, bf16[2,96,1536]{2,1,0:T(8,128)(2,1)S(1)}, u32[]{:S(2)}, u32[]{:S(2)}) collective-permute-start(bf16[2,96,1536]{2,1,0:T(8,128)(2,1)S(1)} %get-tuple-element.56), channel_id=1, source_target_pairs={{0,1},{1,2},{2,3},{3,4},{4,5},{5,6},{6,7},{8,9},{9,10},{10,11},{11... | collective-permute-start | bytes 1769480 | tf_op jit(solution)/shard_map/ppermute | solution.py:414
  10.1 1.3 %collective-permute-start.4 = (bf16[2,96,1536]{2,1,0:T(8,128)(2,1)S(1)}, bf16[2,96,1536]{2,1,0:T(8,128)(2,1)S(1)}, u32[]{:S(2)}, u32[]{:S(2)}) collective-permute-start(bf16[2,96,1536]{2,1,0:T(8,128)(2,1)S(1)} %get-tuple-element.57), channel_id=1, source_target_pairs={{1,0},{2,1},{3,2},{4,3},{5,4},{6,5},{7,6},{9,8},{10,9},{11,10},{12... | collective-permute-start | bytes 1769480 | tf_op jit(solution)/shard_map/ppermute | solution.py:415
  11.4 1.1 %shard_map.59 = (bf16[2,2,256,1536]{3,2,1,0:T(8,128)(2,1)S(1)}, f32[2,128,1536]{2,1,0:T(8,128)S(1)}) custom-call(bf16[2,128,1536]{2,1,0:T(8,128)(2,1)S(1)} %copy-done.1, bf16[2,128,1536]{2,1,0:T(8,128)(2,1)S(1)} %copy-done.2), custom_call_target="tpu_custom_call" | custom-call | flops 1000 | bytes 1000 | tf_op jit(solution)/shard_map/pallas_call | solution.py:417
  12.5 1.1 %shard_map.61 = bf16[2,384,384]{2,1,0:T(8,128)(2,1)S(1)} custom-call(bf16[3,384,768]{2,1,0:T(8,128)(2,1)} %tap.7, bf16[768,384]{1,0:T(8,128)(2,1)} %out.5), custom_call_target="tpu_custom_call" | custom-call | flops 1000 | bytes 1000 | tf_op jit(solution)/shard_map/pallas_call | solution.py:425
  13.7 5.4 %collective-permute-done.piece = bf16[384,384]{1,0:T(8,128)(2,1)S(1)} collective-permute-done((bf16[384,384]{1,0:T(8,128)(2,1)S(1)}, bf16[384,384]{1,0:T(8,128)(2,1)S(1)}, u32[]{:S(2)}, u32[]{:S(2)}) %collective-permute-start) | collective-permute-done | bytes 294944 | tf_op jit(solution)/shard_map/ppermute | solution.py:372
  19.8 2.8 %collective-permute-start.5 = (bf16[384,384]{1,0:T(8,128)(2,1)S(1)}, bf16[384,384]{1,0:T(8,128)(2,1)S(1)}, u32[]{:S(2)}, u32[]{:S(2)}) collective-permute-start(bf16[384,384]{1,0:T(8,128)(2,1)S(1)} %collective-permute-done.piece), channel_id=1, source_target_pairs={{0,8},{8,0},{16,24},{24,16},{1,9},{9,1},{17,25},{25,17},{2,10},{10... | collective-permute-start | bytes 884744 | tf_op jit(solution)/shard_map/ppermute | solution.py:372
  22.7 1.6 %collective-permute-start.2 = (bf16[480,384]{1,0:T(8,128)(2,1)S(1)}, bf16[480,384]{1,0:T(8,128)(2,1)S(1)}, u32[]{:S(2)}, u32[]{:S(2)}) collective-permute-start(bf16[480,384]{1,0:T(8,128)(2,1)S(1)} %shard_map.62.first), channel_id=1, source_target_pairs={{0,2},{1,5},{2,0},{3,7},{4,6},{5,1},{6,4},{7,3},{8,10},{9,13},{10,... | collective-permute-start | bytes 1105928 | tf_op jit(solution)/shard_map/ppermute | solution.py:369
  24.3 4.4 %collective-permute-done.5.first = bf16[384,384]{1,0:T(8,128)(2,1)S(1)} collective-permute-done((bf16[384,384]{1,0:T(8,128)(2,1)S(1)}, bf16[384,384]{1,0:T(8,128)(2,1)S(1)}, u32[]{:S(2)}, u32[]{:S(2)}) %collective-permute-start.5) | collective-permute-done | bytes 294944 | tf_op jit(solution)/shard_map/ppermute | solution.py:372
  28.7 1.7 %collective-permute-start.11 = (bf16[2,384,384]{2,1,0:T(8,128)(2,1)S(1)}, bf16[2,384,384]{2,1,0:T(8,128)(2,1)S(1)}, u32[]{:S(2)}, u32[]{:S(2)}) collective-permute-start(bf16[2,384,384]{2,1,0:T(8,128)(2,1)S(1)} %shard_map.61), channel_id=1, source_target_pairs={{0,8},{8,0},{16,24},{24,16},{1,9},{9,1},{17,25},{25,17},{2,10},{10... | collective-permute-start | bytes 1769480 | tf_op jit(solution)/shard_map/ppermute | solution.py:372
  30.4 1.5 %collective-permute-start.6 = (bf16[384,384]{1,0:T(8,128)(2,1)S(1)}, bf16[384,384]{1,0:T(8,128)(2,1)S(1)}, u32[]{:S(2)}, u32[]{:S(2)}) collective-permute-start(bf16[384,384]{1,0:T(8,128)(2,1)S(1)} %collective-permute-done.5.first), channel_id=1, source_target_pairs={{0,2},{1,5},{2,0},{3,7},{4,6},{5,1},{6,4},{7,3},{8,10},{9,13},{10,... | collective-permute-start | bytes 884744 | tf_op jit(solution)/shard_map/ppermute | solution.py:369
  33.1 1.7 %collective-permute-start.13 = (bf16[2,480,384]{2,1,0:T(8,128)(2,1)S(1)}, bf16[2,480,384]{2,1,0:T(8,128)(2,1)S(1)}, u32[]{:S(2)}, u32[]{:S(2)}) collective-permute-start(bf16[2,480,384]{2,1,0:T(8,128)(2,1)S(1)} %shard_map.63.refs_3_), channel_id=1, source_target_pairs={{0,4},{1,3},{2,6},{3,1},{4,0},{5,7},{6,2},{7,5},{8,12},{9,11},{10,... | collective-permute-start | bytes 2211848 | tf_op jit(solution)/shard_map/ppermute | solution.py:369
  34.8 1.6 %shard_map.66 = (f32[2,384,384]{2,1,0:T(8,128)S(1)}, f32[2,384,384]{2,1,0:T(8,128)S(1)}, bf16[384,768]{1,0:T(8,128)(2,1)S(1)}) custom-call(bf16[2,2,256,1536]{3,2,1,0:T(8,128)(2,1)S(1)} %shard_map.65.left.refs_0_, bf16[3,384,768]{2,1,0:T(8,128)(2,1)S(1)} %copy-done, bf16[768,384]{1,0:T(8,128)(2,1)S(1)} %copy-done.3), custom_call_target="tpu_custom_call" | custom-call | flops 1000 | bytes 1000 | tf_op jit(solution)/shard_map/pallas_call | solution.py:448
  38.5 3.8 %collective-permute-done.11.refs_3_ = bf16[2,384,384]{2,1,0:T(8,128)(2,1)S(1)} collective-permute-done((bf16[2,384,384]{2,1,0:T(8,128)(2,1)S(1)}, bf16[2,384,384]{2,1,0:T(8,128)(2,1)S(1)}, u32[]{:S(2)}, u32[]{:S(2)}) %collective-permute-start.11) | collective-permute-done | bytes 589856 | tf_op jit(solution)/shard_map/ppermute | solution.py:372
  42.2 1.5 %collective-permute-start.8 = (bf16[2,384,384]{2,1,0:T(8,128)(2,1)S(1)}, bf16[2,384,384]{2,1,0:T(8,128)(2,1)S(1)}, u32[]{:S(2)}, u32[]{:S(2)}) collective-permute-start(bf16[2,384,384]{2,1,0:T(8,128)(2,1)S(1)} %shard_map.68.refs_3_), channel_id=1, source_target_pairs={{0,4},{1,3},{2,6},{3,1},{4,0},{5,7},{6,2},{7,5},{8,12},{9,11},{10,... | collective-permute-start | bytes 1769480 | tf_op jit(solution)/shard_map/ppermute | solution.py:369
  44.9 1.4 %shard_map.69 = (f32[2,384,384]{2,1,0:T(8,128)S(1)}, f32[2,384,384]{2,1,0:T(8,128)S(1)}, bf16[4,384,768]{2,1,0:T(8,128)(2,1)S(1)}, bf16[384,768]{1,0:T(8,128)(2,1)S(1)}) custom-call(bf16[2,2,256,1536]{3,2,1,0:T(8,128)(2,1)S(1)} %shard_map.65.left.refs_0_, ...), custom_call_target="tpu_custom_call", output_to_operand_aliasing={{0}: (1, {}), {1}: (2, {})} | custom-call | flops 1000 | bytes 1000 | tf_op jit(solution)/shard_map/pallas_call | solution.py:400
  46.3 1.3 %shard_map.70 = (f32[2,384,384]{2,1,0:T(8,128)S(1)}, f32[2,384,384]{2,1,0:T(8,128)S(1)}, bf16[4,384,768]{2,1,0:T(8,128)(2,1)S(1)}) custom-call(bf16[2,2,256,1536]{3,2,1,0:T(8,128)(2,1)S(1)} %shard_map.65.left.refs_0_, f32[2,384,384]{2,1,0:T(8,128)S(1)} %get-tuple-element.70.refs_1_, ...), custom_call_target="tpu_custom_call", output_to_operand_aliasing={{0}: (1, {}), {1}: (2, {})} | custom-call | flops 1000 | bytes 1000 | tf_op jit(solution)/shard_map/pallas_call | solution.py:400
  47.6 1.3 %shard_map.71 = (f32[2,384,384]{2,1,0:T(8,128)S(1)}, f32[2,384,384]{2,1,0:T(8,128)S(1)}, bf16[4,384,768]{2,1,0:T(8,128)(2,1)S(1)}) custom-call(bf16[2,2,256,1536]{3,2,1,0:T(8,128)(2,1)S(1)} %shard_map.65.left.refs_0_, f32[2,384,384]{2,1,0:T(8,128)S(1)} %get-tuple-element.72.refs_1_, ...), custom_call_target="tpu_custom_call", output_to_operand_aliasing={{0}: (1, {}), {1}: (2, {}), {2}: (5, {})} | custom-call | flops 1000 | bytes 1000 | tf_op jit(solution)/shard_map/pallas_call | solution.py:400
  49.7 2.4 %collective-permute-done.8.refs_2_ = bf16[2,384,384]{2,1,0:T(8,128)(2,1)S(1)} collective-permute-done((bf16[2,384,384]{2,1,0:T(8,128)(2,1)S(1)}, bf16[2,384,384]{2,1,0:T(8,128)(2,1)S(1)}, u32[]{:S(2)}, u32[]{:S(2)}) %collective-permute-start.8) | collective-permute-done | bytes 589856 | tf_op jit(solution)/shard_map/ppermute | solution.py:369
  54.4 0.9 %shard_map.76 = (f32[2,384,384]{2,1,0:T(8,128)S(1)}, bf16[4,384,768]{2,1,0:T(8,128)(2,1)S(1)}) custom-call(bf16[2,2,256,1536]{3,2,1,0:T(8,128)(2,1)S(1)} %shard_map.65.left.refs_0_, f32[2,384,384]{2,1,0:T(8,128)S(1)} %get-tuple-element.91.refs_1_, ...), custom_call_target="tpu_custom_call", output_to_operand_aliasing={{0}: (1, {}), {1}: (3, {})} | custom-call | flops 1000 | bytes 1000 | tf_op jit(solution)/shard_map/pallas_call | solution.py:400
  56.1 3.5 %shard_map.78 = (bf16[2,128,1536]{2,1,0:T(8,128)(2,1)}, bf16[2,128,1536]{2,1,0:T(8,128)(2,1)}) custom-call(bf16[2,128,1536]{2,1,0:T(8,128)(2,1)S(1)} %copy-done.1, bf16[2,128,1536]{2,1,0:T(8,128)(2,1)S(1)} %copy-done.2, f32[2,128,1536]{2,1,0:T(8,128)S(1)} %get-tuple-element.50.slope, bf16[2,2,192,768]{3,2,1,0:T(8,128)(2,1)S(1)} %shard_map.77.right, ...), custom_call_target="tpu_custom_call" | custom-call | flops 1000 | bytes 1000 | tf_op jit(solution)/shard_map/pallas_call | solution.py:505
  (36 shorter events, 9.0 us)
Async XLA Ops:
  1.8 9.6 %copy-start.1 = (bf16[2,128,1536]{2,1,0:T(8,128)(2,1)S(1)}, bf16[2,128,1536]{2,1,0:T(8,128)(2,1)}, u32[]{:S(2)}) copy-start(bf16[2,128,1536]{2,1,0:T(8,128)(2,1)} %signal.5) | copy-start | bytes 2359300
  1.8 9.6 %copy-start.2 = (bf16[2,128,1536]{2,1,0:T(8,128)(2,1)S(1)}, bf16[2,128,1536]{2,1,0:T(8,128)(2,1)}, u32[]{:S(2)}) copy-start(bf16[2,128,1536]{2,1,0:T(8,128)(2,1)} %cot.5) | copy-start | bytes 2359300
  1.8 18.0 %collective-permute-start.1 = (bf16[1,480,384]{2,1,0:T(8,128)(2,1)S(1)}, bf16[1,480,384]{2,1,0:T(8,128)(2,1)S(1)}, u32[]{:S(2)}, u32[]{:S(2)}) collective-permute-start(bf16[1,480,384]{2,1,0:T(8,128)(2,1)S(1)} %get-tuple-element.52), channel_id=1, source_target_pairs={{0,8},{8,0},{16,24},{24,16},{1,9},{9,1},{17,25},{25,17},{2,10},{10... | collective-permute-start | bytes 1105928 | tf_op jit(solution)/shard_map/ppermute | solution.py:372
  4.9 14.2 %collective-permute-start = (bf16[384,384]{1,0:T(8,128)(2,1)S(1)}, bf16[384,384]{1,0:T(8,128)(2,1)S(1)}, u32[]{:S(2)}, u32[]{:S(2)}) collective-permute-start(bf16[384,384]{1,0:T(8,128)(2,1)S(1)} %get-tuple-element.51.after), channel_id=1, source_target_pairs={{0,16},{8,24},{16,0},{24,8},{1,17},{9,25},{17,1},{25,9},{2,18},{10... | collective-permute-start | bytes 884744 | tf_op jit(solution)/shard_map/ppermute | solution.py:372
  8.8 21.6 %collective-permute-start.3 = (bf16[2,96,1536]{2,1,0:T(8,128)(2,1)S(1)}, bf16[2,96,1536]{2,1,0:T(8,128)(2,1)S(1)}, u32[]{:S(2)}, u32[]{:S(2)}) collective-permute-start(bf16[2,96,1536]{2,1,0:T(8,128)(2,1)S(1)} %get-tuple-element.56), channel_id=1, source_target_pairs={{0,1},{1,2},{2,3},{3,4},{4,5},{5,6},{6,7},{8,9},{9,10},{10,11},{11... | collective-permute-start | bytes 1769480 | tf_op jit(solution)/shard_map/ppermute | solution.py:414
  10.1 21.8 %collective-permute-start.4 = (bf16[2,96,1536]{2,1,0:T(8,128)(2,1)S(1)}, bf16[2,96,1536]{2,1,0:T(8,128)(2,1)S(1)}, u32[]{:S(2)}, u32[]{:S(2)}) collective-permute-start(bf16[2,96,1536]{2,1,0:T(8,128)(2,1)S(1)} %get-tuple-element.57), channel_id=1, source_target_pairs={{1,0},{2,1},{3,2},{4,3},{5,4},{6,5},{7,6},{9,8},{10,9},{11,10},{12... | collective-permute-start | bytes 1769480 | tf_op jit(solution)/shard_map/ppermute | solution.py:415
  19.8 8.9 %collective-permute-start.5 = (bf16[384,384]{1,0:T(8,128)(2,1)S(1)}, bf16[384,384]{1,0:T(8,128)(2,1)S(1)}, u32[]{:S(2)}, u32[]{:S(2)}) collective-permute-start(bf16[384,384]{1,0:T(8,128)(2,1)S(1)} %collective-permute-done.piece), channel_id=1, source_target_pairs={{0,8},{8,0},{16,24},{24,16},{1,9},{9,1},{17,25},{25,17},{2,10},{10... | collective-permute-start | bytes 884744 | tf_op jit(solution)/shard_map/ppermute | solution.py:372
  22.7 10.0 %collective-permute-start.2 = (bf16[480,384]{1,0:T(8,128)(2,1)S(1)}, bf16[480,384]{1,0:T(8,128)(2,1)S(1)}, u32[]{:S(2)}, u32[]{:S(2)}) collective-permute-start(bf16[480,384]{1,0:T(8,128)(2,1)S(1)} %shard_map.62.first), channel_id=1, source_target_pairs={{0,2},{1,5},{2,0},{3,7},{4,6},{5,1},{6,4},{7,3},{8,10},{9,13},{10,... | collective-permute-start | bytes 1105928 | tf_op jit(solution)/shard_map/ppermute | solution.py:369
  28.7 13.6 %collective-permute-start.11 = (bf16[2,384,384]{2,1,0:T(8,128)(2,1)S(1)}, bf16[2,384,384]{2,1,0:T(8,128)(2,1)S(1)}, u32[]{:S(2)}, u32[]{:S(2)}) collective-permute-start(bf16[2,384,384]{2,1,0:T(8,128)(2,1)S(1)} %shard_map.61), channel_id=1, source_target_pairs={{0,8},{8,0},{16,24},{24,16},{1,9},{9,1},{17,25},{25,17},{2,10},{10... | collective-permute-start | bytes 1769480 | tf_op jit(solution)/shard_map/ppermute | solution.py:372
  30.4 6.1 %collective-permute-start.7 = (bf16[1,480,384]{2,1,0:T(8,128)(2,1)S(1)}, bf16[1,480,384]{2,1,0:T(8,128)(2,1)S(1)}, u32[]{:S(2)}, u32[]{:S(2)}) collective-permute-start(bf16[1,480,384]{2,1,0:T(8,128)(2,1)S(1)} %collective-permute-done.1.first.refs_3_), channel_id=1, source_target_pairs={{0,1},{1,0},{2,3},{3,2},{4,5},{5,4},{6,7},{7,6},{8,9},{9,8},{10,11... | collective-permute-start | bytes 1105928 | tf_op jit(solution)/shard_map/ppermute | solution.py:369
  30.4 7.8 %collective-permute-start.6 = (bf16[384,384]{1,0:T(8,128)(2,1)S(1)}, bf16[384,384]{1,0:T(8,128)(2,1)S(1)}, u32[]{:S(2)}, u32[]{:S(2)}) collective-permute-start(bf16[384,384]{1,0:T(8,128)(2,1)S(1)} %collective-permute-done.5.first), channel_id=1, source_target_pairs={{0,2},{1,5},{2,0},{3,7},{4,6},{5,1},{6,4},{7,3},{8,10},{9,13},{10,... | collective-permute-start | bytes 884744 | tf_op jit(solution)/shard_map/ppermute | solution.py:369
  31.9 2.9 %copy-start = (bf16[3,384,768]{2,1,0:T(8,128)(2,1)S(1)}, bf16[3,384,768]{2,1,0:T(8,128)(2,1)}, u32[]{:S(2)}) copy-start(bf16[3,384,768]{2,1,0:T(8,128)(2,1)} %tap.7) | copy-start | bytes 5308420
  32.7 2.1 %copy-start.3 = (bf16[768,384]{1,0:T(8,128)(2,1)S(1)}, bf16[768,384]{1,0:T(8,128)(2,1)}, u32[]{:S(2)}) copy-start(bf16[768,384]{1,0:T(8,128)(2,1)} %out.5) | copy-start | bytes 1769476
  33.1 11.5 %collective-permute-start.13 = (bf16[2,480,384]{2,1,0:T(8,128)(2,1)S(1)}, bf16[2,480,384]{2,1,0:T(8,128)(2,1)S(1)}, u32[]{:S(2)}, u32[]{:S(2)}) collective-permute-start(bf16[2,480,384]{2,1,0:T(8,128)(2,1)S(1)} %shard_map.63.refs_3_), channel_id=1, source_target_pairs={{0,4},{1,3},{2,6},{3,1},{4,0},{5,7},{6,2},{7,5},{8,12},{9,11},{10,... | collective-permute-start | bytes 2211848 | tf_op jit(solution)/shard_map/ppermute | solution.py:369
  34.8 10.0 %collective-permute-start.9 = (bf16[2,480,384]{2,1,0:T(8,128)(2,1)S(1)}, bf16[2,480,384]{2,1,0:T(8,128)(2,1)S(1)}, u32[]{:S(2)}, u32[]{:S(2)}) collective-permute-start(bf16[2,480,384]{2,1,0:T(8,128)(2,1)S(1)} %shard_map.63.refs_3_), channel_id=1, source_target_pairs={{0,1},{1,0},{2,3},{3,2},{4,5},{5,4},{6,7},{7,6},{8,9},{9,8},{10,11... | collective-permute-start | bytes 2211848 | tf_op jit(solution)/shard_map/ppermute | solution.py:369
  38.4 7.9 %collective-permute-start.10 = (bf16[2,384,384]{2,1,0:T(8,128)(2,1)S(1)}, bf16[2,384,384]{2,1,0:T(8,128)(2,1)S(1)}, u32[]{:S(2)}, u32[]{:S(2)}) collective-permute-start(bf16[2,384,384]{2,1,0:T(8,128)(2,1)S(1)} %shard_map.68.refs_3_), channel_id=1, source_target_pairs={{0,1},{1,0},{2,3},{3,2},{4,5},{5,4},{6,7},{7,6},{8,9},{9,8},{10,11... | collective-permute-start | bytes 1769480 | tf_op jit(solution)/shard_map/ppermute | solution.py:369
  42.2 5.3 %collective-permute-start.12 = (bf16[2,384,384]{2,1,0:T(8,128)(2,1)S(1)}, bf16[2,384,384]{2,1,0:T(8,128)(2,1)S(1)}, u32[]{:S(2)}, u32[]{:S(2)}) collective-permute-start(bf16[2,384,384]{2,1,0:T(8,128)(2,1)S(1)} %collective-permute-done.11.refs_3_), channel_id=1, source_target_pairs={{0,1},{1,0},{2,3},{3,2},{4,5},{5,4},{6,7},{7,6},{8,9},{9,8},{10,11... | collective-permute-start | bytes 1769480 | tf_op jit(solution)/shard_map/ppermute | solution.py:369
  42.2 9.9 %collective-permute-start.8 = (bf16[2,384,384]{2,1,0:T(8,128)(2,1)S(1)}, bf16[2,384,384]{2,1,0:T(8,128)(2,1)S(1)}, u32[]{:S(2)}, u32[]{:S(2)}) collective-permute-start(bf16[2,384,384]{2,1,0:T(8,128)(2,1)S(1)} %shard_map.68.refs_3_), channel_id=1, source_target_pairs={{0,4},{1,3},{2,6},{3,1},{4,0},{5,7},{6,2},{7,5},{8,12},{9,11},{10,... | collective-permute-start | bytes 1769480 | tf_op jit(solution)/shard_map/ppermute | solution.py:369
  44.6 7.5 %collective-permute-start.14 = (bf16[2,480,384]{2,1,0:T(8,128)(2,1)S(1)}, bf16[2,480,384]{2,1,0:T(8,128)(2,1)S(1)}, u32[]{:S(2)}, u32[]{:S(2)}) collective-permute-start(bf16[2,480,384]{2,1,0:T(8,128)(2,1)S(1)} %collective-permute-done.13.refs_2_), channel_id=1, source_target_pairs={{0,1},{1,0},{2,3},{3,2},{4,5},{5,4},{6,7},{7,6},{8,9},{9,8},{10,11... | collective-permute-start | bytes 2211848 | tf_op jit(solution)/shard_map/ppermute | solution.py:369
  52.1 2.3 %collective-permute-start.15 = (bf16[2,384,384]{2,1,0:T(8,128)(2,1)S(1)}, bf16[2,384,384]{2,1,0:T(8,128)(2,1)S(1)}, u32[]{:S(2)}, u32[]{:S(2)}) collective-permute-start(bf16[2,384,384]{2,1,0:T(8,128)(2,1)S(1)} %collective-permute-done.8.refs_2_), channel_id=1, source_target_pairs={{0,1},{1,0},{2,3},{3,2},{4,5},{5,4},{6,7},{7,6},{8,9},{9,8},{10,11... | collective-permute-start | bytes 1769480 | tf_op jit(solution)/shard_map/ppermute | solution.py:369

commit v6 on v5

--- a/solution.py
+++ b/solution.py
@@ -249,30 +249,36 @@
         copy.wait()
 
 
-def tap_kernel(left, tap, *sums):
-    rows = left.shape[2] - 2 * DILATION_STEP
-    size = tap.shape[0]
+def end_kernel(left, own, mate, buffer, pair_tap, whole_in, right, whole, sems):
+    windows, rows = right.shape[1:3]
+    size = buffer.shape[2]
     core = lax.axis_index("seq") % 2
+    pieces = held("mate_far")
+    copies = []
+    for i, (matrix, half, _) in enumerate(pieces):
+        part = pl.ds(pl.multiple_of(half * size, 128), size)
+        copies.append(pltpu.make_async_copy(buffer.at[i], whole.at[matrix, :, part], sems.at[i]))
+        copies[-1].start()
     lhs = rows_of(left, 0, 0, rows, slot_columns(1, size))
-    for side_in, side, half in zip(sums[:2], sums[2:], (core, 1 - core)):
-        part = pl.ds(pl.multiple_of(half * size, 128), size)
-        side[0] = side_in[0] + jnp.dot(lhs, tap[:, part], preferred_element_type=F32)
-        side[1] = side_in[1]
-
-
-def middle_kernel(own, mate, right):
-    windows, rows = right.shape[1:3]
-    size = own.shape[2]
-    core = lax.axis_index("seq") % 2
     for sums, half in ((own, core), (mate, 1 - core)):
         part = pl.ds(pl.multiple_of(half * size, 128), size)
-        v = sums[0]
+        totals = [sums[0] + jnp.dot(lhs, pair_tap[:, part], preferred_element_type=F32), sums[1]]
+        if sums is mate:
+            for i, (matrix, _, _) in enumerate(pieces):
+                offset = pl.multiple_of((matrix % 3) * DILATION_STEP, DILATION_STEP)
+                mine = rows_of(left, matrix // 3, offset, rows, slot_columns(3, size))
+                term = jnp.dot(mine, buffer[i], preferred_element_type=F32)
+                for which in range(2):
+                    totals[which] = totals[which] + jnp.where(matrix // 3 == which, term, 0.0)
+        v = totals[0]
         square = v * v
         t = jnp.tanh(ROOT * v * (1.0 + CUBIC * square))
         slope = 0.5 * (1.0 + t) + (0.5 * ROOT) * v * (1.0 - t * t) * (1.0 + 3.0 * CUBIC * square)
-        right[0, :, :, part] = (sums[1] * slope).astype(BF16).reshape(windows, rows, size)
+        right[0, :, :, part] = (totals[1] * slope).astype(BF16).reshape(windows, rows, size)
         active = (0.5 * v * (1.0 + t)).astype(BF16).reshape(windows, rows, size)
         right[1, :, 2 * DILATION_STEP :, part] = active[:, DILATION_STEP : rows - DILATION_STEP]
+    for copy in copies:
+        copy.wait()
 
 
 def back_kernel(signal, cot, slope, right, tap, out_t, pair_tap, *refs):
@@ -459,7 +465,7 @@
     own2, left = tie(own2, left)
     far2 = across(own2, 4, 2)
     mate2 = across(own2, 1, 1)
-    p3, last = tie(p3, last)
+    p3, last, _, _ = tie(p3, last, low, high)
     near3 = across(p3, 2, 4)
     last = over(last, 1)
     far_mate2 = across(far2, 1, 1)
@@ -471,37 +477,30 @@
     mate_last = across(last, 1, 1)
     sums, whole2, pair_tap = add_slot(2, near_names, (own2, mate2), left, sums, carries=True)
     sums, whole3 = add_slot(3, near_names, (own3, mate3), left, sums)
-    sums, whole1 = add_slot(1, ("last", "mate_last"), (last, mate_last), left, sums, whole1)
     (own_sums,), whole2, pair_tap = add_slot(
         2, ("far",), (far2,), left, sums[:1], whole2, pair_tap, carries=True
     )
     sums = [own_sums, sums[1]]
-    far3, *sums = tie(far3, *sums)
+    far3, mate_last, *sums = tie(far3, mate_last, *sums)
+    (own_sums,), whole3 = add_slot(3, ("far",), (far3,), left, sums[:1], whole3)
+    far3, own_sums = tie(far3, own_sums)
     far_mate3 = across(far3, 1, 1)
+    sums = [own_sums, sums[1]]
+    sums, whole1 = add_slot(1, ("last", "mate_last"), (last, mate_last), left, sums, whole1)
     (mate_sums,), whole2, pair_tap = add_slot(
         2, ("mate_far",), (far_mate2,), left, sums[1:], whole2, pair_tap, carries=True
     )
     sums = [sums[0], mate_sums]
-    sums = pl.pallas_call(
-        tap_kernel,
-        out_shape=[side_shape] * 2,
-        in_specs=[vmem] * 4,
-        out_specs=[vmem] * 2,
-        input_output_aliases={2: 0, 3: 1},
+    right, whole3 = pl.pallas_call(
+        end_kernel,
+        out_shape=[jax.ShapeDtypeStruct((2, windows, wide_rows, hidden), BF16), whole_shape],
+        in_specs=[vmem] * 5 + [hbm],
+        out_specs=[vmem, hbm],
+        scratch_shapes=[pltpu.SemaphoreType.DMA((2,))],
+        input_output_aliases={5: 1},
         compiler_params=params(4),
-        cost_estimate=cost(0.5),
-    )(left, pair_tap, *sums)
-    (own_sums,), whole3 = add_slot(3, ("far",), (far3,), left, sums[:1], whole3)
-    (mate_sums,), whole3 = add_slot(3, ("mate_far",), (far_mate3,), left, sums[1:], whole3)
-
-    right = pl.pallas_call(
-        middle_kernel,
-        out_shape=jax.ShapeDtypeStruct((2, windows, wide_rows, hidden), BF16),
-        in_specs=[vmem] * 2,
-        out_specs=vmem,
-        compiler_params=params(4),
-        cost_estimate=cost(0.8),
-    )(own_sums, mate_sums)
+        cost_estimate=cost(1.6),
+    )(left, sums[0], sums[1], far_mate3, pair_tap, whole3)
     result, grad_signal = pl.pallas_call(
         back_kernel,
         out_shape=[jax.ShapeDtypeStruct(signal.shape, BF16)] * 2,

time: 60.1 us -> 59.8 us (level)
  starting transfers between devices: 19.4 us -> 21.2 us
  waiting for transfers between devices: 18.5 us -> 17.2 us
    ppermute x4, waiting for transfers between devices: 14.3 us -> 12 us  [over(): return lax.ppermute(block, 'dp', [(i, i ^ bits) for i in range(4)])]
    ppermute x10, starting transfers between devices: 6.63 us -> 8.41 us  [across(): return lax.ppermute(block, 'seq', plane_pairs(count, even, odd))]
    ppermute x10, waiting for transfers between devices: 4.2 us -> 5.18 us  [across(): return lax.ppermute(block, 'seq', plane_pairs(count, even, odd))]
    pallas_call x8 -> x7, Pallas kernels: 7.96 us -> 7.03 us  [add_slot(): pl.pallas_call(functools.partial(slot_kernel, slot, names, sides, not who...]
    pallas_call x2 -> x1, Pallas kernels: 1.55 us -> 1.86 us  [per_device(): pl.pallas_call(end_kernel, out_shape=[jax.ShapeDtypeStruct((2, windows, w...]
  transfers between devices with their start and end apart: 16 -> 16, of which waited for: 7 -> 7; matrix products, arithmetic and copies ran while one was open for 0% -> 0% of each run, Pallas kernels for 24% -> 23%
where the time goes in v6:
time: 59.8 us; the launch traced here: 59.6 us
  starting transfers between devices  21.2 us (35%)
  Pallas kernels  20.2 us (34%)
  waiting for transfers between devices  17.2 us (29%)
  between operations  1.04 us (2%)
    ppermute x4, waiting for transfers between devices, over(): return lax.ppermute(block, 'dp', [(i, i ^ bits) for i in range(4)])  12 us
    ppermute x4, starting transfers between devices, over(): return lax.ppermute(block, 'dp', [(i, i ^ bits) for i in range(4)])  10.2 us
    ppermute x10, starting transfers between devices, across(): return lax.ppermute(block, 'seq', plane_pairs(count, even, odd))  8.41 us
    pallas_call x7, Pallas kernels, add_slot(): pl.pallas_call(functools.partial(slot_kernel, slot, names, sides, not who...  7.03 us
    ppermute x10, waiting for transfers between devices, across(): return lax.ppermute(block, 'seq', plane_pairs(count, even, odd))  5.18 us
    pallas_call x1, Pallas kernels, per_device(): pl.pallas_call(back_kernel, out_shape=[jax.ShapeDtypeStruct(signal.shape,...  3.54 us
    pallas_call x1, Pallas kernels, per_device(): pl.pallas_call(end_kernel, out_shape=[jax.ShapeDtypeStruct((2, windows, w...  1.86 us
    pallas_call x1, Pallas kernels, per_device(): pl.pallas_call(own_kernel, out_shape=[side_shape] * 2 + [tap_shape], in_s...  1.64 us
  transfers between devices with their start and end apart: 16, of which 7 were waited for; matrix products, arithmetic and copies ran while one was open for 0% of the time, Pallas kernels for 23%

profile of v6, /device:TPU:0, one launch (start us, length us, event | category | flops | bytes accessed | tf_op | source)
XLA Modules:
  0.0 59.6 jit_solution(12860980944329574524)
XLA Ops:
  0.6 1.1 %shard_map.60 = (bf16[384,384]{1,0:T(8,128)(2,1)S(1)}, bf16[1,480,384]{2,1,0:T(8,128)(2,1)S(1)}) custom-call(bf16[3,384,768]{2,1,0:T(8,128)(2,1)} %tap.7, bf16[768,384]{1,0:T(8,128)(2,1)} %out.5), custom_call_target="tpu_custom_call" | custom-call | tf_op jit(solution)/shard_map/pallas_call | solution.py:350
  1.8 3.1 %collective-permute-start.1 = (bf16[1,480,384]{2,1,0:T(8,128)(2,1)S(1)}, bf16[1,480,384]{2,1,0:T(8,128)(2,1)S(1)}, u32[]{:S(2)}, u32[]{:S(2)}) collective-permute-start(bf16[1,480,384]{2,1,0:T(8,128)(2,1)S(1)} %get-tuple-element.53), channel_id=1, source_target_pairs={{0,8},{8,0},{16,24},{24,16},{1,9},{9,1},{17,25},{25,17},{2,10},{10... | collective-permute-start | bytes 1105928 | tf_op jit(solution)/shard_map/ppermute | solution.py:378
  4.9 2.6 %collective-permute-start = (bf16[384,384]{1,0:T(8,128)(2,1)S(1)}, bf16[384,384]{1,0:T(8,128)(2,1)S(1)}, u32[]{:S(2)}, u32[]{:S(2)}) collective-permute-start(bf16[384,384]{1,0:T(8,128)(2,1)S(1)} %get-tuple-element.52.after), channel_id=1, source_target_pairs={{0,16},{8,24},{16,0},{24,8},{1,17},{9,25},{17,1},{25,9},{2,18},{10... | collective-permute-start | bytes 884744 | tf_op jit(solution)/shard_map/ppermute | solution.py:378
  7.5 1.3 %shard_map.64 = (bf16[2,96,1536]{2,1,0:T(8,128)(2,1)S(1)}, bf16[2,96,1536]{2,1,0:T(8,128)(2,1)S(1)}) custom-call(bf16[2,128,1536]{2,1,0:T(8,128)(2,1)} %signal.5, bf16[2,128,1536]{2,1,0:T(8,128)(2,1)} %cot.5, bf16[384,384]{1,0:T(8,128)(2,1)S(1)} %get-tuple-element.52.after), custom_call_target="tpu_custom_call" | custom-call | tf_op jit(solution)/shard_map/pallas_call | solution.py:365
  8.8 1.3 %collective-permute-start.3 = (bf16[2,96,1536]{2,1,0:T(8,128)(2,1)S(1)}, bf16[2,96,1536]{2,1,0:T(8,128)(2,1)S(1)}, u32[]{:S(2)}, u32[]{:S(2)}) collective-permute-start(bf16[2,96,1536]{2,1,0:T(8,128)(2,1)S(1)} %get-tuple-element.57), channel_id=1, source_target_pairs={{0,1},{1,2},{2,3},{3,4},{4,5},{5,6},{6,7},{8,9},{9,10},{10,11},{11... | collective-permute-start | bytes 1769480 | tf_op jit(solution)/shard_map/ppermute | solution.py:420
  10.1 1.3 %collective-permute-start.4 = (bf16[2,96,1536]{2,1,0:T(8,128)(2,1)S(1)}, bf16[2,96,1536]{2,1,0:T(8,128)(2,1)S(1)}, u32[]{:S(2)}, u32[]{:S(2)}) collective-permute-start(bf16[2,96,1536]{2,1,0:T(8,128)(2,1)S(1)} %get-tuple-element.58), channel_id=1, source_target_pairs={{1,0},{2,1},{3,2},{4,3},{5,4},{6,5},{7,6},{9,8},{10,9},{11,10},{12... | collective-permute-start | bytes 1769480 | tf_op jit(solution)/shard_map/ppermute | solution.py:421
  12.5 1.1 %shard_map.61 = bf16[2,384,384]{2,1,0:T(8,128)(2,1)S(1)} custom-call(bf16[3,384,768]{2,1,0:T(8,128)(2,1)} %tap.7, bf16[768,384]{1,0:T(8,128)(2,1)} %out.5), custom_call_target="tpu_custom_call" | custom-call | flops 1000 | bytes 1000 | tf_op jit(solution)/shard_map/pallas_call | solution.py:431
  13.7 5.4 %collective-permute-done.piece = bf16[384,384]{1,0:T(8,128)(2,1)S(1)} collective-permute-done((bf16[384,384]{1,0:T(8,128)(2,1)S(1)}, bf16[384,384]{1,0:T(8,128)(2,1)S(1)}, u32[]{:S(2)}, u32[]{:S(2)}) %collective-permute-start) | collective-permute-done | bytes 294944 | tf_op jit(solution)/shard_map/ppermute | solution.py:378
  19.8 2.8 %collective-permute-start.5 = (bf16[384,384]{1,0:T(8,128)(2,1)S(1)}, bf16[384,384]{1,0:T(8,128)(2,1)S(1)}, u32[]{:S(2)}, u32[]{:S(2)}) collective-permute-start(bf16[384,384]{1,0:T(8,128)(2,1)S(1)} %collective-permute-done.piece), channel_id=1, source_target_pairs={{0,8},{8,0},{16,24},{24,16},{1,9},{9,1},{17,25},{25,17},{2,10},{10... | collective-permute-start | bytes 884744 | tf_op jit(solution)/shard_map/ppermute | solution.py:378
  22.7 1.6 %collective-permute-start.2 = (bf16[480,384]{1,0:T(8,128)(2,1)S(1)}, bf16[480,384]{1,0:T(8,128)(2,1)S(1)}, u32[]{:S(2)}, u32[]{:S(2)}) collective-permute-start(bf16[480,384]{1,0:T(8,128)(2,1)S(1)} %shard_map.62.first), channel_id=1, source_target_pairs={{0,2},{1,5},{2,0},{3,7},{4,6},{5,1},{6,4},{7,3},{8,10},{9,13},{10,... | collective-permute-start | bytes 1105928 | tf_op jit(solution)/shard_map/ppermute | solution.py:375
  24.3 4.4 %collective-permute-done.5.first = bf16[384,384]{1,0:T(8,128)(2,1)S(1)} collective-permute-done((bf16[384,384]{1,0:T(8,128)(2,1)S(1)}, bf16[384,384]{1,0:T(8,128)(2,1)S(1)}, u32[]{:S(2)}, u32[]{:S(2)}) %collective-permute-start.5) | collective-permute-done | bytes 294944 | tf_op jit(solution)/shard_map/ppermute | solution.py:378
  28.7 1.7 %collective-permute-start.9 = (bf16[2,384,384]{2,1,0:T(8,128)(2,1)S(1)}, bf16[2,384,384]{2,1,0:T(8,128)(2,1)S(1)}, u32[]{:S(2)}, u32[]{:S(2)}) collective-permute-start(bf16[2,384,384]{2,1,0:T(8,128)(2,1)S(1)} %shard_map.61), channel_id=1, source_target_pairs={{0,8},{8,0},{16,24},{24,16},{1,9},{9,1},{17,25},{25,17},{2,10},{10... | collective-permute-start | bytes 1769480 | tf_op jit(solution)/shard_map/ppermute | solution.py:378
  30.4 1.5 %collective-permute-start.6 = (bf16[384,384]{1,0:T(8,128)(2,1)S(1)}, bf16[384,384]{1,0:T(8,128)(2,1)S(1)}, u32[]{:S(2)}, u32[]{:S(2)}) collective-permute-start(bf16[384,384]{1,0:T(8,128)(2,1)S(1)} %collective-permute-done.5.first), channel_id=1, source_target_pairs={{0,2},{1,5},{2,0},{3,7},{4,6},{5,1},{6,4},{7,3},{8,10},{9,13},{10,... | collective-permute-start | bytes 884744 | tf_op jit(solution)/shard_map/ppermute | solution.py:375
  33.1 1.7 %collective-permute-start.13 = (bf16[2,480,384]{2,1,0:T(8,128)(2,1)S(1)}, bf16[2,480,384]{2,1,0:T(8,128)(2,1)S(1)}, u32[]{:S(2)}, u32[]{:S(2)}) collective-permute-start(bf16[2,480,384]{2,1,0:T(8,128)(2,1)S(1)} %shard_map.63.refs_3_), channel_id=1, source_target_pairs={{0,4},{1,3},{2,6},{3,1},{4,0},{5,7},{6,2},{7,5},{8,12},{9,11},{10,... | collective-permute-start | bytes 2211848 | tf_op jit(solution)/shard_map/ppermute | solution.py:375
  34.8 1.6 %shard_map.66 = (f32[2,384,384]{2,1,0:T(8,128)S(1)}, f32[2,384,384]{2,1,0:T(8,128)S(1)}, bf16[384,768]{1,0:T(8,128)(2,1)S(1)}) custom-call(bf16[2,2,256,1536]{3,2,1,0:T(8,128)(2,1)S(1)} %shard_map.65.left.refs_0_, bf16[3,384,768]{2,1,0:T(8,128)(2,1)S(1)} %copy-done, bf16[768,384]{1,0:T(8,128)(2,1)S(1)} %copy-done.3), custom_call_target="tpu_custom_call" | custom-call | flops 1000 | bytes 1000 | tf_op jit(solution)/shard_map/pallas_call | solution.py:454
  38.5 2.7 %collective-permute-start.8 = (bf16[2,384,384]{2,1,0:T(8,128)(2,1)S(1)}, bf16[2,384,384]{2,1,0:T(8,128)(2,1)S(1)}, u32[]{:S(2)}, u32[]{:S(2)}) collective-permute-start(bf16[2,384,384]{2,1,0:T(8,128)(2,1)S(1)} %shard_map.68.refs_3_), channel_id=1, source_target_pairs={{0,4},{1,3},{2,6},{3,1},{4,0},{5,7},{6,2},{7,5},{8,12},{9,11},{10,... | collective-permute-start | bytes 1769480 | tf_op jit(solution)/shard_map/ppermute | solution.py:375
  41.1 1.5 %collective-permute-done.9.refs_3_ = bf16[2,384,384]{2,1,0:T(8,128)(2,1)S(1)} collective-permute-done((bf16[2,384,384]{2,1,0:T(8,128)(2,1)S(1)}, bf16[2,384,384]{2,1,0:T(8,128)(2,1)S(1)}, u32[]{:S(2)}, u32[]{:S(2)}) %collective-permute-start.9) | collective-permute-done | bytes 589856 | tf_op jit(solution)/shard_map/ppermute | solution.py:378
  42.6 2.0 %collective-permute-done.13.refs_2_ = bf16[2,480,384]{2,1,0:T(8,128)(2,1)S(1)} collective-permute-done((bf16[2,480,384]{2,1,0:T(8,128)(2,1)S(1)}, bf16[2,480,384]{2,1,0:T(8,128)(2,1)S(1)}, u32[]{:S(2)}, u32[]{:S(2)}) %collective-permute-start.13) | collective-permute-done | bytes 737312 | tf_op jit(solution)/shard_map/ppermute | solution.py:375
  45.2 1.4 %shard_map.69 = (f32[2,384,384]{2,1,0:T(8,128)S(1)}, f32[2,384,384]{2,1,0:T(8,128)S(1)}, bf16[4,384,768]{2,1,0:T(8,128)(2,1)S(1)}, bf16[384,768]{1,0:T(8,128)(2,1)S(1)}) custom-call(bf16[2,2,256,1536]{3,2,1,0:T(8,128)(2,1)S(1)} %shard_map.65.left.refs_0_, ...), custom_call_target="tpu_custom_call", output_to_operand_aliasing={{0}: (1, {}), {1}: (2, {})} | custom-call | flops 1000 | bytes 1000 | tf_op jit(solution)/shard_map/pallas_call | solution.py:406
  46.6 1.3 %shard_map.70 = (f32[2,384,384]{2,1,0:T(8,128)S(1)}, f32[2,384,384]{2,1,0:T(8,128)S(1)}, bf16[4,384,768]{2,1,0:T(8,128)(2,1)S(1)}) custom-call(bf16[2,2,256,1536]{3,2,1,0:T(8,128)(2,1)S(1)} %shard_map.65.left.refs_0_, f32[2,384,384]{2,1,0:T(8,128)S(1)} %get-tuple-element.72.refs_1_, ...), custom_call_target="tpu_custom_call", output_to_operand_aliasing={{0}: (1, {}), {1}: (2, {})} | custom-call | flops 1000 | bytes 1000 | tf_op jit(solution)/shard_map/pallas_call | solution.py:406
  48.7 2.3 %collective-permute-done.8.refs_2_ = bf16[2,384,384]{2,1,0:T(8,128)(2,1)S(1)} collective-permute-done((bf16[2,384,384]{2,1,0:T(8,128)(2,1)S(1)}, bf16[2,384,384]{2,1,0:T(8,128)(2,1)S(1)}, u32[]{:S(2)}, u32[]{:S(2)}) %collective-permute-start.8) | collective-permute-done | bytes 589856 | tf_op jit(solution)/shard_map/ppermute | solution.py:375
  51.9 1.3 %shard_map.73 = (f32[2,384,384]{2,1,0:T(8,128)S(1)}, f32[2,384,384]{2,1,0:T(8,128)S(1)}, bf16[4,384,768]{2,1,0:T(8,128)(2,1)S(1)}) custom-call(bf16[2,2,256,1536]{3,2,1,0:T(8,128)(2,1)S(1)} %shard_map.65.left.refs_0_, f32[2,384,384]{2,1,0:T(8,128)S(1)} %get-tuple-element.83.refs_1_, ...), custom_call_target="tpu_custom_call", output_to_operand_aliasing={{0}: (1, {}), {1}: (2, {}), {2}: (5, {})} | custom-call | flops 1000 | bytes 1000 | tf_op jit(solution)/shard_map/pallas_call | solution.py:406
  54.0 1.9 %shard_map.75 = (bf16[2,2,192,768]{3,2,1,0:T(8,128)(2,1)S(1)}, bf16[4,384,768]{2,1,0:T(8,128)(2,1)S(1)}) custom-call(bf16[2,2,256,1536]{3,2,1,0:T(8,128)(2,1)S(1)} %shard_map.65.left.refs_0_, f32[2,384,384]{2,1,0:T(8,128)S(1)} %get-tuple-element.87.own, f32[2,384,384]{2,1,0:T(8,128)S(1)} %get-tuple-element.91.mate, ...), custom_call_target="tpu_custom_call", output_to_operand_aliasing={{1}: (5, {})} | custom-call | flops 1000 | bytes 1000 | tf_op jit(solution)/shard_map/pallas_call | solution.py:494
  55.9 3.5 %shard_map.76 = (bf16[2,128,1536]{2,1,0:T(8,128)(2,1)}, bf16[2,128,1536]{2,1,0:T(8,128)(2,1)}) custom-call(bf16[2,128,1536]{2,1,0:T(8,128)(2,1)S(1)} %copy-done.1, bf16[2,128,1536]{2,1,0:T(8,128)(2,1)S(1)} %copy-done.2, f32[2,128,1536]{2,1,0:T(8,128)S(1)} %get-tuple-element.51.slope, bf16[2,2,192,768]{3,2,1,0:T(8,128)(2,1)S(1)} %get-tuple-element.95.right, ...), custom_call_target="tpu_custom_call" | custom-call | flops 1000 | bytes 1000 | tf_op jit(solution)/shard_map/pallas_call | solution.py:504
  (34 shorter events, 8.3 us)
Async XLA Ops:
  1.8 9.6 %copy-start.1 = (bf16[2,128,1536]{2,1,0:T(8,128)(2,1)S(1)}, bf16[2,128,1536]{2,1,0:T(8,128)(2,1)}, u32[]{:S(2)}) copy-start(bf16[2,128,1536]{2,1,0:T(8,128)(2,1)} %signal.5) | copy-start | bytes 2359300
  1.8 9.6 %copy-start.2 = (bf16[2,128,1536]{2,1,0:T(8,128)(2,1)S(1)}, bf16[2,128,1536]{2,1,0:T(8,128)(2,1)}, u32[]{:S(2)}) copy-start(bf16[2,128,1536]{2,1,0:T(8,128)(2,1)} %cot.5) | copy-start | bytes 2359300
  1.8 18.0 %collective-permute-start.1 = (bf16[1,480,384]{2,1,0:T(8,128)(2,1)S(1)}, bf16[1,480,384]{2,1,0:T(8,128)(2,1)S(1)}, u32[]{:S(2)}, u32[]{:S(2)}) collective-permute-start(bf16[1,480,384]{2,1,0:T(8,128)(2,1)S(1)} %get-tuple-element.53), channel_id=1, source_target_pairs={{0,8},{8,0},{16,24},{24,16},{1,9},{9,1},{17,25},{25,17},{2,10},{10... | collective-permute-start | bytes 1105928 | tf_op jit(solution)/shard_map/ppermute | solution.py:378
  4.9 14.2 %collective-permute-start = (bf16[384,384]{1,0:T(8,128)(2,1)S(1)}, bf16[384,384]{1,0:T(8,128)(2,1)S(1)}, u32[]{:S(2)}, u32[]{:S(2)}) collective-permute-start(bf16[384,384]{1,0:T(8,128)(2,1)S(1)} %get-tuple-element.52.after), channel_id=1, source_target_pairs={{0,16},{8,24},{16,0},{24,8},{1,17},{9,25},{17,1},{25,9},{2,18},{10... | collective-permute-start | bytes 884744 | tf_op jit(solution)/shard_map/ppermute | solution.py:378
  8.8 15.5 %collective-permute-start.3 = (bf16[2,96,1536]{2,1,0:T(8,128)(2,1)S(1)}, bf16[2,96,1536]{2,1,0:T(8,128)(2,1)S(1)}, u32[]{:S(2)}, u32[]{:S(2)}) collective-permute-start(bf16[2,96,1536]{2,1,0:T(8,128)(2,1)S(1)} %get-tuple-element.57), channel_id=1, source_target_pairs={{0,1},{1,2},{2,3},{3,4},{4,5},{5,6},{6,7},{8,9},{9,10},{10,11},{11... | collective-permute-start | bytes 1769480 | tf_op jit(solution)/shard_map/ppermute | solution.py:420
  10.1 14.2 %collective-permute-start.4 = (bf16[2,96,1536]{2,1,0:T(8,128)(2,1)S(1)}, bf16[2,96,1536]{2,1,0:T(8,128)(2,1)S(1)}, u32[]{:S(2)}, u32[]{:S(2)}) collective-permute-start(bf16[2,96,1536]{2,1,0:T(8,128)(2,1)S(1)} %get-tuple-element.58), channel_id=1, source_target_pairs={{1,0},{2,1},{3,2},{4,3},{5,4},{6,5},{7,6},{9,8},{10,9},{11,10},{12... | collective-permute-start | bytes 1769480 | tf_op jit(solution)/shard_map/ppermute | solution.py:421
  19.8 8.9 %collective-permute-start.5 = (bf16[384,384]{1,0:T(8,128)(2,1)S(1)}, bf16[384,384]{1,0:T(8,128)(2,1)S(1)}, u32[]{:S(2)}, u32[]{:S(2)}) collective-permute-start(bf16[384,384]{1,0:T(8,128)(2,1)S(1)} %collective-permute-done.piece), channel_id=1, source_target_pairs={{0,8},{8,0},{16,24},{24,16},{1,9},{9,1},{17,25},{25,17},{2,10},{10... | collective-permute-start | bytes 884744 | tf_op jit(solution)/shard_map/ppermute | solution.py:378
  22.7 10.0 %collective-permute-start.2 = (bf16[480,384]{1,0:T(8,128)(2,1)S(1)}, bf16[480,384]{1,0:T(8,128)(2,1)S(1)}, u32[]{:S(2)}, u32[]{:S(2)}) collective-permute-start(bf16[480,384]{1,0:T(8,128)(2,1)S(1)} %shard_map.62.first), channel_id=1, source_target_pairs={{0,2},{1,5},{2,0},{3,7},{4,6},{5,1},{6,4},{7,3},{8,10},{9,13},{10,... | collective-permute-start | bytes 1105928 | tf_op jit(solution)/shard_map/ppermute | solution.py:375
  28.7 13.9 %collective-permute-start.9 = (bf16[2,384,384]{2,1,0:T(8,128)(2,1)S(1)}, bf16[2,384,384]{2,1,0:T(8,128)(2,1)S(1)}, u32[]{:S(2)}, u32[]{:S(2)}) collective-permute-start(bf16[2,384,384]{2,1,0:T(8,128)(2,1)S(1)} %shard_map.61), channel_id=1, source_target_pairs={{0,8},{8,0},{16,24},{24,16},{1,9},{9,1},{17,25},{25,17},{2,10},{10... | collective-permute-start | bytes 1769480 | tf_op jit(solution)/shard_map/ppermute | solution.py:378
  30.4 6.1 %collective-permute-start.7 = (bf16[1,480,384]{2,1,0:T(8,128)(2,1)S(1)}, bf16[1,480,384]{2,1,0:T(8,128)(2,1)S(1)}, u32[]{:S(2)}, u32[]{:S(2)}) collective-permute-start(bf16[1,480,384]{2,1,0:T(8,128)(2,1)S(1)} %collective-permute-done.1.first.refs_3_), channel_id=1, source_target_pairs={{0,1},{1,0},{2,3},{3,2},{4,5},{5,4},{6,7},{7,6},{8,9},{9,8},{10,11... | collective-permute-start | bytes 1105928 | tf_op jit(solution)/shard_map/ppermute | solution.py:375
  30.4 7.8 %collective-permute-start.6 = (bf16[384,384]{1,0:T(8,128)(2,1)S(1)}, bf16[384,384]{1,0:T(8,128)(2,1)S(1)}, u32[]{:S(2)}, u32[]{:S(2)}) collective-permute-start(bf16[384,384]{1,0:T(8,128)(2,1)S(1)} %collective-permute-done.5.first), channel_id=1, source_target_pairs={{0,2},{1,5},{2,0},{3,7},{4,6},{5,1},{6,4},{7,3},{8,10},{9,13},{10,... | collective-permute-start | bytes 884744 | tf_op jit(solution)/shard_map/ppermute | solution.py:375
  31.9 2.9 %copy-start = (bf16[3,384,768]{2,1,0:T(8,128)(2,1)S(1)}, bf16[3,384,768]{2,1,0:T(8,128)(2,1)}, u32[]{:S(2)}) copy-start(bf16[3,384,768]{2,1,0:T(8,128)(2,1)} %tap.7) | copy-start | bytes 5308420
  32.7 2.1 %copy-start.3 = (bf16[768,384]{1,0:T(8,128)(2,1)S(1)}, bf16[768,384]{1,0:T(8,128)(2,1)}, u32[]{:S(2)}) copy-start(bf16[768,384]{1,0:T(8,128)(2,1)} %out.5) | copy-start | bytes 1769476
  33.1 11.5 %collective-permute-start.13 = (bf16[2,480,384]{2,1,0:T(8,128)(2,1)S(1)}, bf16[2,480,384]{2,1,0:T(8,128)(2,1)S(1)}, u32[]{:S(2)}, u32[]{:S(2)}) collective-permute-start(bf16[2,480,384]{2,1,0:T(8,128)(2,1)S(1)} %shard_map.63.refs_3_), channel_id=1, source_target_pairs={{0,4},{1,3},{2,6},{3,1},{4,0},{5,7},{6,2},{7,5},{8,12},{9,11},{10,... | collective-permute-start | bytes 2211848 | tf_op jit(solution)/shard_map/ppermute | solution.py:375
  34.8 10.4 %collective-permute-start.11 = (bf16[2,480,384]{2,1,0:T(8,128)(2,1)S(1)}, bf16[2,480,384]{2,1,0:T(8,128)(2,1)S(1)}, u32[]{:S(2)}, u32[]{:S(2)}) collective-permute-start(bf16[2,480,384]{2,1,0:T(8,128)(2,1)S(1)} %shard_map.63.refs_3_), channel_id=1, source_target_pairs={{0,1},{1,0},{2,3},{3,2},{4,5},{5,4},{6,7},{7,6},{8,9},{9,8},{10,11... | collective-permute-start | bytes 2211848 | tf_op jit(solution)/shard_map/ppermute | solution.py:375
  38.4 8.2 %collective-permute-start.12 = (bf16[2,384,384]{2,1,0:T(8,128)(2,1)S(1)}, bf16[2,384,384]{2,1,0:T(8,128)(2,1)S(1)}, u32[]{:S(2)}, u32[]{:S(2)}) collective-permute-start(bf16[2,384,384]{2,1,0:T(8,128)(2,1)S(1)} %shard_map.68.refs_3_), channel_id=1, source_target_pairs={{0,1},{1,0},{2,3},{3,2},{4,5},{5,4},{6,7},{7,6},{8,9},{9,8},{10,11... | collective-permute-start | bytes 1769480 | tf_op jit(solution)/shard_map/ppermute | solution.py:375
  38.5 12.5 %collective-permute-start.8 = (bf16[2,384,384]{2,1,0:T(8,128)(2,1)S(1)}, bf16[2,384,384]{2,1,0:T(8,128)(2,1)S(1)}, u32[]{:S(2)}, u32[]{:S(2)}) collective-permute-start(bf16[2,384,384]{2,1,0:T(8,128)(2,1)S(1)} %shard_map.68.refs_3_), channel_id=1, source_target_pairs={{0,4},{1,3},{2,6},{3,1},{4,0},{5,7},{6,2},{7,5},{8,12},{9,11},{10,... | collective-permute-start | bytes 1769480 | tf_op jit(solution)/shard_map/ppermute | solution.py:375
  42.6 8.3 %collective-permute-start.10 = (bf16[2,384,384]{2,1,0:T(8,128)(2,1)S(1)}, bf16[2,384,384]{2,1,0:T(8,128)(2,1)S(1)}, u32[]{:S(2)}, u32[]{:S(2)}) collective-permute-start(bf16[2,384,384]{2,1,0:T(8,128)(2,1)S(1)} %collective-permute-done.9.refs_3_), channel_id=1, source_target_pairs={{0,1},{1,0},{2,3},{3,2},{4,5},{5,4},{6,7},{7,6},{8,9},{9,8},{10,11... | collective-permute-start | bytes 1769480 | tf_op jit(solution)/shard_map/ppermute | solution.py:375
  44.6 8.6 %collective-permute-start.14 = (bf16[2,480,384]{2,1,0:T(8,128)(2,1)S(1)}, bf16[2,480,384]{2,1,0:T(8,128)(2,1)S(1)}, u32[]{:S(2)}, u32[]{:S(2)}) collective-permute-start(bf16[2,480,384]{2,1,0:T(8,128)(2,1)S(1)} %collective-permute-done.13.refs_2_), channel_id=1, source_target_pairs={{0,1},{1,0},{2,3},{3,2},{4,5},{5,4},{6,7},{7,6},{8,9},{9,8},{10,11... | collective-permute-start | bytes 2211848 | tf_op jit(solution)/shard_map/ppermute | solution.py:375
  51.6 2.4 %collective-permute-start.15 = (bf16[2,384,384]{2,1,0:T(8,128)(2,1)S(1)}, bf16[2,384,384]{2,1,0:T(8,128)(2,1)S(1)}, u32[]{:S(2)}, u32[]{:S(2)}) collective-permute-start(bf16[2,384,384]{2,1,0:T(8,128)(2,1)S(1)} %collective-permute-done.8.refs_2_), channel_id=1, source_target_pairs={{0,1},{1,0},{2,3},{3,2},{4,5},{5,4},{6,7},{7,6},{8,9},{9,8},{10,11... | collective-permute-start | bytes 1769480 | tf_op jit(solution)/shard_map/ppermute | solution.py:375

commit v7 on v6

--- a/solution.py
+++ b/solution.py
@@ -481,12 +481,15 @@
         2, ("far",), (far2,), left, sums[:1], whole2, pair_tap, carries=True
     )
     sums = [own_sums, sums[1]]
+    (own_sums,), whole1 = add_slot(1, ("last",), (last,), left, sums[:1], whole1)
+    sums = [own_sums, sums[1]]
     far3, mate_last, *sums = tie(far3, mate_last, *sums)
     (own_sums,), whole3 = add_slot(3, ("far",), (far3,), left, sums[:1], whole3)
     far3, own_sums = tie(far3, own_sums)
     far_mate3 = across(far3, 1, 1)
     sums = [own_sums, sums[1]]
-    sums, whole1 = add_slot(1, ("last", "mate_last"), (last, mate_last), left, sums, whole1)
+    (mate_sums,), whole1 = add_slot(1, ("mate_last",), (mate_last,), left, sums[1:], whole1)
+    sums = [sums[0], mate_sums]
     (mate_sums,), whole2, pair_tap = add_slot(
         2, ("mate_far",), (far_mate2,), left, sums[1:], whole2, pair_tap, carries=True
     )

time: 59.8 us -> 59.4 us (level)
  waiting for transfers between devices: 17.2 us -> 16.6 us
    pallas_call x7 -> x8, Pallas kernels: 7.03 us -> 7.21 us  [add_slot(): pl.pallas_call(functools.partial(slot_kernel, slot, names, sides, not who...]
  transfers between devices with their start and end apart: 16 -> 16, of which waited for: 7 -> 8; matrix products, arithmetic and copies ran while one was open for 0% -> 0% of each run, Pallas kernels for 23% -> 23%
where the time goes in v7:
time: 59.4 us; the launch traced here: 59.2 us
  starting transfers between devices  21.2 us (36%)
  Pallas kernels  20.3 us (34%)
  waiting for transfers between devices  16.6 us (28%)
  between operations  1.04 us (2%)
    ppermute x4, waiting for transfers between devices, over(): return lax.ppermute(block, 'dp', [(i, i ^ bits) for i in range(4)])  12 us
    ppermute x4, starting transfers between devices, over(): return lax.ppermute(block, 'dp', [(i, i ^ bits) for i in range(4)])  10.2 us
    ppermute x10, starting transfers between devices, across(): return lax.ppermute(block, 'seq', plane_pairs(count, even, odd))  8.41 us
    pallas_call x8, Pallas kernels, add_slot(): pl.pallas_call(functools.partial(slot_kernel, slot, names, sides, not who...  7.21 us
    ppermute x10, waiting for transfers between devices, across(): return lax.ppermute(block, 'seq', plane_pairs(count, even, odd))  4.62 us
    pallas_call x1, Pallas kernels, per_device(): pl.pallas_call(back_kernel, out_shape=[jax.ShapeDtypeStruct(signal.shape,...  3.54 us
    pallas_call x1, Pallas kernels, per_device(): pl.pallas_call(end_kernel, out_shape=[jax.ShapeDtypeStruct((2, windows, w...  1.8 us
    pallas_call x1, Pallas kernels, per_device(): pl.pallas_call(own_kernel, out_shape=[side_shape] * 2 + [tap_shape], in_s...  1.64 us
  transfers between devices with their start and end apart: 16, of which 8 were waited for; matrix products, arithmetic and copies ran while one was open for 0% of the time, Pallas kernels for 23%

profile of v7, /device:TPU:0, one launch (start us, length us, event | category | flops | bytes accessed | tf_op | source)
XLA Modules:
  0.0 59.2 jit_solution(2561861870317348977)
XLA Ops:
  0.6 1.1 %shard_map.60 = (bf16[384,384]{1,0:T(8,128)(2,1)S(1)}, bf16[1,480,384]{2,1,0:T(8,128)(2,1)S(1)}) custom-call(bf16[3,384,768]{2,1,0:T(8,128)(2,1)} %tap.7, bf16[768,384]{1,0:T(8,128)(2,1)} %out.5), custom_call_target="tpu_custom_call" | custom-call | tf_op jit(solution)/shard_map/pallas_call | solution.py:350
  1.8 3.1 %collective-permute-start.1 = (bf16[1,480,384]{2,1,0:T(8,128)(2,1)S(1)}, bf16[1,480,384]{2,1,0:T(8,128)(2,1)S(1)}, u32[]{:S(2)}, u32[]{:S(2)}) collective-permute-start(bf16[1,480,384]{2,1,0:T(8,128)(2,1)S(1)} %get-tuple-element.54), channel_id=1, source_target_pairs={{0,8},{8,0},{16,24},{24,16},{1,9},{9,1},{17,25},{25,17},{2,10},{10... | collective-permute-start | bytes 1105928 | tf_op jit(solution)/shard_map/ppermute | solution.py:378
  4.9 2.6 %collective-permute-start = (bf16[384,384]{1,0:T(8,128)(2,1)S(1)}, bf16[384,384]{1,0:T(8,128)(2,1)S(1)}, u32[]{:S(2)}, u32[]{:S(2)}) collective-permute-start(bf16[384,384]{1,0:T(8,128)(2,1)S(1)} %get-tuple-element.53.after), channel_id=1, source_target_pairs={{0,16},{8,24},{16,0},{24,8},{1,17},{9,25},{17,1},{25,9},{2,18},{10... | collective-permute-start | bytes 884744 | tf_op jit(solution)/shard_map/ppermute | solution.py:378
  7.5 1.3 %shard_map.64 = (bf16[2,96,1536]{2,1,0:T(8,128)(2,1)S(1)}, bf16[2,96,1536]{2,1,0:T(8,128)(2,1)S(1)}) custom-call(bf16[2,128,1536]{2,1,0:T(8,128)(2,1)} %signal.5, bf16[2,128,1536]{2,1,0:T(8,128)(2,1)} %cot.5, bf16[384,384]{1,0:T(8,128)(2,1)S(1)} %get-tuple-element.53.after), custom_call_target="tpu_custom_call" | custom-call | tf_op jit(solution)/shard_map/pallas_call | solution.py:365
  8.8 1.3 %collective-permute-start.3 = (bf16[2,96,1536]{2,1,0:T(8,128)(2,1)S(1)}, bf16[2,96,1536]{2,1,0:T(8,128)(2,1)S(1)}, u32[]{:S(2)}, u32[]{:S(2)}) collective-permute-start(bf16[2,96,1536]{2,1,0:T(8,128)(2,1)S(1)} %get-tuple-element.58), channel_id=1, source_target_pairs={{0,1},{1,2},{2,3},{3,4},{4,5},{5,6},{6,7},{8,9},{9,10},{10,11},{11... | collective-permute-start | bytes 1769480 | tf_op jit(solution)/shard_map/ppermute | solution.py:420
  10.1 1.3 %collective-permute-start.4 = (bf16[2,96,1536]{2,1,0:T(8,128)(2,1)S(1)}, bf16[2,96,1536]{2,1,0:T(8,128)(2,1)S(1)}, u32[]{:S(2)}, u32[]{:S(2)}) collective-permute-start(bf16[2,96,1536]{2,1,0:T(8,128)(2,1)S(1)} %get-tuple-element.59), channel_id=1, source_target_pairs={{1,0},{2,1},{3,2},{4,3},{5,4},{6,5},{7,6},{9,8},{10,9},{11,10},{12... | collective-permute-start | bytes 1769480 | tf_op jit(solution)/shard_map/ppermute | solution.py:421
  11.4 1.1 %shard_map.59 = (bf16[2,2,256,1536]{3,2,1,0:T(8,128)(2,1)S(1)}, f32[2,128,1536]{2,1,0:T(8,128)S(1)}) custom-call(bf16[2,128,1536]{2,1,0:T(8,128)(2,1)S(1)} %copy-done.1, bf16[2,128,1536]{2,1,0:T(8,128)(2,1)S(1)} %copy-done.2), custom_call_target="tpu_custom_call" | custom-call | flops 1000 | bytes 1000 | tf_op jit(solution)/shard_map/pallas_call | solution.py:423
  12.5 1.1 %shard_map.61 = bf16[2,384,384]{2,1,0:T(8,128)(2,1)S(1)} custom-call(bf16[3,384,768]{2,1,0:T(8,128)(2,1)} %tap.7, bf16[768,384]{1,0:T(8,128)(2,1)} %out.5), custom_call_target="tpu_custom_call" | custom-call | flops 1000 | bytes 1000 | tf_op jit(solution)/shard_map/pallas_call | solution.py:431
  13.7 5.4 %collective-permute-done.piece = bf16[384,384]{1,0:T(8,128)(2,1)S(1)} collective-permute-done((bf16[384,384]{1,0:T(8,128)(2,1)S(1)}, bf16[384,384]{1,0:T(8,128)(2,1)S(1)}, u32[]{:S(2)}, u32[]{:S(2)}) %collective-permute-start) | collective-permute-done | bytes 294944 | tf_op jit(solution)/shard_map/ppermute | solution.py:378
  19.8 2.8 %collective-permute-start.5 = (bf16[384,384]{1,0:T(8,128)(2,1)S(1)}, bf16[384,384]{1,0:T(8,128)(2,1)S(1)}, u32[]{:S(2)}, u32[]{:S(2)}) collective-permute-start(bf16[384,384]{1,0:T(8,128)(2,1)S(1)} %collective-permute-done.piece), channel_id=1, source_target_pairs={{0,8},{8,0},{16,24},{24,16},{1,9},{9,1},{17,25},{25,17},{2,10},{10... | collective-permute-start | bytes 884744 | tf_op jit(solution)/shard_map/ppermute | solution.py:378
  22.7 1.6 %collective-permute-start.2 = (bf16[480,384]{1,0:T(8,128)(2,1)S(1)}, bf16[480,384]{1,0:T(8,128)(2,1)S(1)}, u32[]{:S(2)}, u32[]{:S(2)}) collective-permute-start(bf16[480,384]{1,0:T(8,128)(2,1)S(1)} %shard_map.62.first), channel_id=1, source_target_pairs={{0,2},{1,5},{2,0},{3,7},{4,6},{5,1},{6,4},{7,3},{8,10},{9,13},{10,... | collective-permute-start | bytes 1105928 | tf_op jit(solution)/shard_map/ppermute | solution.py:375
  24.3 4.4 %collective-permute-done.5.first = bf16[384,384]{1,0:T(8,128)(2,1)S(1)} collective-permute-done((bf16[384,384]{1,0:T(8,128)(2,1)S(1)}, bf16[384,384]{1,0:T(8,128)(2,1)S(1)}, u32[]{:S(2)}, u32[]{:S(2)}) %collective-permute-start.5) | collective-permute-done | bytes 294944 | tf_op jit(solution)/shard_map/ppermute | solution.py:378
  28.7 1.7 %collective-permute-start.9 = (bf16[2,384,384]{2,1,0:T(8,128)(2,1)S(1)}, bf16[2,384,384]{2,1,0:T(8,128)(2,1)S(1)}, u32[]{:S(2)}, u32[]{:S(2)}) collective-permute-start(bf16[2,384,384]{2,1,0:T(8,128)(2,1)S(1)} %shard_map.61), channel_id=1, source_target_pairs={{0,8},{8,0},{16,24},{24,16},{1,9},{9,1},{17,25},{25,17},{2,10},{10... | collective-permute-start | bytes 1769480 | tf_op jit(solution)/shard_map/ppermute | solution.py:378
  30.4 1.5 %collective-permute-start.6 = (bf16[384,384]{1,0:T(8,128)(2,1)S(1)}, bf16[384,384]{1,0:T(8,128)(2,1)S(1)}, u32[]{:S(2)}, u32[]{:S(2)}) collective-permute-start(bf16[384,384]{1,0:T(8,128)(2,1)S(1)} %collective-permute-done.5.first), channel_id=1, source_target_pairs={{0,2},{1,5},{2,0},{3,7},{4,6},{5,1},{6,4},{7,3},{8,10},{9,13},{10,... | collective-permute-start | bytes 884744 | tf_op jit(solution)/shard_map/ppermute | solution.py:375
  33.1 1.7 %collective-permute-start.13 = (bf16[2,480,384]{2,1,0:T(8,128)(2,1)S(1)}, bf16[2,480,384]{2,1,0:T(8,128)(2,1)S(1)}, u32[]{:S(2)}, u32[]{:S(2)}) collective-permute-start(bf16[2,480,384]{2,1,0:T(8,128)(2,1)S(1)} %shard_map.63.refs_3_), channel_id=1, source_target_pairs={{0,4},{1,3},{2,6},{3,1},{4,0},{5,7},{6,2},{7,5},{8,12},{9,11},{10,... | collective-permute-start | bytes 2211848 | tf_op jit(solution)/shard_map/ppermute | solution.py:375
  34.8 1.6 %shard_map.66 = (f32[2,384,384]{2,1,0:T(8,128)S(1)}, f32[2,384,384]{2,1,0:T(8,128)S(1)}, bf16[384,768]{1,0:T(8,128)(2,1)S(1)}) custom-call(bf16[2,2,256,1536]{3,2,1,0:T(8,128)(2,1)S(1)} %shard_map.65.left.refs_0_, bf16[3,384,768]{2,1,0:T(8,128)(2,1)S(1)} %copy-done, bf16[768,384]{1,0:T(8,128)(2,1)S(1)} %copy-done.3), custom_call_target="tpu_custom_call" | custom-call | flops 1000 | bytes 1000 | tf_op jit(solution)/shard_map/pallas_call | solution.py:454
  38.5 2.7 %collective-permute-start.8 = (bf16[2,384,384]{2,1,0:T(8,128)(2,1)S(1)}, bf16[2,384,384]{2,1,0:T(8,128)(2,1)S(1)}, u32[]{:S(2)}, u32[]{:S(2)}) collective-permute-start(bf16[2,384,384]{2,1,0:T(8,128)(2,1)S(1)} %shard_map.68.refs_3_), channel_id=1, source_target_pairs={{0,4},{1,3},{2,6},{3,1},{4,0},{5,7},{6,2},{7,5},{8,12},{9,11},{10,... | collective-permute-start | bytes 1769480 | tf_op jit(solution)/shard_map/ppermute | solution.py:375
  41.1 1.5 %collective-permute-done.9.refs_2_ = bf16[2,384,384]{2,1,0:T(8,128)(2,1)S(1)} collective-permute-done((bf16[2,384,384]{2,1,0:T(8,128)(2,1)S(1)}, bf16[2,384,384]{2,1,0:T(8,128)(2,1)S(1)}, u32[]{:S(2)}, u32[]{:S(2)}) %collective-permute-start.9) | collective-permute-done | bytes 589856 | tf_op jit(solution)/shard_map/ppermute | solution.py:378
  42.6 2.0 %collective-permute-done.13.refs_2_ = bf16[2,480,384]{2,1,0:T(8,128)(2,1)S(1)} collective-permute-done((bf16[2,480,384]{2,1,0:T(8,128)(2,1)S(1)}, bf16[2,480,384]{2,1,0:T(8,128)(2,1)S(1)}, u32[]{:S(2)}, u32[]{:S(2)}) %collective-permute-start.13) | collective-permute-done | bytes 737312 | tf_op jit(solution)/shard_map/ppermute | solution.py:375
  45.2 1.4 %shard_map.69 = (f32[2,384,384]{2,1,0:T(8,128)S(1)}, f32[2,384,384]{2,1,0:T(8,128)S(1)}, bf16[4,384,768]{2,1,0:T(8,128)(2,1)S(1)}, bf16[384,768]{1,0:T(8,128)(2,1)S(1)}) custom-call(bf16[2,2,256,1536]{3,2,1,0:T(8,128)(2,1)S(1)} %shard_map.65.left.refs_0_, ...), custom_call_target="tpu_custom_call", output_to_operand_aliasing={{0}: (1, {}), {1}: (2, {})} | custom-call | flops 1000 | bytes 1000 | tf_op jit(solution)/shard_map/pallas_call | solution.py:406
  46.6 1.3 %shard_map.70 = (f32[2,384,384]{2,1,0:T(8,128)S(1)}, f32[2,384,384]{2,1,0:T(8,128)S(1)}, bf16[4,384,768]{2,1,0:T(8,128)(2,1)S(1)}) custom-call(bf16[2,2,256,1536]{3,2,1,0:T(8,128)(2,1)S(1)} %shard_map.65.left.refs_0_, f32[2,384,384]{2,1,0:T(8,128)S(1)} %get-tuple-element.73.refs_1_, ...), custom_call_target="tpu_custom_call", output_to_operand_aliasing={{0}: (1, {}), {1}: (2, {})} | custom-call | flops 1000 | bytes 1000 | tf_op jit(solution)/shard_map/pallas_call | solution.py:406
  49.4 1.5 %collective-permute-done.8.refs_2_ = bf16[2,384,384]{2,1,0:T(8,128)(2,1)S(1)} collective-permute-done((bf16[2,384,384]{2,1,0:T(8,128)(2,1)S(1)}, bf16[2,384,384]{2,1,0:T(8,128)(2,1)S(1)}, u32[]{:S(2)}, u32[]{:S(2)}) %collective-permute-start.8) | collective-permute-done | bytes 589856 | tf_op jit(solution)/shard_map/ppermute | solution.py:375
  53.7 1.8 %shard_map.76 = (bf16[2,2,192,768]{3,2,1,0:T(8,128)(2,1)S(1)}, bf16[4,384,768]{2,1,0:T(8,128)(2,1)S(1)}) custom-call(bf16[2,2,256,1536]{3,2,1,0:T(8,128)(2,1)S(1)} %shard_map.65.left.refs_0_, f32[2,384,384]{2,1,0:T(8,128)S(1)} %get-tuple-element.86.own, f32[2,384,384]{2,1,0:T(8,128)S(1)} %get-tuple-element.93.mate, ...), custom_call_target="tpu_custom_call", output_to_operand_aliasing={{1}: (5, {})} | custom-call | flops 1000 | bytes 1000 | tf_op jit(solution)/shard_map/pallas_call | solution.py:497
  55.5 3.5 %shard_map.77 = (bf16[2,128,1536]{2,1,0:T(8,128)(2,1)}, bf16[2,128,1536]{2,1,0:T(8,128)(2,1)}) custom-call(bf16[2,128,1536]{2,1,0:T(8,128)(2,1)S(1)} %copy-done.1, bf16[2,128,1536]{2,1,0:T(8,128)(2,1)S(1)} %copy-done.2, f32[2,128,1536]{2,1,0:T(8,128)S(1)} %get-tuple-element.52.slope, bf16[2,2,192,768]{3,2,1,0:T(8,128)(2,1)S(1)} %get-tuple-element.97.right, ...), custom_call_target="tpu_custom_call" | custom-call | flops 1000 | bytes 1000 | tf_op jit(solution)/shard_map/pallas_call | solution.py:507
  (35 shorter events, 8.8 us)
Async XLA Ops:
  1.8 9.6 %copy-start.1 = (bf16[2,128,1536]{2,1,0:T(8,128)(2,1)S(1)}, bf16[2,128,1536]{2,1,0:T(8,128)(2,1)}, u32[]{:S(2)}) copy-start(bf16[2,128,1536]{2,1,0:T(8,128)(2,1)} %signal.5) | copy-start | bytes 2359300
  1.8 9.6 %copy-start.2 = (bf16[2,128,1536]{2,1,0:T(8,128)(2,1)S(1)}, bf16[2,128,1536]{2,1,0:T(8,128)(2,1)}, u32[]{:S(2)}) copy-start(bf16[2,128,1536]{2,1,0:T(8,128)(2,1)} %cot.5) | copy-start | bytes 2359300
  1.8 18.0 %collective-permute-start.1 = (bf16[1,480,384]{2,1,0:T(8,128)(2,1)S(1)}, bf16[1,480,384]{2,1,0:T(8,128)(2,1)S(1)}, u32[]{:S(2)}, u32[]{:S(2)}) collective-permute-start(bf16[1,480,384]{2,1,0:T(8,128)(2,1)S(1)} %get-tuple-element.54), channel_id=1, source_target_pairs={{0,8},{8,0},{16,24},{24,16},{1,9},{9,1},{17,25},{25,17},{2,10},{10... | collective-permute-start | bytes 1105928 | tf_op jit(solution)/shard_map/ppermute | solution.py:378
  4.9 14.2 %collective-permute-start = (bf16[384,384]{1,0:T(8,128)(2,1)S(1)}, bf16[384,384]{1,0:T(8,128)(2,1)S(1)}, u32[]{:S(2)}, u32[]{:S(2)}) collective-permute-start(bf16[384,384]{1,0:T(8,128)(2,1)S(1)} %get-tuple-element.53.after), channel_id=1, source_target_pairs={{0,16},{8,24},{16,0},{24,8},{1,17},{9,25},{17,1},{25,9},{2,18},{10... | collective-permute-start | bytes 884744 | tf_op jit(solution)/shard_map/ppermute | solution.py:378
  8.8 15.5 %collective-permute-start.3 = (bf16[2,96,1536]{2,1,0:T(8,128)(2,1)S(1)}, bf16[2,96,1536]{2,1,0:T(8,128)(2,1)S(1)}, u32[]{:S(2)}, u32[]{:S(2)}) collective-permute-start(bf16[2,96,1536]{2,1,0:T(8,128)(2,1)S(1)} %get-tuple-element.58), channel_id=1, source_target_pairs={{0,1},{1,2},{2,3},{3,4},{4,5},{5,6},{6,7},{8,9},{9,10},{10,11},{11... | collective-permute-start | bytes 1769480 | tf_op jit(solution)/shard_map/ppermute | solution.py:420
  10.1 14.2 %collective-permute-start.4 = (bf16[2,96,1536]{2,1,0:T(8,128)(2,1)S(1)}, bf16[2,96,1536]{2,1,0:T(8,128)(2,1)S(1)}, u32[]{:S(2)}, u32[]{:S(2)}) collective-permute-start(bf16[2,96,1536]{2,1,0:T(8,128)(2,1)S(1)} %get-tuple-element.59), channel_id=1, source_target_pairs={{1,0},{2,1},{3,2},{4,3},{5,4},{6,5},{7,6},{9,8},{10,9},{11,10},{12... | collective-permute-start | bytes 1769480 | tf_op jit(solution)/shard_map/ppermute | solution.py:421
  19.8 8.9 %collective-permute-start.5 = (bf16[384,384]{1,0:T(8,128)(2,1)S(1)}, bf16[384,384]{1,0:T(8,128)(2,1)S(1)}, u32[]{:S(2)}, u32[]{:S(2)}) collective-permute-start(bf16[384,384]{1,0:T(8,128)(2,1)S(1)} %collective-permute-done.piece), channel_id=1, source_target_pairs={{0,8},{8,0},{16,24},{24,16},{1,9},{9,1},{17,25},{25,17},{2,10},{10... | collective-permute-start | bytes 884744 | tf_op jit(solution)/shard_map/ppermute | solution.py:378
  22.7 10.0 %collective-permute-start.2 = (bf16[480,384]{1,0:T(8,128)(2,1)S(1)}, bf16[480,384]{1,0:T(8,128)(2,1)S(1)}, u32[]{:S(2)}, u32[]{:S(2)}) collective-permute-start(bf16[480,384]{1,0:T(8,128)(2,1)S(1)} %shard_map.62.first), channel_id=1, source_target_pairs={{0,2},{1,5},{2,0},{3,7},{4,6},{5,1},{6,4},{7,3},{8,10},{9,13},{10,... | collective-permute-start | bytes 1105928 | tf_op jit(solution)/shard_map/ppermute | solution.py:375
  28.7 13.9 %collective-permute-start.9 = (bf16[2,384,384]{2,1,0:T(8,128)(2,1)S(1)}, bf16[2,384,384]{2,1,0:T(8,128)(2,1)S(1)}, u32[]{:S(2)}, u32[]{:S(2)}) collective-permute-start(bf16[2,384,384]{2,1,0:T(8,128)(2,1)S(1)} %shard_map.61), channel_id=1, source_target_pairs={{0,8},{8,0},{16,24},{24,16},{1,9},{9,1},{17,25},{25,17},{2,10},{10... | collective-permute-start | bytes 1769480 | tf_op jit(solution)/shard_map/ppermute | solution.py:378
  30.4 6.1 %collective-permute-start.7 = (bf16[1,480,384]{2,1,0:T(8,128)(2,1)S(1)}, bf16[1,480,384]{2,1,0:T(8,128)(2,1)S(1)}, u32[]{:S(2)}, u32[]{:S(2)}) collective-permute-start(bf16[1,480,384]{2,1,0:T(8,128)(2,1)S(1)} %collective-permute-done.1.first.refs_3_), channel_id=1, source_target_pairs={{0,1},{1,0},{2,3},{3,2},{4,5},{5,4},{6,7},{7,6},{8,9},{9,8},{10,11... | collective-permute-start | bytes 1105928 | tf_op jit(solution)/shard_map/ppermute | solution.py:375
  30.4 7.8 %collective-permute-start.6 = (bf16[384,384]{1,0:T(8,128)(2,1)S(1)}, bf16[384,384]{1,0:T(8,128)(2,1)S(1)}, u32[]{:S(2)}, u32[]{:S(2)}) collective-permute-start(bf16[384,384]{1,0:T(8,128)(2,1)S(1)} %collective-permute-done.5.first), channel_id=1, source_target_pairs={{0,2},{1,5},{2,0},{3,7},{4,6},{5,1},{6,4},{7,3},{8,10},{9,13},{10,... | collective-permute-start | bytes 884744 | tf_op jit(solution)/shard_map/ppermute | solution.py:375
  31.9 2.9 %copy-start = (bf16[3,384,768]{2,1,0:T(8,128)(2,1)S(1)}, bf16[3,384,768]{2,1,0:T(8,128)(2,1)}, u32[]{:S(2)}) copy-start(bf16[3,384,768]{2,1,0:T(8,128)(2,1)} %tap.7) | copy-start | bytes 5308420
  32.7 2.1 %copy-start.3 = (bf16[768,384]{1,0:T(8,128)(2,1)S(1)}, bf16[768,384]{1,0:T(8,128)(2,1)}, u32[]{:S(2)}) copy-start(bf16[768,384]{1,0:T(8,128)(2,1)} %out.5) | copy-start | bytes 1769476
  33.1 11.5 %collective-permute-start.13 = (bf16[2,480,384]{2,1,0:T(8,128)(2,1)S(1)}, bf16[2,480,384]{2,1,0:T(8,128)(2,1)S(1)}, u32[]{:S(2)}, u32[]{:S(2)}) collective-permute-start(bf16[2,480,384]{2,1,0:T(8,128)(2,1)S(1)} %shard_map.63.refs_3_), channel_id=1, source_target_pairs={{0,4},{1,3},{2,6},{3,1},{4,0},{5,7},{6,2},{7,5},{8,12},{9,11},{10,... | collective-permute-start | bytes 2211848 | tf_op jit(solution)/shard_map/ppermute | solution.py:375
  34.8 10.4 %collective-permute-start.11 = (bf16[2,480,384]{2,1,0:T(8,128)(2,1)S(1)}, bf16[2,480,384]{2,1,0:T(8,128)(2,1)S(1)}, u32[]{:S(2)}, u32[]{:S(2)}) collective-permute-start(bf16[2,480,384]{2,1,0:T(8,128)(2,1)S(1)} %shard_map.63.refs_3_), channel_id=1, source_target_pairs={{0,1},{1,0},{2,3},{3,2},{4,5},{5,4},{6,7},{7,6},{8,9},{9,8},{10,11... | collective-permute-start | bytes 2211848 | tf_op jit(solution)/shard_map/ppermute | solution.py:375
  38.4 8.2 %collective-permute-start.12 = (bf16[2,384,384]{2,1,0:T(8,128)(2,1)S(1)}, bf16[2,384,384]{2,1,0:T(8,128)(2,1)S(1)}, u32[]{:S(2)}, u32[]{:S(2)}) collective-permute-start(bf16[2,384,384]{2,1,0:T(8,128)(2,1)S(1)} %shard_map.68.refs_3_), channel_id=1, source_target_pairs={{0,1},{1,0},{2,3},{3,2},{4,5},{5,4},{6,7},{7,6},{8,9},{9,8},{10,11... | collective-permute-start | bytes 1769480 | tf_op jit(solution)/shard_map/ppermute | solution.py:375
  38.5 12.5 %collective-permute-start.8 = (bf16[2,384,384]{2,1,0:T(8,128)(2,1)S(1)}, bf16[2,384,384]{2,1,0:T(8,128)(2,1)S(1)}, u32[]{:S(2)}, u32[]{:S(2)}) collective-permute-start(bf16[2,384,384]{2,1,0:T(8,128)(2,1)S(1)} %shard_map.68.refs_3_), channel_id=1, source_target_pairs={{0,4},{1,3},{2,6},{3,1},{4,0},{5,7},{6,2},{7,5},{8,12},{9,11},{10,... | collective-permute-start | bytes 1769480 | tf_op jit(solution)/shard_map/ppermute | solution.py:375
  42.6 8.3 %collective-permute-start.10 = (bf16[2,384,384]{2,1,0:T(8,128)(2,1)S(1)}, bf16[2,384,384]{2,1,0:T(8,128)(2,1)S(1)}, u32[]{:S(2)}, u32[]{:S(2)}) collective-permute-start(bf16[2,384,384]{2,1,0:T(8,128)(2,1)S(1)} %collective-permute-done.9.refs_2_), channel_id=1, source_target_pairs={{0,1},{1,0},{2,3},{3,2},{4,5},{5,4},{6,7},{7,6},{8,9},{9,8},{10,11... | collective-permute-start | bytes 1769480 | tf_op jit(solution)/shard_map/ppermute | solution.py:375
  44.6 8.0 %collective-permute-start.14 = (bf16[2,480,384]{2,1,0:T(8,128)(2,1)S(1)}, bf16[2,480,384]{2,1,0:T(8,128)(2,1)S(1)}, u32[]{:S(2)}, u32[]{:S(2)}) collective-permute-start(bf16[2,480,384]{2,1,0:T(8,128)(2,1)S(1)} %collective-permute-done.13.refs_2_), channel_id=1, source_target_pairs={{0,1},{1,0},{2,3},{3,2},{4,5},{5,4},{6,7},{7,6},{8,9},{9,8},{10,11... | collective-permute-start | bytes 2211848 | tf_op jit(solution)/shard_map/ppermute | solution.py:375
  51.6 2.1 %collective-permute-start.15 = (bf16[2,384,384]{2,1,0:T(8,128)(2,1)S(1)}, bf16[2,384,384]{2,1,0:T(8,128)(2,1)S(1)}, u32[]{:S(2)}, u32[]{:S(2)}) collective-permute-start(bf16[2,384,384]{2,1,0:T(8,128)(2,1)S(1)} %collective-permute-done.8.refs_2_), channel_id=1, source_target_pairs={{0,1},{1,0},{2,3},{3,2},{4,5},{5,4},{6,7},{7,6},{8,9},{9,8},{10,11... | collective-permute-start | bytes 1769480 | tf_op jit(solution)/shard_map/ppermute | solution.py:375
